TPU v7x, 32 devices: a whole 2x2x4 slice. The times are simulated.
32 devices in a mesh: front: 2 (over core), row: 4 (over y, x), col: 4 (over z).
Axes of the slice: x: 2, y: 2, z: 4, core: 2. Of those that a mesh axis runs over, the one named last changes fastest.
Arguments:
- child_blocks: bfloat16 [16384, 8192], P(('front', 'row'), 'col'), may hold values from -0.0625 to 0.0625
- sketch: bfloat16 [8192, 512], P('col'), may hold values from -6 to 6
- block_map: int32 [2, 64], P('front'), may hold values from 0 to 95, as said below
Outputs:
- parent_basis: float32 [512, 12288], P('col', ('front', 'row'))
Inputs may be any that keep to these rules, and one draw needn't show every extreme that they name: `block_map`: each row lists 8192 / 128 different parent blocks in increasing order.
All inputs are finite; a program needn't handle non-finite values.
Results may differ from a plain program's by a relative error of at most 0.0003.
Values sent between devices are 32-bit elements; how exact they have to be, the bound alone decides.
No kernel may reach another device: no remote copies, remote signals or barrier semaphores. Data moves between devices by JAX's collectives and lax.ppermute only.
A program may use at most 128 MiB of HBM per device.

v0:
```python
import jax
import jax.numpy as jnp
from jax import lax
from jax.experimental import pallas as pl
from jax.experimental.pallas import tpu as pltpu
from jax.sharding import PartitionSpec as P


P_SIZE = 12288
BLK = 128
COLUMN_CHUNKS = 2


def grant(mebibytes):
    return pltpu.CompilerParams(vmem_limit_bytes=mebibytes << 20)


def product_pieces(panel, sketch, dests, sub, chunks):
    blocks, _, depth = panel.shape
    count = len(dests)
    width = sketch.shape[1] // chunks
    step = max(blocks // 2, 1)

    def kernel(dest_ref, a_ref, b_ref, *outs):
        product = jnp.dot(a_ref[...].reshape(step * sub, depth), b_ref[...], preferred_element_type=jnp.float32)
        rows = pl.ds(pl.program_id(1) * step, step)
        for k in range(count):

            @pl.when(pl.program_id(0) == k)
            def _():
                for h in range(chunks):
                    outs[k * chunks + h][rows] = product[:, h * width : (h + 1) * width].reshape(step, sub, width)

    outs = pl.pallas_call(
        kernel,
        out_shape=[jax.ShapeDtypeStruct((blocks, sub, width), jnp.float32)] * (count * chunks),
        grid_spec=pltpu.PrefetchScalarGridSpec(
            num_scalar_prefetch=1,
            grid=(count, blocks // step),
            in_specs=[
                pl.BlockSpec((step, sub, depth), lambda p, g, d: (g, d[p], 0)),
                pl.BlockSpec(memory_space=pltpu.VMEM),
            ],
            out_specs=[pl.BlockSpec(memory_space=pltpu.VMEM)] * (count * chunks),
        ),
        cost_estimate=pl.CostEstimate(
            flops=2 * count * blocks * sub * depth * width * chunks,
            bytes_accessed=count * blocks * sub * (2 * depth + 4 * width * chunks) + 2 * depth * width * chunks,
            transcendentals=0,
        ),
        compiler_params=grant(28),
        name="product_pieces",
    )(jnp.stack(dests), panel, sketch)
    return [outs[k * chunks : (k + 1) * chunks] for k in range(count)]


def pack_slots(held, inverse, slots):
    children = len(held)
    offsets = inverse.shape[1]
    _, sub, width = held[0].shape

    def kernel(inv_ref, *refs):
        for o in range(offsets):
            out = refs[children + o]

            def fill(j, carry, o=o, out=out):
                total = jnp.zeros((sub, width), jnp.float32)
                for k in range(children):
                    at = inv_ref[(k * offsets + o) * slots + j]
                    block = refs[k][jnp.maximum(at, 0)]
                    total = total + jnp.where(at >= 0, block, 0.0)
                out[j] = total
                return carry

            lax.fori_loop(0, slots, fill, 0)

    moved = 4 * sub * width * slots * offsets * (children + 1)
    return pl.pallas_call(
        kernel,
        out_shape=[jax.ShapeDtypeStruct((slots, sub, width), jnp.float32)] * offsets,
        in_specs=[pl.BlockSpec(memory_space=pltpu.SMEM)] + [pl.BlockSpec(memory_space=pltpu.VMEM)] * children,
        out_specs=[pl.BlockSpec(memory_space=pltpu.VMEM)] * offsets,
        cost_estimate=pl.CostEstimate(flops=moved, bytes_accessed=moved, transcendentals=0),
        compiler_params=grant(12),
        name="pack_slots",
    )(inverse.reshape(-1), *held)


def on_last(a, b):
    return lax.dot_general(a, b, (((1,), (1,)), ((), ())), preferred_element_type=jnp.float32)


def on_first(a, b):
    return lax.dot_general(a, b, (((0,), (0,)), ((), ())), preferred_element_type=jnp.float32)


def plain(a, b):
    return jnp.dot(a, b, preferred_element_type=jnp.float32)


def split(x):
    high = x.astype(jnp.bfloat16)
    return high, (x - high.astype(jnp.float32)).astype(jnp.bfloat16)


def triple(dot, a, b):
    return dot(a[0], b[0]) + (dot(a[0], b[1]) + dot(a[1], b[0]))


def gram_pieces(arrived, here, siblings, members, tile):
    slots, sub, width = arrived[0][0].shape
    rows, n = slots * sub, width * len(arrived)
    count = n // tile
    height = count * (count + 1) // 2 * tile
    piece = height // (siblings * members)
    counts = [len(a) for a in arrived]

    def kernel(here_ref, *refs):
        inputs, (share_ref, *out_refs, packed_ref) = refs[: sum(counts)], refs[sum(counts) :]
        at = 0
        for h, addends in enumerate(counts):
            share_ref[:, h * width : (h + 1) * width] = sum(r[...] for r in inputs[at : at + addends]).reshape(rows, width)
            at += addends
        high, low = split(share_ref[...])
        at = 0
        for i in range(count):
            here, upto = slice(i * tile, (i + 1) * tile), slice(0, (i + 1) * tile)
            strip = triple(on_first, (high[:, here], low[:, here]), (high[:, upto], low[:, upto]))
            for j in range(i + 1):
                packed_ref[at * tile : (at + 1) * tile, :] = strip[:, j * tile : (j + 1) * tile]
                at += 1
        for s in range(siblings):
            for m in range(members):
                spot = ((here_ref[0] ^ s) * members + (here_ref[1] ^ m)) * piece
                out_refs[s][m * piece : (m + 1) * piece, :] = packed_ref[pl.ds(pl.multiple_of(spot, 8), piece), :]

    flat = [x for a in arrived for x in a]
    outs = pl.pallas_call(
        kernel,
        out_shape=[jax.ShapeDtypeStruct((rows, n), jnp.float32)]
        + [jax.ShapeDtypeStruct((members * piece, tile), jnp.float32)] * siblings,
        in_specs=[pl.BlockSpec(memory_space=pltpu.SMEM)] + [pl.BlockSpec(memory_space=pltpu.VMEM)] * len(flat),
        out_specs=[pl.BlockSpec(memory_space=pltpu.VMEM)] * (1 + siblings),
        scratch_shapes=[pltpu.VMEM((height, tile), jnp.float32)],
        cost_estimate=pl.CostEstimate(
            flops=6 * height * tile * rows, bytes_accessed=4 * (len(flat) + 1) * rows * width, transcendentals=0
        ),
        compiler_params=grant(20),
        name="gram_pieces",
    )(here, *flat)
    return outs[0], list(outs[1:])


def basis_pieces(pieces, share, here, siblings, tile):
    rows, n = share.shape
    count = n // tile
    members = len(pieces)
    height = count * (count + 1) // 2 * tile
    piece = height // (siblings * members)
    small, enough = 1e-2, 4e-4

    def kernel(here_ref, *refs):
        piece_refs, share_ref = refs[:members], refs[members]
        out_refs, (packed_ref, g_ref, x_ref, e_ref) = refs[members + 1 : -4], refs[-4:]
        for s in range(siblings):
            for m in range(members):
                spot = ((here_ref[0] ^ s) * members + (here_ref[1] ^ m)) * piece
                packed_ref[pl.ds(pl.multiple_of(spot, 8), piece), :] = piece_refs[m][s * piece : (s + 1) * piece, :]
        at = 0
        for i in range(count):
            here = slice(i * tile, (i + 1) * tile)
            for j in range(i + 1):
                there = slice(j * tile, (j + 1) * tile)
                block = packed_ref[at * tile : (at + 1) * tile, :]
                g_ref[here, there] = block
                if j < i:
                    g_ref[there, here] = block.T
                at += 1
        row_id = lax.broadcasted_iota(jnp.int32, (n, n), 0)
        col_id = lax.broadcasted_iota(jnp.int32, (n, n), 1)

        def eye():
            return jnp.where(row_id == col_id, 1.0, 0.0)

        def half_lower(e):
            return jnp.where(row_id > col_id, e, jnp.where(row_id == col_id, 0.5 * e, 0.0))

        g = g_ref[...]
        diagonal = jnp.where(row_id == col_id, g, 0.0)
        down = 1.0 / jnp.sqrt(jnp.sum(diagonal, axis=1, keepdims=True))
        across = 1.0 / jnp.sqrt(jnp.sum(diagonal, axis=0, keepdims=True))
        x_ref[...] = jnp.where(row_id == col_id, down, 0.0)
        start = g * down * across - eye()
        e_ref[...] = start

        def rough(state):
            e = e_ref[...]
            f = half_lower(e)
            fb, eb = f.astype(jnp.bfloat16), e.astype(jnp.bfloat16)
            t = plain(fb, eb)
            e = on_last((f + t).astype(jnp.bfloat16), fb) - t - on_last(eb, fb)
            e_ref[...] = e
            x = x_ref[...]
            x_ref[...] = x - plain(fb, x.astype(jnp.bfloat16))
            return state[0] + 1, jnp.sum(e * e)

        lax.while_loop(lambda s: (s[0] < 12) & (s[1] > small) & (s[1] < 1e6), rough, (0, jnp.sum(start * start)))

        def fine(state):
            x = split(x_ref[...])
            e = triple(on_last, split(triple(plain, x, split(g_ref[...]))), x) - eye()
            x_ref[...] = x_ref[...] - plain(half_lower(e).astype(jnp.bfloat16), x[0])
            return state[0] + 1, jnp.sum(e * e)

        _, last = lax.while_loop(
            lambda s: (s[0] < 4) & jnp.logical_not(s[1] < enough), fine, (0, jnp.float32(1.0))
        )

        @pl.when(jnp.logical_not(last < enough))
        def _():
            x_ref[...] = eye()
            e_ref[...] = g_ref[...]
            lane = lax.broadcasted_iota(jnp.int32, (1, n), 1)
            below = lax.broadcasted_iota(jnp.int32, (n, 1), 0)

            def eliminate(j, carry):
                row = e_ref[pl.ds(j, 1), :]
                scale = 1.0 / jnp.sqrt(jnp.sum(jnp.where(lane == j, row, 0.0), axis=1, keepdims=True))
                row = jnp.where(lane > j, row * scale, 0.0)
                solved = x_ref[pl.ds(j, 1), :] * scale
                column = jnp.sum(jnp.where(col_id == j, e_ref[...], 0.0), axis=1, keepdims=True) * scale
                column = jnp.where(below > j, column, 0.0)
                e_ref[...] = e_ref[...] - column * row
                x_ref[...] = x_ref[...] - column * solved
                x_ref[pl.ds(j, 1), :] = solved
                return carry

            lax.fori_loop(0, n, eliminate, 0)

        split_share = split(share_ref[...])
        for k in range(count):
            strip = pl.multiple_of((here_ref[2] ^ k) * tile, tile)
            out_refs[k][...] = triple(on_last, split_share, split(x_ref[pl.ds(strip, tile), :]))

    return pl.pallas_call(
        kernel,
        out_shape=[jax.ShapeDtypeStruct((rows, tile), jnp.float32)] * count,
        in_specs=[pl.BlockSpec(memory_space=pltpu.SMEM)] + [pl.BlockSpec(memory_space=pltpu.VMEM)] * (1 + members),
        out_specs=[pl.BlockSpec(memory_space=pltpu.VMEM)] * count,
        scratch_shapes=[pltpu.VMEM((height, tile), jnp.float32)] + [pltpu.VMEM((n, n), jnp.float32)] * 3,
        cost_estimate=pl.CostEstimate(flops=12 * n * n * n, bytes_accessed=4 * n * (n + rows), transcendentals=0),
        compiler_params=grant(40),
        name="basis_pieces",
    )(here, *pieces, share)


def lay_out(pieces, here, slots, sub, blk):
    width = pieces[0].shape[1]

    def kernel(here_ref, *refs):
        out_ref, block_ref = refs[-2:]
        for j in range(slots):
            for k in range(len(pieces)):
                spot = pl.ds(pl.multiple_of((here_ref[0] ^ k) * sub, sub), sub)
                block_ref[j, spot, :] = refs[k][j * sub : (j + 1) * sub, :]
        for j in range(slots):
            out_ref[:, j * blk : (j + 1) * blk] = block_ref[j].T

    return pl.pallas_call(
        kernel,
        out_shape=jax.ShapeDtypeStruct((width, slots * blk), jnp.float32),
        in_specs=[pl.BlockSpec(memory_space=pltpu.SMEM)] + [pl.BlockSpec(memory_space=pltpu.VMEM)] * len(pieces),
        out_specs=pl.BlockSpec(memory_space=pltpu.VMEM),
        scratch_shapes=[pltpu.VMEM((slots, blk, width), jnp.float32)],
        compiler_params=grant(12),
        name="lay_out",
    )(here.reshape(1), *pieces)


def shards(child_blocks, sketch, block_map):
    fronts, rows, cols = (lax.axis_size(a) for a in ("front", "row", "col"))
    siblings = min(4, fronts)
    front_here, row_here, col_here = (lax.axis_index(a) for a in ("front", "row", "col"))
    sib_here = front_here % siblings
    total_blocks = block_map.shape[1]
    blocks = total_blocks // rows
    sub = BLK // cols
    sketch_cols = sketch.shape[1]
    parent_blocks = P_SIZE // BLK
    slots = parent_blocks // (siblings * rows)
    spread = parent_blocks - total_blocks
    panel = child_blocks.reshape(blocks, BLK, child_blocks.shape[1])
    both = ("front", "row")

    def place(front, row):
        return front * rows + row

    def may_reach(row, sib, target_row):
        low, high = row * blocks, row * blocks + blocks - 1 + spread
        first = (sib * rows + target_row) * slots
        return low <= first + slots - 1 and first <= high

    maps = [block_map[0]]
    level = 1
    while level < siblings:
        pairs = [(i, i ^ level) for i in range(fronts)]
        maps = maps + [lax.ppermute(m, "front", pairs) for m in maps]
        level *= 2
    own = jnp.stack([lax.dynamic_slice_in_dim(m, row_here * blocks, blocks) for m in maps])
    offset_ids = jnp.arange(rows, dtype=jnp.int32)
    wanted = (sib_here * rows + (row_here ^ offset_ids))[:, None] * slots + jnp.arange(slots, dtype=jnp.int32)[None]
    hit = own[:, None, None, :] == wanted[None, :, :, None]
    inverse = jnp.max(jnp.where(hit, jnp.arange(blocks, dtype=jnp.int32), -1), axis=-1)

    def clipped(dest):
        return jnp.clip(dest, 0, cols - 1)

    wants = []
    for stage in range(1, cols):
        up_dest, down_dest = cols - stage + col_here, stage - cols + col_here
        if stage <= cols // 2:
            wants.append(clipped(jnp.where(up_dest < cols, up_dest, down_dest)))
        else:
            wants += [clipped(up_dest), clipped(down_dest)]
    wants.append(col_here)
    panel = pltpu.with_memory_space_constraint(panel, pltpu.HBM)
    products = [*product_pieces(panel, sketch, wants[:1], sub, COLUMN_CHUNKS)]
    products += product_pieces(panel, sketch, wants[1:], sub, COLUMN_CHUNKS)

    arrived = []
    for chunk in range(COLUMN_CHUNKS):
        pieces = iter(products)
        came_up = came_down = None
        for stage in range(1, cols):
            up = down = next(pieces)[chunk]
            if stage > cols // 2:
                down = next(pieces)[chunk]
            if came_up is not None:
                up, down = up + came_up, down + came_down
            came_up = lax.ppermute(up, "col", [(i, i + 1) for i in range(stage)])
            came_down = lax.ppermute(down, "col", [(i, i - 1) for i in range(cols - stage, cols)])
        held = [next(pieces)[chunk] + came_up + came_down]
        level = 1
        while level < siblings:
            pairs = [(i, i ^ level) for i in range(fronts)]
            held = held + [lax.ppermute(h, "front", pairs) for h in held]
            level *= 2
        slotted = pack_slots(held, inverse, slots)
        came = [slotted[0]]
        for k in range(1, rows)[::-1]:
            pairs = [
                (place(f, r), place(f, r ^ k))
                for f in range(fronts)
                for r in range(rows)
                if may_reach(r, f % siblings, r ^ k)
            ]
            came.append(lax.ppermute(slotted[k], both, pairs))
        arrived.append(came)

    width = sketch_cols // cols
    here = jnp.stack([sib_here, row_here, col_here])
    share, halves = gram_pieces(arrived, here, siblings, rows, width)

    def swap(x, name, level):
        return lax.ppermute(x, name, [(i, i ^ level) for i in range(lax.axis_size(name))])

    levels = [1 << k for k in range(siblings.bit_length() - 1)]
    kept = dict(enumerate(halves))
    for level in levels:
        kept = {s: kept[s] + swap(kept[s ^ level], "front", level) for s in kept if not s & level}
    parts = kept[0].reshape(rows, kept[0].shape[0] // rows, width)
    piece = parts[0]
    for k in range(1, rows)[::-1]:
        piece = piece + swap(parts[k], "row", k)
    piece = piece + sum(swap(piece, "col", k) for k in range(1, cols)[::-1])
    mine = [piece]
    for level in levels:
        mine = mine + [swap(p, "front", level) for p in mine]
    mine = jnp.concatenate(mine, axis=0)
    pieces = [mine] + [swap(mine, "row", k) for k in range(1, rows)]

    basis = basis_pieces(pieces, share, here, siblings, width)
    pieces = [basis[0]] + [swap(basis[k], "col", k) for k in range(1, cols)]
    return lay_out(pieces, col_here, slots, sub, BLK)


def solution(mesh):
    placed = (P(("front", "row"), "col"), P("col", None), P("front", None))

    return jax.shard_map(shards, mesh=mesh, in_specs=placed, out_specs=P("col", ("front", "row")), check_vma=False)
```

profile of v0, /device:TPU:0, one launch (start us, length us, event | category | flops | bytes accessed | tf_op | source)
XLA Modules:
  0.0 324.6 jit_solution(17221465189847142523)
XLA Ops:
  1.6 3.8 %product_pieces.3 = (f32[16,32,256]{2,1,0:T(8,128)}, f32[16,32,256]{2,1,0:T(8,128)}) custom-call(s32[1]{0:T(128)} %bitcast.9.dest_ref, bf16[16,128,2048]{2,1,0:T(8,128)(2,1)} %bitcast.11, bf16[2048,512]{1,0:T(8,128)(2,1)S(1)} %copy-done), custom_call_target="tpu_custom_call" | custom-call | flops 1073741824 | bytes 5242880 | tf_op jit(solution)/shard_map/product_pieces/pallas_call | solution.py:34
  5.4 5.8 %collective-permute-start.11 = (f32[16,32,256]{2,1,0:T(8,128)}, f32[16,32,256]{2,1,0:T(8,128)}, u32[]{:S(2)}, u32[]{:S(2)}) collective-permute-start(f32[16,32,256]{2,1,0:T(8,128)} %get-tuple-element.42), channel_id=1, source_target_pairs={{0,1},{4,5},{8,9},{12,13},{16,17},{20,21},{24,25},{28,29}} | collective-permute-start | bytes 1572872 | tf_op jit(solution)/shard_map/ppermute | solution.py:340
  12.6 2.1 collective-permute-start.1
  16.2 9.5 %product_pieces.2 = (f32[16,32,256]{2,1,0:T(8,128)S(1)}, f32[16,32,256]{2,1,0:T(8,128)S(1)}, f32[16,32,256]{2,1,0:T(8,128)S(1)}, f32[16,32,256]{2,1,0:T(8,128)S(...) custom-call(s32[4]{0:T(128)S(1)} %pad_add_fusion.2.dest_ref, ...), custom_call_target="tpu_custom_call" | custom-call | flops 4294967296 | bytes 14680064 | tf_op jit(solution)/shard_map/product_pieces/pallas_call | solution.py:34
  25.8 1.7 fusion.2
  29.5 4.7 %collective-permute-done.1 = f32[16,32,256]{2,1,0:T(8,128)} collective-permute-done((f32[16,32,256]{2,1,0:T(8,128)}, f32[16,32,256]{2,1,0:T(8,128)}, u32[]{:S(2)}, u32[]{:S(2)}) %collective-permute-start.1) | collective-permute-done | bytes 524320 | tf_op jit(solution)/shard_map/ppermute | solution.py:340
  34.2 2.1 fusion.3
  36.3 5.2 %collective-permute-start.2 = (f32[16,32,256]{2,1,0:T(8,128)}, f32[16,32,256]{2,1,0:T(8,128)}, u32[]{:S(2)}, u32[]{:S(2)}) collective-permute-start(f32[16,32,256]{2,1,0:T(8,128)} %get-tuple-element.57), channel_id=1, source_target_pairs={{0,1},{1,2},{4,5},{5,6},{8,9},{9,10},{12,13},{13,14},{16,17},{17,1... | collective-permute-start | bytes 1572872 | tf_op jit(solution)/shard_map/ppermute | solution.py:340
  42.2 3.1 collective-permute-done.12
  45.4 5.2 %collective-permute-start.13 = (f32[16,32,256]{2,1,0:T(8,128)S(1)}, f32[16,32,256]{2,1,0:T(8,128)}, u32[]{:S(2)}, u32[]{:S(2)}) collective-permute-start(f32[16,32,256]{2,1,0:T(8,128)S(1)} %add.118), channel_id=1, source_target_pairs={{0,1},{1,2},{2,3},{4,5},{5,6},{6,7},{8,9},{9,10},{10,11},{12,13},{... | collective-permute-start | bytes 1572872 | tf_op jit(solution)/shard_map/ppermute | solution.py:340
  52.1 4.6 %collective-permute-done.2 = f32[16,32,256]{2,1,0:T(8,128)} collective-permute-done((f32[16,32,256]{2,1,0:T(8,128)}, f32[16,32,256]{2,1,0:T(8,128)}, u32[]{:S(2)}, u32[]{:S(2)}) %collective-permute-start.2) | collective-permute-done | bytes 524320 | tf_op jit(solution)/shard_map/ppermute | solution.py:340
  56.7 1.9 add.112
  58.6 4.4 %collective-permute-start.3 = (f32[16,32,256]{2,1,0:T(8,128)}, f32[16,32,256]{2,1,0:T(8,128)S(1)}, u32[]{:S(2)}, u32[]{:S(2)}) collective-permute-start(f32[16,32,256]{2,1,0:T(8,128)} %add.112), channel_id=1, source_target_pairs={{0,1},{1,2},{2,3},{4,5},{5,6},{6,7},{8,9},{9,10},{10,11},{12,13},{... | collective-permute-start | bytes 1572872 | tf_op jit(solution)/shard_map/ppermute | solution.py:340
  64.5 3.3 %collective-permute-done.13 = f32[16,32,256]{2,1,0:T(8,128)} collective-permute-done((f32[16,32,256]{2,1,0:T(8,128)S(1)}, f32[16,32,256]{2,1,0:T(8,128)}, u32[]{:S(2)}, u32[]{:S(2)}) %collective-permute-start.13) | collective-permute-done | bytes 524320 | tf_op jit(solution)/shard_map/ppermute | solution.py:340
  69.4 8.6 %collective-permute-done.3 = f32[16,32,256]{2,1,0:T(8,128)S(1)} collective-permute-done((f32[16,32,256]{2,1,0:T(8,128)}, f32[16,32,256]{2,1,0:T(8,128)S(1)}, u32[]{:S(2)}, u32[]{:S(2)}) %collective-permute-start.3) | collective-permute-done | bytes 524320 | tf_op jit(solution)/shard_map/ppermute | solution.py:340
  81.2 4.4 %collective-permute-start.18 = (f32[12,32,256]{2,1,0:T(8,128)S(1)}, f32[12,32,256]{2,1,0:T(8,128)S(1)}, u32[]{:S(2)}, u32[]{:S(2)}) collective-permute-start(f32[12,32,256]{2,1,0:T(8,128)S(1)} %get-tuple-element.45), channel_id=1, source_target_pairs={{0,12},{4,8},{24,20},{28,16},{1,13},{5,9},{25,21},{29,17},{2,14},{... | collective-permute-start | bytes 1179656 | tf_op jit(solution)/shard_map/ppermute | solution.py:357
  86.9 2.5 collective-permute-start.20
  93.3 5.0 %collective-permute-start.9 = (f32[12,32,256]{2,1,0:T(8,128)S(1)}, f32[12,32,256]{2,1,0:T(8,128)S(1)}, u32[]{:S(2)}, u32[]{:S(2)}) collective-permute-start(f32[12,32,256]{2,1,0:T(8,128)S(1)} %get-tuple-element.37), channel_id=1, source_target_pairs={{0,8},{4,12},{24,16},{28,20},{1,9},{5,13},{25,17},{29,21},{2,10},{... | collective-permute-start | bytes 1179656 | tf_op jit(solution)/shard_map/ppermute | solution.py:357
  99.3 4.3 %collective-permute-done.8.refs_1_ = f32[12,32,256]{2,1,0:T(8,128)S(1)} collective-permute-done((f32[12,32,256]{2,1,0:T(8,128)S(1)}, f32[12,32,256]{2,1,0:T(8,128)S(1)}, u32[]{:S(2)}, u32[]{:S(2)}) %collective-permute-start.8) | collective-permute-done | bytes 393248 | tf_op jit(solution)/shard_map/ppermute | solution.py:357
  103.6 2.1 collective-permute-done.9.refs_2_
  107.2 1.6 collective-permute-done.21
  108.9 2.6 collective-permute-start.22
  114.4 1.7 collective-permute-done.23
  117.2 3.9 %collective-permute-start.25 = (f32[160,128]{1,0:T(8,128)S(1)}, f32[160,128]{1,0:T(8,128)S(1)}, u32[]{:S(2)}, u32[]{:S(2)}) collective-permute-start(f32[160,128]{1,0:T(8,128)S(1)} %fusion.1), channel_id=1, source_target_pairs={{0,3},{1,2},{2,1},{3,0},{4,7},{5,6},{6,5},{7,4},{8,11},{9,10},{10,... | collective-permute-start | bytes 245768 | tf_op jit(solution)/shard_map/ppermute | solution.py:365
  123.9 4.5 %collective-permute-done.26 = f32[160,128]{1,0:T(8,128)S(1)} collective-permute-done((f32[160,128]{1,0:T(8,128)S(1)}, f32[160,128]{1,0:T(8,128)S(1)}, u32[]{:S(2)}, u32[]{:S(2)}) %collective-permute-start.26) | collective-permute-done | bytes 81952 | tf_op jit(solution)/shard_map/ppermute | solution.py:365
  130.6 1.8 collective-permute-start.30
  133.3 3.6 %collective-permute-done.29.refs_1_ = f32[320,128]{1,0:T(8,128)S(1)} collective-permute-done((f32[320,128]{1,0:T(8,128)S(1)}, f32[320,128]{1,0:T(8,128)S(1)}, u32[]{:S(2)}, u32[]{:S(2)}) %collective-permute-start.29) | collective-permute-done | bytes 163872 | tf_op jit(solution)/shard_map/ppermute | solution.py:365
  136.9 3.3 %collective-permute-done.30.refs_2_ = f32[320,128]{1,0:T(8,128)S(1)} collective-permute-done((f32[320,128]{1,0:T(8,128)S(1)}, f32[320,128]{1,0:T(8,128)S(1)}, u32[]{:S(2)}, u32[]{:S(2)}) %collective-permute-start.30) | collective-permute-done | bytes 163872 | tf_op jit(solution)/shard_map/ppermute | solution.py:365
  140.2 164.9 %basis_pieces.1 = (f32[384,128]{1,0:T(8,128)S(1)}, f32[384,128]{1,0:T(8,128)S(1)}, f32[384,128]{1,0:T(8,128)S(1)}, f32[384,128]{1,0:T(8,128)S(1)}) custom-call(s32[3]{0:T(128)S(1)} %pad_add_fusion.1.here_ref, f32[320,128]{1,0:T(8,128)S(1)} %pad_maximum_fusion.refs_0_, f32[320,128]{1,0:T(8,128)S(1)} %collective-permute-done.29.refs_1_, ...), custom_call_target="tpu_custom_call" | custom-call | flops 1610612736 | bytes 1835008 | tf_op jit(solution)/shard_map/basis_pieces/pallas_call | solution.py:245
  305.8 3.4 %collective-permute-start.33 = (f32[384,128]{1,0:T(8,128)S(1)}, f32[384,128]{1,0:T(8,128)S(1)}, u32[]{:S(2)}, u32[]{:S(2)}) collective-permute-start(f32[384,128]{1,0:T(8,128)S(1)} %get-tuple-element.53), channel_id=1, source_target_pairs={{0,2},{1,3},{2,0},{3,1},{4,6},{5,7},{6,4},{7,5},{8,10},{9,11},{10,... | collective-permute-start | bytes 589832 | tf_op jit(solution)/shard_map/ppermute | solution.py:365
  309.6 5.1 %collective-permute-done.32.refs_1_ = f32[384,128]{1,0:T(8,128)S(1)} collective-permute-done((f32[384,128]{1,0:T(8,128)S(1)}, f32[384,128]{1,0:T(8,128)S(1)}, u32[]{:S(2)}, u32[]{:S(2)}) %collective-permute-start.32) | collective-permute-done | bytes 196640 | tf_op jit(solution)/shard_map/ppermute | solution.py:365
  314.6 8.8 %collective-permute-done.33.refs_2_ = f32[384,128]{1,0:T(8,128)S(1)} collective-permute-done((f32[384,128]{1,0:T(8,128)S(1)}, f32[384,128]{1,0:T(8,128)S(1)}, u32[]{:S(2)}, u32[]{:S(2)}) %collective-permute-start.33) | collective-permute-done | bytes 196640 | tf_op jit(solution)/shard_map/ppermute | solution.py:365
  (78 shorter events, 35.0 us)
Async XLA Ops:
  5.4 20.4 %collective-permute-start.11 = (f32[16,32,256]{2,1,0:T(8,128)}, f32[16,32,256]{2,1,0:T(8,128)}, u32[]{:S(2)}, u32[]{:S(2)}) collective-permute-start(f32[16,32,256]{2,1,0:T(8,128)} %get-tuple-element.42), channel_id=1, source_target_pairs={{0,1},{4,5},{8,9},{12,13},{16,17},{20,21},{24,25},{28,29}} | collective-permute-start | bytes 1572872 | tf_op jit(solution)/shard_map/ppermute | solution.py:340
  11.2 14.7 %collective-permute-start.14 = (f32[16,32,256]{2,1,0:T(8,128)}, f32[16,32,256]{2,1,0:T(8,128)}, u32[]{:S(2)}, u32[]{:S(2)}) collective-permute-start(f32[16,32,256]{2,1,0:T(8,128)} %get-tuple-element.42), channel_id=1, source_target_pairs={{3,2},{7,6},{11,10},{15,14},{19,18},{23,22},{27,26},{31,30}} | collective-permute-start | bytes 1572872 | tf_op jit(solution)/shard_map/ppermute | solution.py:341
  12.6 21.6 %collective-permute-start.1 = (f32[16,32,256]{2,1,0:T(8,128)}, f32[16,32,256]{2,1,0:T(8,128)}, u32[]{:S(2)}, u32[]{:S(2)}) collective-permute-start(f32[16,32,256]{2,1,0:T(8,128)} %get-tuple-element.33), channel_id=1, source_target_pairs={{0,1},{4,5},{8,9},{12,13},{16,17},{20,21},{24,25},{28,29}} | collective-permute-start | bytes 1572872 | tf_op jit(solution)/shard_map/ppermute | solution.py:340
  14.7 19.5 %collective-permute-start.4 = (f32[16,32,256]{2,1,0:T(8,128)}, f32[16,32,256]{2,1,0:T(8,128)}, u32[]{:S(2)}, u32[]{:S(2)}) collective-permute-start(f32[16,32,256]{2,1,0:T(8,128)} %get-tuple-element.33), channel_id=1, source_target_pairs={{3,2},{7,6},{11,10},{15,14},{19,18},{23,22},{27,26},{31,30}} | collective-permute-start | bytes 1572872 | tf_op jit(solution)/shard_map/ppermute | solution.py:341
  27.5 17.8 %collective-permute-start.12 = (f32[16,32,256]{2,1,0:T(8,128)S(1)}, f32[16,32,256]{2,1,0:T(8,128)S(1)}, u32[]{:S(2)}, u32[]{:S(2)}) collective-permute-start(f32[16,32,256]{2,1,0:T(8,128)S(1)} %get-tuple-element.55), channel_id=1, source_target_pairs={{0,1},{1,2},{4,5},{5,6},{8,9},{9,10},{12,13},{13,14},{16,17},{17,1... | collective-permute-start | bytes 1572872 | tf_op jit(solution)/shard_map/ppermute | solution.py:340
  28.8 21.8 %collective-permute-start.15 = (f32[16,32,256]{2,1,0:T(8,128)S(1)}, f32[16,32,256]{2,1,0:T(8,128)S(1)}, u32[]{:S(2)}, u32[]{:S(2)}) collective-permute-start(f32[16,32,256]{2,1,0:T(8,128)S(1)} %get-tuple-element.56), channel_id=1, source_target_pairs={{2,1},{3,2},{6,5},{7,6},{10,9},{11,10},{14,13},{15,14},{18,17},{19... | collective-permute-start | bytes 1572872 | tf_op jit(solution)/shard_map/ppermute | solution.py:341
  36.3 20.4 %collective-permute-start.2 = (f32[16,32,256]{2,1,0:T(8,128)}, f32[16,32,256]{2,1,0:T(8,128)}, u32[]{:S(2)}, u32[]{:S(2)}) collective-permute-start(f32[16,32,256]{2,1,0:T(8,128)} %get-tuple-element.57), channel_id=1, source_target_pairs={{0,1},{1,2},{4,5},{5,6},{8,9},{9,10},{12,13},{13,14},{16,17},{17,1... | collective-permute-start | bytes 1572872 | tf_op jit(solution)/shard_map/ppermute | solution.py:340
  41.5 21.5 %collective-permute-start.5 = (f32[16,32,256]{2,1,0:T(8,128)S(1)}, f32[16,32,256]{2,1,0:T(8,128)S(1)}, u32[]{:S(2)}, u32[]{:S(2)}) collective-permute-start(f32[16,32,256]{2,1,0:T(8,128)S(1)} %get-tuple-element.58), channel_id=1, source_target_pairs={{2,1},{3,2},{6,5},{7,6},{10,9},{11,10},{14,13},{15,14},{18,17},{19... | collective-permute-start | bytes 1572872 | tf_op jit(solution)/shard_map/ppermute | solution.py:341
  45.4 22.4 %collective-permute-start.13 = (f32[16,32,256]{2,1,0:T(8,128)S(1)}, f32[16,32,256]{2,1,0:T(8,128)}, u32[]{:S(2)}, u32[]{:S(2)}) collective-permute-start(f32[16,32,256]{2,1,0:T(8,128)S(1)} %add.118), channel_id=1, source_target_pairs={{0,1},{1,2},{2,3},{4,5},{5,6},{6,7},{8,9},{9,10},{10,11},{12,13},{... | collective-permute-start | bytes 1572872 | tf_op jit(solution)/shard_map/ppermute | solution.py:340
  50.7 17.1 %collective-permute-start.16 = (f32[16,32,256]{2,1,0:T(8,128)S(1)}, f32[16,32,256]{2,1,0:T(8,128)}, u32[]{:S(2)}, u32[]{:S(2)}) collective-permute-start(f32[16,32,256]{2,1,0:T(8,128)S(1)} %add.121), channel_id=1, source_target_pairs={{1,0},{2,1},{3,2},{5,4},{6,5},{7,6},{9,8},{10,9},{11,10},{13,12},{... | collective-permute-start | bytes 1572872 | tf_op jit(solution)/shard_map/ppermute | solution.py:341
  52.0 17.4 %collective-permute-start = (s32[64]{0:T(128)S(1)}, s32[64]{0:T(128)S(1)}, u32[]{:S(2)}, u32[]{:S(2)}) collective-permute-start(s32[64]{0:T(128)S(1)} %bitcast.13), channel_id=1, source_target_pairs={{0,16},{16,0},{1,17},{17,1},{2,18},{18,2},{3,19},{19,3},{4,20},{20... | collective-permute-start | bytes 776 | tf_op jit(solution)/shard_map/ppermute | solution.py:307
  58.6 19.4 %collective-permute-start.3 = (f32[16,32,256]{2,1,0:T(8,128)}, f32[16,32,256]{2,1,0:T(8,128)S(1)}, u32[]{:S(2)}, u32[]{:S(2)}) collective-permute-start(f32[16,32,256]{2,1,0:T(8,128)} %add.112), channel_id=1, source_target_pairs={{0,1},{1,2},{2,3},{4,5},{5,6},{6,7},{8,9},{9,10},{10,11},{12,13},{... | collective-permute-start | bytes 1572872 | tf_op jit(solution)/shard_map/ppermute | solution.py:340
  63.1 14.9 %collective-permute-start.6 = (f32[16,32,256]{2,1,0:T(8,128)S(1)}, f32[16,32,256]{2,1,0:T(8,128)S(1)}, u32[]{:S(2)}, u32[]{:S(2)}) collective-permute-start(f32[16,32,256]{2,1,0:T(8,128)S(1)} %add.115), channel_id=1, source_target_pairs={{1,0},{2,1},{3,2},{5,4},{6,5},{7,6},{9,8},{10,9},{11,10},{13,12},{... | collective-permute-start | bytes 1572872 | tf_op jit(solution)/shard_map/ppermute | solution.py:341
  69.3 10.7 %collective-permute-start.17 = (f32[16,32,256]{2,1,0:T(8,128)S(1)}, f32[16,32,256]{2,1,0:T(8,128)S(1)}, u32[]{:S(2)}, u32[]{:S(2)}) collective-permute-start(f32[16,32,256]{2,1,0:T(8,128)S(1)} %add_add_fusion.refs_0_), channel_id=1, source_target_pairs={{0,16},{16,0},{1,17},{17,1},{2,18},{18,2},{3,19},{19,3},{4,20},{20... | collective-permute-start | bytes 1572872 | tf_op jit(solution)/shard_map/ppermute | solution.py:346
  79.2 10.3 %collective-permute-start.7 = (f32[16,32,256]{2,1,0:T(8,128)S(1)}, f32[16,32,256]{2,1,0:T(8,128)S(1)}, u32[]{:S(2)}, u32[]{:S(2)}) collective-permute-start(f32[16,32,256]{2,1,0:T(8,128)S(1)} %add_add_fusion.1.refs_0_), channel_id=1, source_target_pairs={{0,16},{16,0},{1,17},{17,1},{2,18},{18,2},{3,19},{19,3},{4,20},{20... | collective-permute-start | bytes 1572872 | tf_op jit(solution)/shard_map/ppermute | solution.py:346
  81.2 12.1 %collective-permute-start.18 = (f32[12,32,256]{2,1,0:T(8,128)S(1)}, f32[12,32,256]{2,1,0:T(8,128)S(1)}, u32[]{:S(2)}, u32[]{:S(2)}) collective-permute-start(f32[12,32,256]{2,1,0:T(8,128)S(1)} %get-tuple-element.45), channel_id=1, source_target_pairs={{0,12},{4,8},{24,20},{28,16},{1,13},{5,9},{25,21},{29,17},{2,14},{... | collective-permute-start | bytes 1179656 | tf_op jit(solution)/shard_map/ppermute | solution.py:357
  85.6 12.8 %collective-permute-start.19 = (f32[12,32,256]{2,1,0:T(8,128)S(1)}, f32[12,32,256]{2,1,0:T(8,128)S(1)}, u32[]{:S(2)}, u32[]{:S(2)}) collective-permute-start(f32[12,32,256]{2,1,0:T(8,128)S(1)} %get-tuple-element.46), channel_id=1, source_target_pairs={{0,8},{4,12},{24,16},{28,20},{1,9},{5,13},{25,17},{29,21},{2,10},{... | collective-permute-start | bytes 1179656 | tf_op jit(solution)/shard_map/ppermute | solution.py:357
  86.9 11.4 %collective-permute-start.20 = (f32[12,32,256]{2,1,0:T(8,128)S(1)}, f32[12,32,256]{2,1,0:T(8,128)S(1)}, u32[]{:S(2)}, u32[]{:S(2)}) collective-permute-start(f32[12,32,256]{2,1,0:T(8,128)S(1)} %get-tuple-element.47), channel_id=1, source_target_pairs={{0,4},{8,12},{20,16},{28,24},{1,5},{9,13},{21,17},{29,25},{2,6},{1... | collective-permute-start | bytes 1179656 | tf_op jit(solution)/shard_map/ppermute | solution.py:357
  90.7 8.7 %collective-permute-start.10 = (f32[12,32,256]{2,1,0:T(8,128)S(1)}, f32[12,32,256]{2,1,0:T(8,128)S(1)}, u32[]{:S(2)}, u32[]{:S(2)}) collective-permute-start(f32[12,32,256]{2,1,0:T(8,128)S(1)} %get-tuple-element.38), channel_id=1, source_target_pairs={{0,4},{8,12},{20,16},{28,24},{1,5},{9,13},{21,17},{29,25},{2,6},{1... | collective-permute-start | bytes 1179656 | tf_op jit(solution)/shard_map/ppermute | solution.py:357
  92.0 11.6 %collective-permute-start.8 = (f32[12,32,256]{2,1,0:T(8,128)S(1)}, f32[12,32,256]{2,1,0:T(8,128)S(1)}, u32[]{:S(2)}, u32[]{:S(2)}) collective-permute-start(f32[12,32,256]{2,1,0:T(8,128)S(1)} %get-tuple-element.36), channel_id=1, source_target_pairs={{0,12},{4,8},{24,20},{28,16},{1,13},{5,9},{25,21},{29,17},{2,14},{... | collective-permute-start | bytes 1179656 | tf_op jit(solution)/shard_map/ppermute | solution.py:357
  93.3 12.4 %collective-permute-start.9 = (f32[12,32,256]{2,1,0:T(8,128)S(1)}, f32[12,32,256]{2,1,0:T(8,128)S(1)}, u32[]{:S(2)}, u32[]{:S(2)}) collective-permute-start(f32[12,32,256]{2,1,0:T(8,128)S(1)} %get-tuple-element.37), channel_id=1, source_target_pairs={{0,8},{4,12},{24,16},{28,20},{1,9},{5,13},{25,17},{29,21},{2,10},{... | collective-permute-start | bytes 1179656 | tf_op jit(solution)/shard_map/ppermute | solution.py:357
  108.9 5.5 %collective-permute-start.22 = (f32[160,128]{1,0:T(8,128)S(1)}, f32[160,128]{1,0:T(8,128)S(1)}, u32[]{:S(2)}, u32[]{:S(2)}) collective-permute-start(f32[160,128]{1,0:T(8,128)S(1)} %get-tuple-element.59), channel_id=1, source_target_pairs={{0,12},{4,8},{8,4},{12,0},{1,13},{5,9},{9,5},{13,1},{2,14},{6,10},... | collective-permute-start | bytes 245768 | tf_op jit(solution)/shard_map/ppermute | solution.py:365
  111.6 5.6 %collective-permute-start.24 = (f32[160,128]{1,0:T(8,128)S(1)}, f32[160,128]{1,0:T(8,128)S(1)}, u32[]{:S(2)}, u32[]{:S(2)}) collective-permute-start(f32[160,128]{1,0:T(8,128)S(1)} %get-tuple-element.60), channel_id=1, source_target_pairs={{0,4},{4,0},{8,12},{12,8},{1,5},{5,1},{9,13},{13,9},{2,6},{6,2},{1... | collective-permute-start | bytes 245768 | tf_op jit(solution)/shard_map/ppermute | solution.py:365
  117.2 6.7 %collective-permute-start.25 = (f32[160,128]{1,0:T(8,128)S(1)}, f32[160,128]{1,0:T(8,128)S(1)}, u32[]{:S(2)}, u32[]{:S(2)}) collective-permute-start(f32[160,128]{1,0:T(8,128)S(1)} %fusion.1), channel_id=1, source_target_pairs={{0,3},{1,2},{2,1},{3,0},{4,7},{5,6},{6,5},{7,4},{8,11},{9,10},{10,... | collective-permute-start | bytes 245768 | tf_op jit(solution)/shard_map/ppermute | solution.py:365
  121.1 7.3 %collective-permute-start.26 = (f32[160,128]{1,0:T(8,128)S(1)}, f32[160,128]{1,0:T(8,128)S(1)}, u32[]{:S(2)}, u32[]{:S(2)}) collective-permute-start(f32[160,128]{1,0:T(8,128)S(1)} %fusion.1), channel_id=1, source_target_pairs={{0,2},{1,3},{2,0},{3,1},{4,6},{5,7},{6,4},{7,5},{8,10},{9,11},{10,... | collective-permute-start | bytes 245768 | tf_op jit(solution)/shard_map/ppermute | solution.py:365
  122.2 6.2 %collective-permute-start.27 = (f32[160,128]{1,0:T(8,128)S(1)}, f32[160,128]{1,0:T(8,128)S(1)}, u32[]{:S(2)}, u32[]{:S(2)}) collective-permute-start(f32[160,128]{1,0:T(8,128)S(1)} %fusion.1), channel_id=1, source_target_pairs={{0,1},{1,0},{2,3},{3,2},{4,5},{5,4},{6,7},{7,6},{8,9},{9,8},{10,11... | collective-permute-start | bytes 245768 | tf_op jit(solution)/shard_map/ppermute | solution.py:365
  129.8 7.1 %collective-permute-start.29 = (f32[320,128]{1,0:T(8,128)S(1)}, f32[320,128]{1,0:T(8,128)S(1)}, u32[]{:S(2)}, u32[]{:S(2)}) collective-permute-start(f32[320,128]{1,0:T(8,128)S(1)} %pad_maximum_fusion.refs_0_), channel_id=1, source_target_pairs={{0,4},{4,0},{8,12},{12,8},{1,5},{5,1},{9,13},{13,9},{2,6},{6,2},{1... | collective-permute-start | bytes 491528 | tf_op jit(solution)/shard_map/ppermute | solution.py:365
  130.6 9.6 %collective-permute-start.30 = (f32[320,128]{1,0:T(8,128)S(1)}, f32[320,128]{1,0:T(8,128)S(1)}, u32[]{:S(2)}, u32[]{:S(2)}) collective-permute-start(f32[320,128]{1,0:T(8,128)S(1)} %pad_maximum_fusion.refs_0_), channel_id=1, source_target_pairs={{0,8},{4,12},{8,0},{12,4},{1,9},{5,13},{9,1},{13,5},{2,10},{6,14},... | collective-permute-start | bytes 491528 | tf_op jit(solution)/shard_map/ppermute | solution.py:365
  132.5 7.8 %collective-permute-start.31 = (f32[320,128]{1,0:T(8,128)S(1)}, f32[320,128]{1,0:T(8,128)S(1)}, u32[]{:S(2)}, u32[]{:S(2)}) collective-permute-start(f32[320,128]{1,0:T(8,128)S(1)} %pad_maximum_fusion.refs_0_), channel_id=1, source_target_pairs={{0,12},{4,8},{8,4},{12,0},{1,13},{5,9},{9,5},{13,1},{2,14},{6,10},... | collective-permute-start | bytes 491528 | tf_op jit(solution)/shard_map/ppermute | solution.py:365
  305.1 9.5 %collective-permute-start.32 = (f32[384,128]{1,0:T(8,128)S(1)}, f32[384,128]{1,0:T(8,128)S(1)}, u32[]{:S(2)}, u32[]{:S(2)}) collective-permute-start(f32[384,128]{1,0:T(8,128)S(1)} %get-tuple-element.52), channel_id=1, source_target_pairs={{0,1},{1,0},{2,3},{3,2},{4,5},{5,4},{6,7},{7,6},{8,9},{9,8},{10,11... | collective-permute-start | bytes 589832 | tf_op jit(solution)/shard_map/ppermute | solution.py:365
  305.8 17.6 %collective-permute-start.33 = (f32[384,128]{1,0:T(8,128)S(1)}, f32[384,128]{1,0:T(8,128)S(1)}, u32[]{:S(2)}, u32[]{:S(2)}) collective-permute-start(f32[384,128]{1,0:T(8,128)S(1)} %get-tuple-element.53), channel_id=1, source_target_pairs={{0,2},{1,3},{2,0},{3,1},{4,6},{5,7},{6,4},{7,5},{8,10},{9,11},{10,... | collective-permute-start | bytes 589832 | tf_op jit(solution)/shard_map/ppermute | solution.py:365
  309.2 14.2 %collective-permute-start.34 = (f32[384,128]{1,0:T(8,128)S(1)}, f32[384,128]{1,0:T(8,128)S(1)}, u32[]{:S(2)}, u32[]{:S(2)}) collective-permute-start(f32[384,128]{1,0:T(8,128)S(1)} %get-tuple-element.54), channel_id=1, source_target_pairs={{0,3},{1,2},{2,1},{3,0},{4,7},{5,6},{6,5},{7,4},{8,11},{9,10},{10,... | collective-permute-start | bytes 589832 | tf_op jit(solution)/shard_map/ppermute | solution.py:365
  (8 other events, 110.7 us)
where the time goes:
time: 326 us; the launch traced here: 325 us
  Pallas kernels  183 us (56%)
  waiting for transfers between devices  65.2 us (20%)
  starting transfers between devices  64.4 us (20%)
  other arithmetic  9.31 us (3%)
    pallas_call x1, Pallas kernels, basis_pieces(): pl.pallas_call(kernel, out_shape=[jax.ShapeDtypeStruct((rows, tile), jnp....  165 us
    ppermute x14, waiting for transfers between devices, swap(): lax.ppermute(x, name, [(i, i ^ level) for i in range(lax.axis_size(name))])  33.5 us
    ppermute x6, waiting for transfers between devices, shards(): came_up = lax.ppermute(up, 'col', [(i, i + 1) for i in range(stage)])  24.3 us
    ppermute x6, starting transfers between devices, shards(): came_up = lax.ppermute(up, 'col', [(i, i + 1) for i in range(stage)])  23.9 us
    ppermute x14, starting transfers between devices, swap(): lax.ppermute(x, name, [(i, i ^ level) for i in range(lax.axis_size(name))])  17.6 us
    ppermute x6, starting transfers between devices, shards(): came.append(lax.ppermute(slotted[k], both, pairs))  15.8 us
    pallas_call x2, Pallas kernels, product_pieces(): pl.pallas_call(kernel, out_shape=[jax.ShapeDtypeStruct((blocks, sub, widt...  13.3 us
    ppermute x6, waiting for transfers between devices, shards(): came.append(lax.ppermute(slotted[k], both, pairs))  7.33 us
  transfers between devices with their start and end apart: 35, of which 19 were waited for; matrix products, arithmetic and copies ran while one was open for 3% of the time, Pallas kernels for 4%

commit v1 on v0

--- a/solution.py
+++ b/solution.py
@@ -15,11 +15,13 @@
     return pltpu.CompilerParams(vmem_limit_bytes=mebibytes << 20)
 
 
-def product_pieces(panel, sketch, dests, sub, chunks):
+def product_pieces(panel, sketch, dests, sub, chunks, chunk=None):
     blocks, _, depth = panel.shape
     count = len(dests)
+    outs_each = chunks if chunk is None else 1
     width = sketch.shape[1] // chunks
-    step = max(blocks // 2, 1)
+    across = width * outs_each
+    step = max(blocks // 2, 1) if chunk is None else max(blocks // 4, 1)
 
     def kernel(dest_ref, a_ref, b_ref, *outs):
         product = jnp.dot(a_ref[...].reshape(step * sub, depth), b_ref[...], preferred_element_type=jnp.float32)
@@ -28,30 +30,31 @@
 
             @pl.when(pl.program_id(0) == k)
             def _():
-                for h in range(chunks):
-                    outs[k * chunks + h][rows] = product[:, h * width : (h + 1) * width].reshape(step, sub, width)
+                for h in range(outs_each):
+                    part = product[:, h * width : (h + 1) * width]
+                    outs[k * outs_each + h][rows] = part.reshape(step, sub, width)
 
     outs = pl.pallas_call(
         kernel,
-        out_shape=[jax.ShapeDtypeStruct((blocks, sub, width), jnp.float32)] * (count * chunks),
+        out_shape=[jax.ShapeDtypeStruct((blocks, sub, width), jnp.float32)] * (count * outs_each),
         grid_spec=pltpu.PrefetchScalarGridSpec(
             num_scalar_prefetch=1,
             grid=(count, blocks // step),
             in_specs=[
                 pl.BlockSpec((step, sub, depth), lambda p, g, d: (g, d[p], 0)),
-                pl.BlockSpec(memory_space=pltpu.VMEM),
+                pl.BlockSpec((depth, across), lambda p, g, d: (0, chunk or 0)),
             ],
-            out_specs=[pl.BlockSpec(memory_space=pltpu.VMEM)] * (count * chunks),
+            out_specs=[pl.BlockSpec(memory_space=pltpu.VMEM)] * (count * outs_each),
         ),
         cost_estimate=pl.CostEstimate(
-            flops=2 * count * blocks * sub * depth * width * chunks,
-            bytes_accessed=count * blocks * sub * (2 * depth + 4 * width * chunks) + 2 * depth * width * chunks,
+            flops=2 * count * blocks * sub * depth * across,
+            bytes_accessed=count * blocks * sub * (2 * depth + 4 * across) + 2 * depth * across,
             transcendentals=0,
         ),
         compiler_params=grant(28),
         name="product_pieces",
     )(jnp.stack(dests), panel, sketch)
-    return [outs[k * chunks : (k + 1) * chunks] for k in range(count)]
+    return [outs[k * outs_each : (k + 1) * outs_each] for k in range(count)]
 
 
 def pack_slots(held, inverse, slots):
@@ -183,7 +186,8 @@
             return jnp.where(row_id == col_id, 1.0, 0.0)
 
         def half_lower(e):
-            return jnp.where(row_id > col_id, e, jnp.where(row_id == col_id, 0.5 * e, 0.0))
+            rows, columns = row_id[: e.shape[0], : e.shape[1]], col_id[: e.shape[0], : e.shape[1]]
+            return jnp.where(rows > columns, e, jnp.where(rows == columns, 0.5 * e, 0.0))
 
         g = g_ref[...]
         diagonal = jnp.where(row_id == col_id, g, 0.0)
@@ -193,24 +197,54 @@
         start = g * down * across - eye()
         e_ref[...] = start
 
+        half = n // 2
+        top, low = slice(0, half), slice(half, n)
+
+        def subtract_product(fb, xb):
+            x_ref[top, top] = x_ref[top, top] - plain(fb[top, top], xb[top, top])
+            x_ref[low, top] = x_ref[low, top] - plain(fb[low, :], xb[:, top])
+            x_ref[low, low] = x_ref[low, low] - plain(fb[low, low], xb[low, low])
+
         def rough(state):
             e = e_ref[...]
             f = half_lower(e)
             fb, eb = f.astype(jnp.bfloat16), e.astype(jnp.bfloat16)
-            t = plain(fb, eb)
-            e = on_last((f + t).astype(jnp.bfloat16), fb) - t - on_last(eb, fb)
-            e_ref[...] = e
-            x = x_ref[...]
-            x_ref[...] = x - plain(fb, x.astype(jnp.bfloat16))
-            return state[0] + 1, jnp.sum(e * e)
+            t = jnp.concatenate([plain(fb[top, top], eb[top, :]), plain(fb[low, :], eb)], axis=0)
+            w = (f + t - e).astype(jnp.bfloat16)
+            left = on_last(w[:, top], fb[top, top]) - t[:, top]
+            right = on_last(w, fb[low, :]) - t[:, low]
+            e_ref[:, top] = left
+            e_ref[:, low] = right
+            subtract_product(fb, x_ref[...].astype(jnp.bfloat16))
+            return state[0] + 1, jnp.sum(left * left) + jnp.sum(right * right)
 
         lax.while_loop(lambda s: (s[0] < 12) & (s[1] > small) & (s[1] < 1e6), rough, (0, jnp.sum(start * start)))
 
         def fine(state):
-            x = split(x_ref[...])
-            e = triple(on_last, split(triple(plain, x, split(g_ref[...]))), x) - eye()
-            x_ref[...] = x_ref[...] - plain(half_lower(e).astype(jnp.bfloat16), x[0])
-            return state[0] + 1, jnp.sum(e * e)
+            x, g = split(x_ref[...]), split(g_ref[...])
+
+            def cut(pair, rows, columns):
+                return pair[0][rows, columns], pair[1][rows, columns]
+
+            every = slice(0, n)
+            upper = split(triple(plain, cut(x, top, top), cut(g, top, top)))
+            lower = split(triple(plain, cut(x, low, every), g))
+            first = cut(x, top, top)
+            corner = jnp.where(row_id[top, top] == col_id[top, top], 1.0, 0.0)
+            e_top = triple(on_last, upper, first) - corner
+            e_side = triple(on_last, cut(lower, every, top), first)
+            e_low = triple(on_last, lower, cut(x, low, every)) - corner
+            f_top, f_low = half_lower(e_top), half_lower(e_low)
+            fb = jnp.concatenate(
+                [
+                    jnp.concatenate([f_top, jnp.zeros_like(f_top)], axis=1),
+                    jnp.concatenate([e_side, f_low], axis=1),
+                ],
+                axis=0,
+            ).astype(jnp.bfloat16)
+            subtract_product(fb, x[0])
+            size = jnp.sum(e_top * e_top) + 2.0 * jnp.sum(e_side * e_side) + jnp.sum(e_low * e_low)
+            return state[0] + 1, size
 
         _, last = lax.while_loop(
             lambda s: (s[0] < 4) & jnp.logical_not(s[1] < enough), fine, (0, jnp.float32(1.0))
@@ -238,9 +272,15 @@
             lax.fori_loop(0, n, eliminate, 0)
 
         split_share = split(share_ref[...])
-        for k in range(count):
-            strip = pl.multiple_of((here_ref[2] ^ k) * tile, tile)
-            out_refs[k][...] = triple(on_last, split_share, split(x_ref[pl.ds(strip, tile), :]))
+        for i in range(count):
+            upto = slice(0, (i + 1) * tile)
+            strip = split(x_ref[i * tile : (i + 1) * tile, upto])
+            product = triple(on_last, (split_share[0][:, upto], split_share[1][:, upto]), strip)
+            for k in range(count):
+
+                @pl.when(here_ref[2] == (i ^ k))
+                def _():
+                    out_refs[k][...] = product
 
     return pl.pallas_call(
         kernel,
@@ -324,7 +364,8 @@
             wants += [clipped(up_dest), clipped(down_dest)]
     wants.append(col_here)
     panel = pltpu.with_memory_space_constraint(panel, pltpu.HBM)
-    products = [*product_pieces(panel, sketch, wants[:1], sub, COLUMN_CHUNKS)]
+    sketch = pltpu.with_memory_space_constraint(sketch, pltpu.HBM)
+    products = [[product_pieces(panel, sketch, wants[:1], sub, COLUMN_CHUNKS, h)[0][0] for h in range(COLUMN_CHUNKS)]]
     products += product_pieces(panel, sketch, wants[1:], sub, COLUMN_CHUNKS)
 
     arrived = []

time: 326 us -> 322 us (0.988)
  waiting for transfers between devices: 65.2 us -> 58.6 us
    ppermute x6, waiting for transfers between devices: 24.3 us -> 17.4 us  [shards(): came_up = lax.ppermute(up, 'col', [(i, i + 1) for i in range(stage)])]
    pallas_call x2 -> x3, Pallas kernels: 13.3 us -> 17.2 us  [product_pieces(): pl.pallas_call(kernel, out_shape=[jax.ShapeDtypeStruct((blocks, sub, widt...]
  transfers between devices with their start and end apart: 35 -> 35, of which waited for: 19 -> 19; matrix products, arithmetic and copies ran while one was open for 3% -> 3% of each run, Pallas kernels for 4% -> 5%
where the time goes in v1:
time: 322 us; the launch traced here: 321 us
  Pallas kernels  186 us (58%)
  starting transfers between devices  65.3 us (20%)
  waiting for transfers between devices  58.6 us (18%)
  other arithmetic  10.6 us (3%)
    pallas_call x1, Pallas kernels, basis_pieces(): pl.pallas_call(kernel, out_shape=[jax.ShapeDtypeStruct((rows, tile), jnp....  164 us
    ppermute x14, waiting for transfers between devices, swap(): lax.ppermute(x, name, [(i, i ^ level) for i in range(lax.axis_size(name))])  33.5 us
    ppermute x6, starting transfers between devices, shards(): came_up = lax.ppermute(up, 'col', [(i, i + 1) for i in range(stage)])  24.4 us
    ppermute x6, waiting for transfers between devices, shards(): came_up = lax.ppermute(up, 'col', [(i, i + 1) for i in range(stage)])  17.4 us
    ppermute x14, starting transfers between devices, swap(): lax.ppermute(x, name, [(i, i ^ level) for i in range(lax.axis_size(name))])  17.3 us
    pallas_call x3, Pallas kernels, product_pieces(): pl.pallas_call(kernel, out_shape=[jax.ShapeDtypeStruct((blocks, sub, widt...  17.2 us
    ppermute x6, starting transfers between devices, shards(): came.append(lax.ppermute(slotted[k], both, pairs))  15.8 us
    ppermute x6, starting transfers between devices, shards(): lax.ppermute(down, 'col', [(i, i - 1) for i in range(cols - stage, cols)])  7.69 us
  transfers between devices with their start and end apart: 35, of which 19 were waited for; matrix products, arithmetic and copies ran while one was open for 3% of the time, Pallas kernels for 5%

profile of v1, /device:TPU:0, one launch (start us, length us, event | category | flops | bytes accessed | tf_op | source)
XLA Modules:
  0.0 321.4 jit_solution(2592554874379852968)
XLA Ops:
  0.0 3.5 %product_pieces.5 = f32[16,32,256]{2,1,0:T(8,128)S(1)} custom-call(s32[1]{0:T(128)} %bitcast.9.dest_ref, bf16[16,128,2048]{2,1,0:T(8,128)(2,1)} %bitcast.11, bf16[2048,512]{1,0:T(8,128)(2,1)} %b_ref.5), custom_call_target="tpu_custom_call" | custom-call | flops 536870912 | bytes 3670016 | tf_op jit(solution)/shard_map/product_pieces/pallas_call | solution.py:37
  3.5 5.8 %collective-permute-start.11 = (f32[16,32,256]{2,1,0:T(8,128)S(1)}, f32[16,32,256]{2,1,0:T(8,128)}, u32[]{:S(2)}, u32[]{:S(2)}) collective-permute-start(f32[16,32,256]{2,1,0:T(8,128)S(1)} %product_pieces.5), channel_id=1, source_target_pairs={{0,1},{4,5},{8,9},{12,13},{16,17},{20,21},{24,25},{28,29}} | collective-permute-start | bytes 1572872 | tf_op jit(solution)/shard_map/ppermute | solution.py:381
  10.7 3.5 %product_pieces.4 = f32[16,32,256]{2,1,0:T(8,128)S(1)} custom-call(s32[1]{0:T(128)} %bitcast.9.dest_ref, bf16[16,128,2048]{2,1,0:T(8,128)(2,1)} %bitcast.12, bf16[2048,512]{1,0:T(8,128)(2,1)} %b_ref.5), custom_call_target="tpu_custom_call" | custom-call | flops 536870912 | bytes 3670016 | tf_op jit(solution)/shard_map/product_pieces/pallas_call | solution.py:37
  14.2 2.1 collective-permute-start.1
  17.8 10.3 %product_pieces.3 = (f32[16,32,256]{2,1,0:T(8,128)S(1)}, f32[16,32,256]{2,1,0:T(8,128)S(1)}, f32[16,32,256]{2,1,0:T(8,128)S(1)}, f32[16,32,256]{2,1,0:T(8,128)S(...) custom-call(s32[4]{0:T(128)S(1)} %pad_add_fusion.2.dest_ref, ...), custom_call_target="tpu_custom_call" | custom-call | flops 4294967296 | bytes 14680064 | tf_op jit(solution)/shard_map/product_pieces/pallas_call | solution.py:37
  31.5 2.1 fusion.3
  33.6 4.9 %collective-permute-start.2 = (f32[16,32,256]{2,1,0:T(8,128)}, f32[16,32,256]{2,1,0:T(8,128)}, u32[]{:S(2)}, u32[]{:S(2)}) collective-permute-start(f32[16,32,256]{2,1,0:T(8,128)} %get-tuple-element.53), channel_id=1, source_target_pairs={{0,1},{1,2},{4,5},{5,6},{8,9},{9,10},{12,13},{13,14},{16,17},{17,1... | collective-permute-start | bytes 1572872 | tf_op jit(solution)/shard_map/ppermute | solution.py:381
  39.9 3.1 collective-permute-done.12
  43.1 5.2 %collective-permute-start.13 = (f32[16,32,256]{2,1,0:T(8,128)S(1)}, f32[16,32,256]{2,1,0:T(8,128)}, u32[]{:S(2)}, u32[]{:S(2)}) collective-permute-start(f32[16,32,256]{2,1,0:T(8,128)S(1)} %add.118), channel_id=1, source_target_pairs={{0,1},{1,2},{2,3},{4,5},{5,6},{6,7},{8,9},{9,10},{10,11},{12,13},{... | collective-permute-start | bytes 1572872 | tf_op jit(solution)/shard_map/ppermute | solution.py:381
  50.5 3.8 %collective-permute-done.2 = f32[16,32,256]{2,1,0:T(8,128)} collective-permute-done((f32[16,32,256]{2,1,0:T(8,128)}, f32[16,32,256]{2,1,0:T(8,128)}, u32[]{:S(2)}, u32[]{:S(2)}) %collective-permute-start.2) | collective-permute-done | bytes 524320 | tf_op jit(solution)/shard_map/ppermute | solution.py:381
  54.3 1.9 add.112
  56.2 5.2 %collective-permute-start.3 = (f32[16,32,256]{2,1,0:T(8,128)}, f32[16,32,256]{2,1,0:T(8,128)}, u32[]{:S(2)}, u32[]{:S(2)}) collective-permute-start(f32[16,32,256]{2,1,0:T(8,128)} %add.112), channel_id=1, source_target_pairs={{0,1},{1,2},{2,3},{4,5},{5,6},{6,7},{8,9},{9,10},{10,11},{12,13},{... | collective-permute-start | bytes 1572872 | tf_op jit(solution)/shard_map/ppermute | solution.py:381
  63.9 1.5 collective-permute-done.13
  67.0 8.9 %collective-permute-done.3 = f32[16,32,256]{2,1,0:T(8,128)} collective-permute-done((f32[16,32,256]{2,1,0:T(8,128)}, f32[16,32,256]{2,1,0:T(8,128)}, u32[]{:S(2)}, u32[]{:S(2)}) %collective-permute-start.3) | collective-permute-done | bytes 524320 | tf_op jit(solution)/shard_map/ppermute | solution.py:381
  79.5 4.4 %collective-permute-start.18 = (f32[12,32,256]{2,1,0:T(8,128)S(1)}, f32[12,32,256]{2,1,0:T(8,128)S(1)}, u32[]{:S(2)}, u32[]{:S(2)}) collective-permute-start(f32[12,32,256]{2,1,0:T(8,128)S(1)} %get-tuple-element.41), channel_id=1, source_target_pairs={{0,12},{4,8},{24,20},{28,16},{1,13},{5,9},{25,21},{29,17},{2,14},{... | collective-permute-start | bytes 1179656 | tf_op jit(solution)/shard_map/ppermute | solution.py:398
  85.2 2.5 collective-permute-start.20
  91.5 5.0 %collective-permute-start.9 = (f32[12,32,256]{2,1,0:T(8,128)S(1)}, f32[12,32,256]{2,1,0:T(8,128)S(1)}, u32[]{:S(2)}, u32[]{:S(2)}) collective-permute-start(f32[12,32,256]{2,1,0:T(8,128)S(1)} %get-tuple-element.34), channel_id=1, source_target_pairs={{0,8},{4,12},{24,16},{28,20},{1,9},{5,13},{25,17},{29,21},{2,10},{... | collective-permute-start | bytes 1179656 | tf_op jit(solution)/shard_map/ppermute | solution.py:398
  97.6 4.3 %collective-permute-done.8.refs_1_ = f32[12,32,256]{2,1,0:T(8,128)S(1)} collective-permute-done((f32[12,32,256]{2,1,0:T(8,128)S(1)}, f32[12,32,256]{2,1,0:T(8,128)S(1)}, u32[]{:S(2)}, u32[]{:S(2)}) %collective-permute-start.8) | collective-permute-done | bytes 393248 | tf_op jit(solution)/shard_map/ppermute | solution.py:398
  101.8 2.1 collective-permute-done.9.refs_2_
  105.5 1.6 collective-permute-done.21
  107.2 2.6 collective-permute-start.22
  111.2 1.5 collective-permute-done.22
  112.7 1.7 collective-permute-done.23
  115.4 3.5 %collective-permute-start.25 = (f32[160,128]{1,0:T(8,128)S(1)}, f32[160,128]{1,0:T(8,128)S(1)}, u32[]{:S(2)}, u32[]{:S(2)}) collective-permute-start(f32[160,128]{1,0:T(8,128)S(1)} %fusion.1), channel_id=1, source_target_pairs={{0,3},{1,2},{2,1},{3,0},{4,7},{5,6},{6,5},{7,4},{8,11},{9,10},{10,... | collective-permute-start | bytes 245768 | tf_op jit(solution)/shard_map/ppermute | solution.py:406
  121.8 4.6 %collective-permute-done.26 = f32[160,128]{1,0:T(8,128)S(1)} collective-permute-done((f32[160,128]{1,0:T(8,128)S(1)}, f32[160,128]{1,0:T(8,128)S(1)}, u32[]{:S(2)}, u32[]{:S(2)}) %collective-permute-start.26) | collective-permute-done | bytes 81952 | tf_op jit(solution)/shard_map/ppermute | solution.py:406
  128.7 1.9 collective-permute-start.30
  131.3 3.6 %collective-permute-done.29.refs_1_ = f32[320,128]{1,0:T(8,128)S(1)} collective-permute-done((f32[320,128]{1,0:T(8,128)S(1)}, f32[320,128]{1,0:T(8,128)S(1)}, u32[]{:S(2)}, u32[]{:S(2)}) %collective-permute-start.29) | collective-permute-done | bytes 163872 | tf_op jit(solution)/shard_map/ppermute | solution.py:406
  134.9 3.4 %collective-permute-done.30.refs_2_ = f32[320,128]{1,0:T(8,128)S(1)} collective-permute-done((f32[320,128]{1,0:T(8,128)S(1)}, f32[320,128]{1,0:T(8,128)S(1)}, u32[]{:S(2)}, u32[]{:S(2)}) %collective-permute-start.30) | collective-permute-done | bytes 163872 | tf_op jit(solution)/shard_map/ppermute | solution.py:406
  138.3 163.8 %basis_pieces.1 = (f32[384,128]{1,0:T(8,128)S(1)}, f32[384,128]{1,0:T(8,128)S(1)}, f32[384,128]{1,0:T(8,128)S(1)}, f32[384,128]{1,0:T(8,128)S(1)}) custom-call(s32[3]{0:T(128)S(1)} %pad_add_fusion.1.here_ref, f32[320,128]{1,0:T(8,128)S(1)} %pad_maximum_fusion.refs_0_, f32[320,128]{1,0:T(8,128)S(1)} %collective-permute-done.29.refs_1_, ...), custom_call_target="tpu_custom_call" | custom-call | flops 1610612736 | bytes 1835008 | tf_op jit(solution)/shard_map/basis_pieces/pallas_call | solution.py:285
  302.6 3.4 %collective-permute-start.33 = (f32[384,128]{1,0:T(8,128)S(1)}, f32[384,128]{1,0:T(8,128)S(1)}, u32[]{:S(2)}, u32[]{:S(2)}) collective-permute-start(f32[384,128]{1,0:T(8,128)S(1)} %get-tuple-element.49), channel_id=1, source_target_pairs={{0,2},{1,3},{2,0},{3,1},{4,6},{5,7},{6,4},{7,5},{8,10},{9,11},{10,... | collective-permute-start | bytes 589832 | tf_op jit(solution)/shard_map/ppermute | solution.py:406
  306.6 5.1 %collective-permute-done.32.refs_1_ = f32[384,128]{1,0:T(8,128)S(1)} collective-permute-done((f32[384,128]{1,0:T(8,128)S(1)}, f32[384,128]{1,0:T(8,128)S(1)}, u32[]{:S(2)}, u32[]{:S(2)}) %collective-permute-start.32) | collective-permute-done | bytes 196640 | tf_op jit(solution)/shard_map/ppermute | solution.py:406
  311.6 8.5 %collective-permute-done.33.refs_2_ = f32[384,128]{1,0:T(8,128)S(1)} collective-permute-done((f32[384,128]{1,0:T(8,128)S(1)}, f32[384,128]{1,0:T(8,128)S(1)}, u32[]{:S(2)}, u32[]{:S(2)}) %collective-permute-start.33) | collective-permute-done | bytes 196640 | tf_op jit(solution)/shard_map/ppermute | solution.py:406
  (71 shorter events, 36.1 us)
Async XLA Ops:
  3.5 24.6 %collective-permute-start.11 = (f32[16,32,256]{2,1,0:T(8,128)S(1)}, f32[16,32,256]{2,1,0:T(8,128)}, u32[]{:S(2)}, u32[]{:S(2)}) collective-permute-start(f32[16,32,256]{2,1,0:T(8,128)S(1)} %product_pieces.5), channel_id=1, source_target_pairs={{0,1},{4,5},{8,9},{12,13},{16,17},{20,21},{24,25},{28,29}} | collective-permute-start | bytes 1572872 | tf_op jit(solution)/shard_map/ppermute | solution.py:381
  9.2 18.9 %collective-permute-start.14 = (f32[16,32,256]{2,1,0:T(8,128)S(1)}, f32[16,32,256]{2,1,0:T(8,128)}, u32[]{:S(2)}, u32[]{:S(2)}) collective-permute-start(f32[16,32,256]{2,1,0:T(8,128)S(1)} %product_pieces.5), channel_id=1, source_target_pairs={{3,2},{7,6},{11,10},{15,14},{19,18},{23,22},{27,26},{31,30}} | collective-permute-start | bytes 1572872 | tf_op jit(solution)/shard_map/ppermute | solution.py:382
  14.2 17.3 %collective-permute-start.1 = (f32[16,32,256]{2,1,0:T(8,128)S(1)}, f32[16,32,256]{2,1,0:T(8,128)}, u32[]{:S(2)}, u32[]{:S(2)}) collective-permute-start(f32[16,32,256]{2,1,0:T(8,128)S(1)} %product_pieces.4), channel_id=1, source_target_pairs={{0,1},{4,5},{8,9},{12,13},{16,17},{20,21},{24,25},{28,29}} | collective-permute-start | bytes 1572872 | tf_op jit(solution)/shard_map/ppermute | solution.py:381
  16.2 15.2 %collective-permute-start.4 = (f32[16,32,256]{2,1,0:T(8,128)S(1)}, f32[16,32,256]{2,1,0:T(8,128)}, u32[]{:S(2)}, u32[]{:S(2)}) collective-permute-start(f32[16,32,256]{2,1,0:T(8,128)S(1)} %product_pieces.4), channel_id=1, source_target_pairs={{3,2},{7,6},{11,10},{15,14},{19,18},{23,22},{27,26},{31,30}} | collective-permute-start | bytes 1572872 | tf_op jit(solution)/shard_map/ppermute | solution.py:382
  29.4 13.6 %collective-permute-start.12 = (f32[16,32,256]{2,1,0:T(8,128)S(1)}, f32[16,32,256]{2,1,0:T(8,128)S(1)}, u32[]{:S(2)}, u32[]{:S(2)}) collective-permute-start(f32[16,32,256]{2,1,0:T(8,128)S(1)} %get-tuple-element.51), channel_id=1, source_target_pairs={{0,1},{1,2},{4,5},{5,6},{8,9},{9,10},{12,13},{13,14},{16,17},{17,1... | collective-permute-start | bytes 1572872 | tf_op jit(solution)/shard_map/ppermute | solution.py:381
  30.7 17.5 %collective-permute-start.15 = (f32[16,32,256]{2,1,0:T(8,128)S(1)}, f32[16,32,256]{2,1,0:T(8,128)S(1)}, u32[]{:S(2)}, u32[]{:S(2)}) collective-permute-start(f32[16,32,256]{2,1,0:T(8,128)S(1)} %get-tuple-element.52), channel_id=1, source_target_pairs={{2,1},{3,2},{6,5},{7,6},{10,9},{11,10},{14,13},{15,14},{18,17},{19... | collective-permute-start | bytes 1572872 | tf_op jit(solution)/shard_map/ppermute | solution.py:382
  33.6 20.8 %collective-permute-start.2 = (f32[16,32,256]{2,1,0:T(8,128)}, f32[16,32,256]{2,1,0:T(8,128)}, u32[]{:S(2)}, u32[]{:S(2)}) collective-permute-start(f32[16,32,256]{2,1,0:T(8,128)} %get-tuple-element.53), channel_id=1, source_target_pairs={{0,1},{1,2},{4,5},{5,6},{8,9},{9,10},{12,13},{13,14},{16,17},{17,1... | collective-permute-start | bytes 1572872 | tf_op jit(solution)/shard_map/ppermute | solution.py:381
  38.4 23.0 %collective-permute-start.5 = (f32[16,32,256]{2,1,0:T(8,128)S(1)}, f32[16,32,256]{2,1,0:T(8,128)}, u32[]{:S(2)}, u32[]{:S(2)}) collective-permute-start(f32[16,32,256]{2,1,0:T(8,128)S(1)} %get-tuple-element.54), channel_id=1, source_target_pairs={{2,1},{3,2},{6,5},{7,6},{10,9},{11,10},{14,13},{15,14},{18,17},{19... | collective-permute-start | bytes 1572872 | tf_op jit(solution)/shard_map/ppermute | solution.py:382
  43.1 22.4 %collective-permute-start.13 = (f32[16,32,256]{2,1,0:T(8,128)S(1)}, f32[16,32,256]{2,1,0:T(8,128)}, u32[]{:S(2)}, u32[]{:S(2)}) collective-permute-start(f32[16,32,256]{2,1,0:T(8,128)S(1)} %add.118), channel_id=1, source_target_pairs={{0,1},{1,2},{2,3},{4,5},{5,6},{6,7},{8,9},{9,10},{10,11},{12,13},{... | collective-permute-start | bytes 1572872 | tf_op jit(solution)/shard_map/ppermute | solution.py:381
  49.1 16.3 %collective-permute-start.16 = (f32[16,32,256]{2,1,0:T(8,128)}, f32[16,32,256]{2,1,0:T(8,128)}, u32[]{:S(2)}, u32[]{:S(2)}) collective-permute-start(f32[16,32,256]{2,1,0:T(8,128)} %add.121), channel_id=1, source_target_pairs={{1,0},{2,1},{3,2},{5,4},{6,5},{7,6},{9,8},{10,9},{11,10},{13,12},{... | collective-permute-start | bytes 1572872 | tf_op jit(solution)/shard_map/ppermute | solution.py:382
  50.4 16.4 %collective-permute-start = (s32[64]{0:T(128)S(1)}, s32[64]{0:T(128)S(1)}, u32[]{:S(2)}, u32[]{:S(2)}) collective-permute-start(s32[64]{0:T(128)S(1)} %bitcast.14), channel_id=1, source_target_pairs={{0,16},{16,0},{1,17},{17,1},{2,18},{18,2},{3,19},{19,3},{4,20},{20... | collective-permute-start | bytes 776 | tf_op jit(solution)/shard_map/ppermute | solution.py:347
  56.2 19.6 %collective-permute-start.3 = (f32[16,32,256]{2,1,0:T(8,128)}, f32[16,32,256]{2,1,0:T(8,128)}, u32[]{:S(2)}, u32[]{:S(2)}) collective-permute-start(f32[16,32,256]{2,1,0:T(8,128)} %add.112), channel_id=1, source_target_pairs={{0,1},{1,2},{2,3},{4,5},{5,6},{6,7},{8,9},{9,10},{10,11},{12,13},{... | collective-permute-start | bytes 1572872 | tf_op jit(solution)/shard_map/ppermute | solution.py:381
  62.6 13.7 %collective-permute-start.6 = (f32[16,32,256]{2,1,0:T(8,128)S(1)}, f32[16,32,256]{2,1,0:T(8,128)S(1)}, u32[]{:S(2)}, u32[]{:S(2)}) collective-permute-start(f32[16,32,256]{2,1,0:T(8,128)S(1)} %add.115), channel_id=1, source_target_pairs={{1,0},{2,1},{3,2},{5,4},{6,5},{7,6},{9,8},{10,9},{11,10},{13,12},{... | collective-permute-start | bytes 1572872 | tf_op jit(solution)/shard_map/ppermute | solution.py:382
  66.8 11.4 %collective-permute-start.17 = (f32[16,32,256]{2,1,0:T(8,128)S(1)}, f32[16,32,256]{2,1,0:T(8,128)S(1)}, u32[]{:S(2)}, u32[]{:S(2)}) collective-permute-start(f32[16,32,256]{2,1,0:T(8,128)S(1)} %add_add_fusion.refs_0_), channel_id=1, source_target_pairs={{0,16},{16,0},{1,17},{17,1},{2,18},{18,2},{3,19},{19,3},{4,20},{20... | collective-permute-start | bytes 1572872 | tf_op jit(solution)/shard_map/ppermute | solution.py:387
  77.4 10.2 %collective-permute-start.7 = (f32[16,32,256]{2,1,0:T(8,128)S(1)}, f32[16,32,256]{2,1,0:T(8,128)S(1)}, u32[]{:S(2)}, u32[]{:S(2)}) collective-permute-start(f32[16,32,256]{2,1,0:T(8,128)S(1)} %add_add_fusion.1.refs_0_), channel_id=1, source_target_pairs={{0,16},{16,0},{1,17},{17,1},{2,18},{18,2},{3,19},{19,3},{4,20},{20... | collective-permute-start | bytes 1572872 | tf_op jit(solution)/shard_map/ppermute | solution.py:387
  79.5 12.1 %collective-permute-start.18 = (f32[12,32,256]{2,1,0:T(8,128)S(1)}, f32[12,32,256]{2,1,0:T(8,128)S(1)}, u32[]{:S(2)}, u32[]{:S(2)}) collective-permute-start(f32[12,32,256]{2,1,0:T(8,128)S(1)} %get-tuple-element.41), channel_id=1, source_target_pairs={{0,12},{4,8},{24,20},{28,16},{1,13},{5,9},{25,21},{29,17},{2,14},{... | collective-permute-start | bytes 1179656 | tf_op jit(solution)/shard_map/ppermute | solution.py:398
  83.8 12.8 %collective-permute-start.19 = (f32[12,32,256]{2,1,0:T(8,128)S(1)}, f32[12,32,256]{2,1,0:T(8,128)S(1)}, u32[]{:S(2)}, u32[]{:S(2)}) collective-permute-start(f32[12,32,256]{2,1,0:T(8,128)S(1)} %get-tuple-element.42), channel_id=1, source_target_pairs={{0,8},{4,12},{24,16},{28,20},{1,9},{5,13},{25,17},{29,21},{2,10},{... | collective-permute-start | bytes 1179656 | tf_op jit(solution)/shard_map/ppermute | solution.py:398
  85.2 11.4 %collective-permute-start.20 = (f32[12,32,256]{2,1,0:T(8,128)S(1)}, f32[12,32,256]{2,1,0:T(8,128)S(1)}, u32[]{:S(2)}, u32[]{:S(2)}) collective-permute-start(f32[12,32,256]{2,1,0:T(8,128)S(1)} %get-tuple-element.43), channel_id=1, source_target_pairs={{0,4},{8,12},{20,16},{28,24},{1,5},{9,13},{21,17},{29,25},{2,6},{1... | collective-permute-start | bytes 1179656 | tf_op jit(solution)/shard_map/ppermute | solution.py:398
  88.9 8.7 %collective-permute-start.10 = (f32[12,32,256]{2,1,0:T(8,128)S(1)}, f32[12,32,256]{2,1,0:T(8,128)S(1)}, u32[]{:S(2)}, u32[]{:S(2)}) collective-permute-start(f32[12,32,256]{2,1,0:T(8,128)S(1)} %get-tuple-element.35), channel_id=1, source_target_pairs={{0,4},{8,12},{20,16},{28,24},{1,5},{9,13},{21,17},{29,25},{2,6},{1... | collective-permute-start | bytes 1179656 | tf_op jit(solution)/shard_map/ppermute | solution.py:398
  90.2 11.6 %collective-permute-start.8 = (f32[12,32,256]{2,1,0:T(8,128)S(1)}, f32[12,32,256]{2,1,0:T(8,128)S(1)}, u32[]{:S(2)}, u32[]{:S(2)}) collective-permute-start(f32[12,32,256]{2,1,0:T(8,128)S(1)} %get-tuple-element.33), channel_id=1, source_target_pairs={{0,12},{4,8},{24,20},{28,16},{1,13},{5,9},{25,21},{29,17},{2,14},{... | collective-permute-start | bytes 1179656 | tf_op jit(solution)/shard_map/ppermute | solution.py:398
  91.5 12.4 %collective-permute-start.9 = (f32[12,32,256]{2,1,0:T(8,128)S(1)}, f32[12,32,256]{2,1,0:T(8,128)S(1)}, u32[]{:S(2)}, u32[]{:S(2)}) collective-permute-start(f32[12,32,256]{2,1,0:T(8,128)S(1)} %get-tuple-element.34), channel_id=1, source_target_pairs={{0,8},{4,12},{24,16},{28,20},{1,9},{5,13},{25,17},{29,21},{2,10},{... | collective-permute-start | bytes 1179656 | tf_op jit(solution)/shard_map/ppermute | solution.py:398
  107.2 5.5 %collective-permute-start.22 = (f32[160,128]{1,0:T(8,128)S(1)}, f32[160,128]{1,0:T(8,128)S(1)}, u32[]{:S(2)}, u32[]{:S(2)}) collective-permute-start(f32[160,128]{1,0:T(8,128)S(1)} %get-tuple-element.55), channel_id=1, source_target_pairs={{0,12},{4,8},{8,4},{12,0},{1,13},{5,9},{9,5},{13,1},{2,14},{6,10},... | collective-permute-start | bytes 245768 | tf_op jit(solution)/shard_map/ppermute | solution.py:406
  109.8 5.6 %collective-permute-start.24 = (f32[160,128]{1,0:T(8,128)S(1)}, f32[160,128]{1,0:T(8,128)S(1)}, u32[]{:S(2)}, u32[]{:S(2)}) collective-permute-start(f32[160,128]{1,0:T(8,128)S(1)} %get-tuple-element.56), channel_id=1, source_target_pairs={{0,4},{4,0},{8,12},{12,8},{1,5},{5,1},{9,13},{13,9},{2,6},{6,2},{1... | collective-permute-start | bytes 245768 | tf_op jit(solution)/shard_map/ppermute | solution.py:406
  115.4 6.4 %collective-permute-start.25 = (f32[160,128]{1,0:T(8,128)S(1)}, f32[160,128]{1,0:T(8,128)S(1)}, u32[]{:S(2)}, u32[]{:S(2)}) collective-permute-start(f32[160,128]{1,0:T(8,128)S(1)} %fusion.1), channel_id=1, source_target_pairs={{0,3},{1,2},{2,1},{3,0},{4,7},{5,6},{6,5},{7,4},{8,11},{9,10},{10,... | collective-permute-start | bytes 245768 | tf_op jit(solution)/shard_map/ppermute | solution.py:406
  118.9 7.5 %collective-permute-start.26 = (f32[160,128]{1,0:T(8,128)S(1)}, f32[160,128]{1,0:T(8,128)S(1)}, u32[]{:S(2)}, u32[]{:S(2)}) collective-permute-start(f32[160,128]{1,0:T(8,128)S(1)} %fusion.1), channel_id=1, source_target_pairs={{0,2},{1,3},{2,0},{3,1},{4,6},{5,7},{6,4},{7,5},{8,10},{9,11},{10,... | collective-permute-start | bytes 245768 | tf_op jit(solution)/shard_map/ppermute | solution.py:406
  120.4 6.0 %collective-permute-start.27 = (f32[160,128]{1,0:T(8,128)S(1)}, f32[160,128]{1,0:T(8,128)S(1)}, u32[]{:S(2)}, u32[]{:S(2)}) collective-permute-start(f32[160,128]{1,0:T(8,128)S(1)} %fusion.1), channel_id=1, source_target_pairs={{0,1},{1,0},{2,3},{3,2},{4,5},{5,4},{6,7},{7,6},{8,9},{9,8},{10,11... | collective-permute-start | bytes 245768 | tf_op jit(solution)/shard_map/ppermute | solution.py:406
  127.8 7.1 %collective-permute-start.29 = (f32[320,128]{1,0:T(8,128)S(1)}, f32[320,128]{1,0:T(8,128)S(1)}, u32[]{:S(2)}, u32[]{:S(2)}) collective-permute-start(f32[320,128]{1,0:T(8,128)S(1)} %pad_maximum_fusion.refs_0_), channel_id=1, source_target_pairs={{0,4},{4,0},{8,12},{12,8},{1,5},{5,1},{9,13},{13,9},{2,6},{6,2},{1... | collective-permute-start | bytes 491528 | tf_op jit(solution)/shard_map/ppermute | solution.py:406
  128.7 9.7 %collective-permute-start.30 = (f32[320,128]{1,0:T(8,128)S(1)}, f32[320,128]{1,0:T(8,128)S(1)}, u32[]{:S(2)}, u32[]{:S(2)}) collective-permute-start(f32[320,128]{1,0:T(8,128)S(1)} %pad_maximum_fusion.refs_0_), channel_id=1, source_target_pairs={{0,8},{4,12},{8,0},{12,4},{1,9},{5,13},{9,1},{13,5},{2,10},{6,14},... | collective-permute-start | bytes 491528 | tf_op jit(solution)/shard_map/ppermute | solution.py:406
  130.6 7.8 %collective-permute-start.31 = (f32[320,128]{1,0:T(8,128)S(1)}, f32[320,128]{1,0:T(8,128)S(1)}, u32[]{:S(2)}, u32[]{:S(2)}) collective-permute-start(f32[320,128]{1,0:T(8,128)S(1)} %pad_maximum_fusion.refs_0_), channel_id=1, source_target_pairs={{0,12},{4,8},{8,4},{12,0},{1,13},{5,9},{9,5},{13,1},{2,14},{6,10},... | collective-permute-start | bytes 491528 | tf_op jit(solution)/shard_map/ppermute | solution.py:406
  302.1 9.5 %collective-permute-start.32 = (f32[384,128]{1,0:T(8,128)S(1)}, f32[384,128]{1,0:T(8,128)S(1)}, u32[]{:S(2)}, u32[]{:S(2)}) collective-permute-start(f32[384,128]{1,0:T(8,128)S(1)} %get-tuple-element.48), channel_id=1, source_target_pairs={{0,1},{1,0},{2,3},{3,2},{4,5},{5,4},{6,7},{7,6},{8,9},{9,8},{10,11... | collective-permute-start | bytes 589832 | tf_op jit(solution)/shard_map/ppermute | solution.py:406
  302.6 17.6 %collective-permute-start.33 = (f32[384,128]{1,0:T(8,128)S(1)}, f32[384,128]{1,0:T(8,128)S(1)}, u32[]{:S(2)}, u32[]{:S(2)}) collective-permute-start(f32[384,128]{1,0:T(8,128)S(1)} %get-tuple-element.49), channel_id=1, source_target_pairs={{0,2},{1,3},{2,0},{3,1},{4,6},{5,7},{6,4},{7,5},{8,10},{9,11},{10,... | collective-permute-start | bytes 589832 | tf_op jit(solution)/shard_map/ppermute | solution.py:406
  306.0 14.2 %collective-permute-start.34 = (f32[384,128]{1,0:T(8,128)S(1)}, f32[384,128]{1,0:T(8,128)S(1)}, u32[]{:S(2)}, u32[]{:S(2)}) collective-permute-start(f32[384,128]{1,0:T(8,128)S(1)} %get-tuple-element.50), channel_id=1, source_target_pairs={{0,3},{1,2},{2,1},{3,0},{4,7},{5,6},{6,5},{7,4},{8,11},{9,10},{10,... | collective-permute-start | bytes 589832 | tf_op jit(solution)/shard_map/ppermute | solution.py:406
  (4 other events, 40.3 us)

commit v2 on v1

--- a/solution.py
+++ b/solution.py
@@ -154,21 +154,21 @@
     return outs[0], list(outs[1:])
 
 
-def basis_pieces(pieces, share, here, siblings, tile):
+def basis_pieces(pieces, share, here, members, tile):
     rows, n = share.shape
     count = n // tile
-    members = len(pieces)
+    siblings = len(pieces)
     height = count * (count + 1) // 2 * tile
     piece = height // (siblings * members)
     small, enough = 1e-2, 4e-4
 
     def kernel(here_ref, *refs):
-        piece_refs, share_ref = refs[:members], refs[members]
-        out_refs, (packed_ref, g_ref, x_ref, e_ref) = refs[members + 1 : -4], refs[-4:]
+        piece_refs, share_ref = refs[:siblings], refs[siblings]
+        out_refs, (packed_ref, g_ref, x_ref, e_ref) = refs[siblings + 1 : -4], refs[-4:]
         for s in range(siblings):
             for m in range(members):
                 spot = ((here_ref[0] ^ s) * members + (here_ref[1] ^ m)) * piece
-                packed_ref[pl.ds(pl.multiple_of(spot, 8), piece), :] = piece_refs[m][s * piece : (s + 1) * piece, :]
+                packed_ref[pl.ds(pl.multiple_of(spot, 8), piece), :] = piece_refs[s][m * piece : (m + 1) * piece, :]
         at = 0
         for i in range(count):
             here = slice(i * tile, (i + 1) * tile)
@@ -285,7 +285,7 @@
     return pl.pallas_call(
         kernel,
         out_shape=[jax.ShapeDtypeStruct((rows, tile), jnp.float32)] * count,
-        in_specs=[pl.BlockSpec(memory_space=pltpu.SMEM)] + [pl.BlockSpec(memory_space=pltpu.VMEM)] * (1 + members),
+        in_specs=[pl.BlockSpec(memory_space=pltpu.SMEM)] + [pl.BlockSpec(memory_space=pltpu.VMEM)] * (1 + siblings),
         out_specs=[pl.BlockSpec(memory_space=pltpu.VMEM)] * count,
         scratch_shapes=[pltpu.VMEM((height, tile), jnp.float32)] + [pltpu.VMEM((n, n), jnp.float32)] * 3,
         cost_estimate=pl.CostEstimate(flops=12 * n * n * n, bytes_accessed=4 * n * (n + rows), transcendentals=0),
@@ -414,14 +414,16 @@
     for k in range(1, rows)[::-1]:
         piece = piece + swap(parts[k], "row", k)
     piece = piece + sum(swap(piece, "col", k) for k in range(1, cols)[::-1])
-    mine = [piece]
+    back = {0: piece}
+    for k in range(1, rows)[::-1]:
+        back[k] = swap(piece, "row", k)
+    pieces = [jnp.concatenate([back[k] for k in range(rows)], axis=0)]
     for level in levels:
-        mine = mine + [swap(p, "front", level) for p in mine]
-    mine = jnp.concatenate(mine, axis=0)
-    pieces = [mine] + [swap(mine, "row", k) for k in range(1, rows)]
-
-    basis = basis_pieces(pieces, share, here, siblings, width)
-    pieces = [basis[0]] + [swap(basis[k], "col", k) for k in range(1, cols)]
+        pieces = pieces + [swap(p, "front", level) for p in pieces]
+
+    basis = basis_pieces(pieces, share, here, rows, width)
+    came = {k: swap(basis[k], "col", k) for k in range(1, cols)[::-1]}
+    pieces = [basis[0]] + [came[k] for k in range(1, cols)]
     return lay_out(pieces, col_here, slots, sub, BLK)
 
 

time: 322 us -> 321 us (level)
  transfers between devices with their start and end apart: 35 -> 35, of which waited for: 19 -> 20; matrix products, arithmetic and copies ran while one was open for 3% -> 3% of each run, Pallas kernels for 5% -> 5%
where the time goes in v2:
time: 321 us; the launch traced here: 319 us
  Pallas kernels  186 us (58%)
  starting transfers between devices  65.3 us (20%)
  waiting for transfers between devices  56.6 us (18%)
  other arithmetic  10.6 us (3%)
    pallas_call x1, Pallas kernels, basis_pieces(): pl.pallas_call(kernel, out_shape=[jax.ShapeDtypeStruct((rows, tile), jnp....  164 us
    ppermute x14, waiting for transfers between devices, swap(): lax.ppermute(x, name, [(i, i ^ level) for i in range(lax.axis_size(name))])  31.5 us
    ppermute x6, starting transfers between devices, shards(): came_up = lax.ppermute(up, 'col', [(i, i + 1) for i in range(stage)])  24.4 us
    ppermute x6, waiting for transfers between devices, shards(): came_up = lax.ppermute(up, 'col', [(i, i + 1) for i in range(stage)])  17.4 us
    ppermute x14, starting transfers between devices, swap(): lax.ppermute(x, name, [(i, i ^ level) for i in range(lax.axis_size(name))])  17.3 us
    pallas_call x3, Pallas kernels, product_pieces(): pl.pallas_call(kernel, out_shape=[jax.ShapeDtypeStruct((blocks, sub, widt...  17.2 us
    ppermute x6, starting transfers between devices, shards(): came.append(lax.ppermute(slotted[k], both, pairs))  15.8 us
    ppermute x6, starting transfers between devices, shards(): lax.ppermute(down, 'col', [(i, i - 1) for i in range(cols - stage, cols)])  7.69 us
  transfers between devices with their start and end apart: 35, of which 20 were waited for; matrix products, arithmetic and copies ran while one was open for 3% of the time, Pallas kernels for 5%

profile of v2, /device:TPU:0, one launch (start us, length us, event | category | flops | bytes accessed | tf_op | source)
XLA Modules:
  0.0 319.4 jit_solution(14426990039449672746)
XLA Ops:
  0.0 3.5 %product_pieces.5 = f32[16,32,256]{2,1,0:T(8,128)S(1)} custom-call(s32[1]{0:T(128)} %bitcast.9.dest_ref, bf16[16,128,2048]{2,1,0:T(8,128)(2,1)} %bitcast.11, bf16[2048,512]{1,0:T(8,128)(2,1)} %b_ref.5), custom_call_target="tpu_custom_call" | custom-call | flops 536870912 | bytes 3670016 | tf_op jit(solution)/shard_map/product_pieces/pallas_call | solution.py:37
  3.5 5.8 %collective-permute-start.11 = (f32[16,32,256]{2,1,0:T(8,128)S(1)}, f32[16,32,256]{2,1,0:T(8,128)}, u32[]{:S(2)}, u32[]{:S(2)}) collective-permute-start(f32[16,32,256]{2,1,0:T(8,128)S(1)} %product_pieces.5), channel_id=1, source_target_pairs={{0,1},{4,5},{8,9},{12,13},{16,17},{20,21},{24,25},{28,29}} | collective-permute-start | bytes 1572872 | tf_op jit(solution)/shard_map/ppermute | solution.py:381
  10.7 3.5 %product_pieces.4 = f32[16,32,256]{2,1,0:T(8,128)S(1)} custom-call(s32[1]{0:T(128)} %bitcast.9.dest_ref, bf16[16,128,2048]{2,1,0:T(8,128)(2,1)} %bitcast.12, bf16[2048,512]{1,0:T(8,128)(2,1)} %b_ref.5), custom_call_target="tpu_custom_call" | custom-call | flops 536870912 | bytes 3670016 | tf_op jit(solution)/shard_map/product_pieces/pallas_call | solution.py:37
  14.2 2.1 collective-permute-start.1
  17.8 10.3 %product_pieces.3 = (f32[16,32,256]{2,1,0:T(8,128)S(1)}, f32[16,32,256]{2,1,0:T(8,128)S(1)}, f32[16,32,256]{2,1,0:T(8,128)S(1)}, f32[16,32,256]{2,1,0:T(8,128)S(...) custom-call(s32[4]{0:T(128)S(1)} %pad_add_fusion.2.dest_ref, ...), custom_call_target="tpu_custom_call" | custom-call | flops 4294967296 | bytes 14680064 | tf_op jit(solution)/shard_map/product_pieces/pallas_call | solution.py:37
  31.5 2.1 fusion.3
  33.6 4.9 %collective-permute-start.2 = (f32[16,32,256]{2,1,0:T(8,128)}, f32[16,32,256]{2,1,0:T(8,128)}, u32[]{:S(2)}, u32[]{:S(2)}) collective-permute-start(f32[16,32,256]{2,1,0:T(8,128)} %get-tuple-element.53), channel_id=1, source_target_pairs={{0,1},{1,2},{4,5},{5,6},{8,9},{9,10},{12,13},{13,14},{16,17},{17,1... | collective-permute-start | bytes 1572872 | tf_op jit(solution)/shard_map/ppermute | solution.py:381
  39.9 3.1 collective-permute-done.12
  43.1 5.2 %collective-permute-start.13 = (f32[16,32,256]{2,1,0:T(8,128)S(1)}, f32[16,32,256]{2,1,0:T(8,128)}, u32[]{:S(2)}, u32[]{:S(2)}) collective-permute-start(f32[16,32,256]{2,1,0:T(8,128)S(1)} %add.118), channel_id=1, source_target_pairs={{0,1},{1,2},{2,3},{4,5},{5,6},{6,7},{8,9},{9,10},{10,11},{12,13},{... | collective-permute-start | bytes 1572872 | tf_op jit(solution)/shard_map/ppermute | solution.py:381
  50.5 3.8 %collective-permute-done.2 = f32[16,32,256]{2,1,0:T(8,128)} collective-permute-done((f32[16,32,256]{2,1,0:T(8,128)}, f32[16,32,256]{2,1,0:T(8,128)}, u32[]{:S(2)}, u32[]{:S(2)}) %collective-permute-start.2) | collective-permute-done | bytes 524320 | tf_op jit(solution)/shard_map/ppermute | solution.py:381
  54.3 1.9 add.112
  56.2 5.2 %collective-permute-start.3 = (f32[16,32,256]{2,1,0:T(8,128)}, f32[16,32,256]{2,1,0:T(8,128)}, u32[]{:S(2)}, u32[]{:S(2)}) collective-permute-start(f32[16,32,256]{2,1,0:T(8,128)} %add.112), channel_id=1, source_target_pairs={{0,1},{1,2},{2,3},{4,5},{5,6},{6,7},{8,9},{9,10},{10,11},{12,13},{... | collective-permute-start | bytes 1572872 | tf_op jit(solution)/shard_map/ppermute | solution.py:381
  63.9 1.5 collective-permute-done.13
  67.0 8.9 %collective-permute-done.3 = f32[16,32,256]{2,1,0:T(8,128)} collective-permute-done((f32[16,32,256]{2,1,0:T(8,128)}, f32[16,32,256]{2,1,0:T(8,128)}, u32[]{:S(2)}, u32[]{:S(2)}) %collective-permute-start.3) | collective-permute-done | bytes 524320 | tf_op jit(solution)/shard_map/ppermute | solution.py:381
  79.5 4.4 %collective-permute-start.18 = (f32[12,32,256]{2,1,0:T(8,128)S(1)}, f32[12,32,256]{2,1,0:T(8,128)S(1)}, u32[]{:S(2)}, u32[]{:S(2)}) collective-permute-start(f32[12,32,256]{2,1,0:T(8,128)S(1)} %get-tuple-element.41), channel_id=1, source_target_pairs={{0,12},{4,8},{24,20},{28,16},{1,13},{5,9},{25,21},{29,17},{2,14},{... | collective-permute-start | bytes 1179656 | tf_op jit(solution)/shard_map/ppermute | solution.py:398
  85.2 2.5 collective-permute-start.20
  91.5 5.0 %collective-permute-start.9 = (f32[12,32,256]{2,1,0:T(8,128)S(1)}, f32[12,32,256]{2,1,0:T(8,128)S(1)}, u32[]{:S(2)}, u32[]{:S(2)}) collective-permute-start(f32[12,32,256]{2,1,0:T(8,128)S(1)} %get-tuple-element.34), channel_id=1, source_target_pairs={{0,8},{4,12},{24,16},{28,20},{1,9},{5,13},{25,17},{29,21},{2,10},{... | collective-permute-start | bytes 1179656 | tf_op jit(solution)/shard_map/ppermute | solution.py:398
  97.6 4.3 %collective-permute-done.8.refs_1_ = f32[12,32,256]{2,1,0:T(8,128)S(1)} collective-permute-done((f32[12,32,256]{2,1,0:T(8,128)S(1)}, f32[12,32,256]{2,1,0:T(8,128)S(1)}, u32[]{:S(2)}, u32[]{:S(2)}) %collective-permute-start.8) | collective-permute-done | bytes 393248 | tf_op jit(solution)/shard_map/ppermute | solution.py:398
  101.8 2.1 collective-permute-done.9.refs_2_
  105.5 1.6 collective-permute-done.21
  107.2 2.6 collective-permute-start.22
  112.7 1.7 collective-permute-done.23
  115.4 3.5 %collective-permute-start.25 = (f32[160,128]{1,0:T(8,128)S(1)}, f32[160,128]{1,0:T(8,128)S(1)}, u32[]{:S(2)}, u32[]{:S(2)}) collective-permute-start(f32[160,128]{1,0:T(8,128)S(1)} %fusion.1), channel_id=1, source_target_pairs={{0,3},{1,2},{2,1},{3,0},{4,7},{5,6},{6,5},{7,4},{8,11},{9,10},{10,... | collective-permute-start | bytes 245768 | tf_op jit(solution)/shard_map/ppermute | solution.py:406
  121.8 4.6 %collective-permute-done.26 = f32[160,128]{1,0:T(8,128)S(1)} collective-permute-done((f32[160,128]{1,0:T(8,128)S(1)}, f32[160,128]{1,0:T(8,128)S(1)}, u32[]{:S(2)}, u32[]{:S(2)}) %collective-permute-start.26) | collective-permute-done | bytes 81952 | tf_op jit(solution)/shard_map/ppermute | solution.py:406
  127.3 1.9 collective-permute-start.29
  131.1 1.5 collective-permute-done.29
  132.6 2.0 collective-permute-done.30
  134.6 1.6 collective-permute-done.31.refs_1_
  136.3 163.8 %basis_pieces.1 = (f32[384,128]{1,0:T(8,128)S(1)}, f32[384,128]{1,0:T(8,128)S(1)}, f32[384,128]{1,0:T(8,128)S(1)}, f32[384,128]{1,0:T(8,128)S(1)}) custom-call(s32[3]{0:T(128)S(1)} %pad_add_fusion.1.here_ref, f32[640,128]{1,0:T(8,128)S(1)} %pad_maximum_fusion.refs_0_, f32[640,128]{1,0:T(8,128)S(1)} %collective-permute-done.31.refs_1_, ...), custom_call_target="tpu_custom_call" | custom-call | flops 1610612736 | bytes 1835008 | tf_op jit(solution)/shard_map/basis_pieces/pallas_call | solution.py:285
  300.6 3.4 %collective-permute-start.33 = (f32[384,128]{1,0:T(8,128)S(1)}, f32[384,128]{1,0:T(8,128)S(1)}, u32[]{:S(2)}, u32[]{:S(2)}) collective-permute-start(f32[384,128]{1,0:T(8,128)S(1)} %get-tuple-element.49), channel_id=1, source_target_pairs={{0,2},{1,3},{2,0},{3,1},{4,6},{5,7},{6,4},{7,5},{8,10},{9,11},{10,... | collective-permute-start | bytes 589832 | tf_op jit(solution)/shard_map/ppermute | solution.py:406
  304.5 6.2 %collective-permute-done.32.refs_1_ = f32[384,128]{1,0:T(8,128)S(1)} collective-permute-done((f32[384,128]{1,0:T(8,128)S(1)}, f32[384,128]{1,0:T(8,128)S(1)}, u32[]{:S(2)}, u32[]{:S(2)}) %collective-permute-start.32) | collective-permute-done | bytes 196640 | tf_op jit(solution)/shard_map/ppermute | solution.py:406
  310.8 7.4 %collective-permute-done.33.refs_2_ = f32[384,128]{1,0:T(8,128)S(1)} collective-permute-done((f32[384,128]{1,0:T(8,128)S(1)}, f32[384,128]{1,0:T(8,128)S(1)}, u32[]{:S(2)}, u32[]{:S(2)}) %collective-permute-start.33) | collective-permute-done | bytes 196640 | tf_op jit(solution)/shard_map/ppermute | solution.py:406
  (71 shorter events, 37.4 us)
Async XLA Ops:
  3.5 24.6 %collective-permute-start.11 = (f32[16,32,256]{2,1,0:T(8,128)S(1)}, f32[16,32,256]{2,1,0:T(8,128)}, u32[]{:S(2)}, u32[]{:S(2)}) collective-permute-start(f32[16,32,256]{2,1,0:T(8,128)S(1)} %product_pieces.5), channel_id=1, source_target_pairs={{0,1},{4,5},{8,9},{12,13},{16,17},{20,21},{24,25},{28,29}} | collective-permute-start | bytes 1572872 | tf_op jit(solution)/shard_map/ppermute | solution.py:381
  9.2 18.9 %collective-permute-start.14 = (f32[16,32,256]{2,1,0:T(8,128)S(1)}, f32[16,32,256]{2,1,0:T(8,128)}, u32[]{:S(2)}, u32[]{:S(2)}) collective-permute-start(f32[16,32,256]{2,1,0:T(8,128)S(1)} %product_pieces.5), channel_id=1, source_target_pairs={{3,2},{7,6},{11,10},{15,14},{19,18},{23,22},{27,26},{31,30}} | collective-permute-start | bytes 1572872 | tf_op jit(solution)/shard_map/ppermute | solution.py:382
  14.2 17.3 %collective-permute-start.1 = (f32[16,32,256]{2,1,0:T(8,128)S(1)}, f32[16,32,256]{2,1,0:T(8,128)}, u32[]{:S(2)}, u32[]{:S(2)}) collective-permute-start(f32[16,32,256]{2,1,0:T(8,128)S(1)} %product_pieces.4), channel_id=1, source_target_pairs={{0,1},{4,5},{8,9},{12,13},{16,17},{20,21},{24,25},{28,29}} | collective-permute-start | bytes 1572872 | tf_op jit(solution)/shard_map/ppermute | solution.py:381
  16.2 15.2 %collective-permute-start.4 = (f32[16,32,256]{2,1,0:T(8,128)S(1)}, f32[16,32,256]{2,1,0:T(8,128)}, u32[]{:S(2)}, u32[]{:S(2)}) collective-permute-start(f32[16,32,256]{2,1,0:T(8,128)S(1)} %product_pieces.4), channel_id=1, source_target_pairs={{3,2},{7,6},{11,10},{15,14},{19,18},{23,22},{27,26},{31,30}} | collective-permute-start | bytes 1572872 | tf_op jit(solution)/shard_map/ppermute | solution.py:382
  29.4 13.6 %collective-permute-start.12 = (f32[16,32,256]{2,1,0:T(8,128)S(1)}, f32[16,32,256]{2,1,0:T(8,128)S(1)}, u32[]{:S(2)}, u32[]{:S(2)}) collective-permute-start(f32[16,32,256]{2,1,0:T(8,128)S(1)} %get-tuple-element.51), channel_id=1, source_target_pairs={{0,1},{1,2},{4,5},{5,6},{8,9},{9,10},{12,13},{13,14},{16,17},{17,1... | collective-permute-start | bytes 1572872 | tf_op jit(solution)/shard_map/ppermute | solution.py:381
  30.7 17.5 %collective-permute-start.15 = (f32[16,32,256]{2,1,0:T(8,128)S(1)}, f32[16,32,256]{2,1,0:T(8,128)S(1)}, u32[]{:S(2)}, u32[]{:S(2)}) collective-permute-start(f32[16,32,256]{2,1,0:T(8,128)S(1)} %get-tuple-element.52), channel_id=1, source_target_pairs={{2,1},{3,2},{6,5},{7,6},{10,9},{11,10},{14,13},{15,14},{18,17},{19... | collective-permute-start | bytes 1572872 | tf_op jit(solution)/shard_map/ppermute | solution.py:382
  33.6 20.8 %collective-permute-start.2 = (f32[16,32,256]{2,1,0:T(8,128)}, f32[16,32,256]{2,1,0:T(8,128)}, u32[]{:S(2)}, u32[]{:S(2)}) collective-permute-start(f32[16,32,256]{2,1,0:T(8,128)} %get-tuple-element.53), channel_id=1, source_target_pairs={{0,1},{1,2},{4,5},{5,6},{8,9},{9,10},{12,13},{13,14},{16,17},{17,1... | collective-permute-start | bytes 1572872 | tf_op jit(solution)/shard_map/ppermute | solution.py:381
  38.4 23.0 %collective-permute-start.5 = (f32[16,32,256]{2,1,0:T(8,128)S(1)}, f32[16,32,256]{2,1,0:T(8,128)}, u32[]{:S(2)}, u32[]{:S(2)}) collective-permute-start(f32[16,32,256]{2,1,0:T(8,128)S(1)} %get-tuple-element.54), channel_id=1, source_target_pairs={{2,1},{3,2},{6,5},{7,6},{10,9},{11,10},{14,13},{15,14},{18,17},{19... | collective-permute-start | bytes 1572872 | tf_op jit(solution)/shard_map/ppermute | solution.py:382
  43.1 22.4 %collective-permute-start.13 = (f32[16,32,256]{2,1,0:T(8,128)S(1)}, f32[16,32,256]{2,1,0:T(8,128)}, u32[]{:S(2)}, u32[]{:S(2)}) collective-permute-start(f32[16,32,256]{2,1,0:T(8,128)S(1)} %add.118), channel_id=1, source_target_pairs={{0,1},{1,2},{2,3},{4,5},{5,6},{6,7},{8,9},{9,10},{10,11},{12,13},{... | collective-permute-start | bytes 1572872 | tf_op jit(solution)/shard_map/ppermute | solution.py:381
  49.1 16.3 %collective-permute-start.16 = (f32[16,32,256]{2,1,0:T(8,128)}, f32[16,32,256]{2,1,0:T(8,128)}, u32[]{:S(2)}, u32[]{:S(2)}) collective-permute-start(f32[16,32,256]{2,1,0:T(8,128)} %add.121), channel_id=1, source_target_pairs={{1,0},{2,1},{3,2},{5,4},{6,5},{7,6},{9,8},{10,9},{11,10},{13,12},{... | collective-permute-start | bytes 1572872 | tf_op jit(solution)/shard_map/ppermute | solution.py:382
  50.4 16.4 %collective-permute-start = (s32[64]{0:T(128)S(1)}, s32[64]{0:T(128)S(1)}, u32[]{:S(2)}, u32[]{:S(2)}) collective-permute-start(s32[64]{0:T(128)S(1)} %bitcast.14), channel_id=1, source_target_pairs={{0,16},{16,0},{1,17},{17,1},{2,18},{18,2},{3,19},{19,3},{4,20},{20... | collective-permute-start | bytes 776 | tf_op jit(solution)/shard_map/ppermute | solution.py:347
  56.2 19.6 %collective-permute-start.3 = (f32[16,32,256]{2,1,0:T(8,128)}, f32[16,32,256]{2,1,0:T(8,128)}, u32[]{:S(2)}, u32[]{:S(2)}) collective-permute-start(f32[16,32,256]{2,1,0:T(8,128)} %add.112), channel_id=1, source_target_pairs={{0,1},{1,2},{2,3},{4,5},{5,6},{6,7},{8,9},{9,10},{10,11},{12,13},{... | collective-permute-start | bytes 1572872 | tf_op jit(solution)/shard_map/ppermute | solution.py:381
  62.6 13.7 %collective-permute-start.6 = (f32[16,32,256]{2,1,0:T(8,128)S(1)}, f32[16,32,256]{2,1,0:T(8,128)S(1)}, u32[]{:S(2)}, u32[]{:S(2)}) collective-permute-start(f32[16,32,256]{2,1,0:T(8,128)S(1)} %add.115), channel_id=1, source_target_pairs={{1,0},{2,1},{3,2},{5,4},{6,5},{7,6},{9,8},{10,9},{11,10},{13,12},{... | collective-permute-start | bytes 1572872 | tf_op jit(solution)/shard_map/ppermute | solution.py:382
  66.8 11.4 %collective-permute-start.17 = (f32[16,32,256]{2,1,0:T(8,128)S(1)}, f32[16,32,256]{2,1,0:T(8,128)S(1)}, u32[]{:S(2)}, u32[]{:S(2)}) collective-permute-start(f32[16,32,256]{2,1,0:T(8,128)S(1)} %add_add_fusion.refs_0_), channel_id=1, source_target_pairs={{0,16},{16,0},{1,17},{17,1},{2,18},{18,2},{3,19},{19,3},{4,20},{20... | collective-permute-start | bytes 1572872 | tf_op jit(solution)/shard_map/ppermute | solution.py:387
  77.4 10.2 %collective-permute-start.7 = (f32[16,32,256]{2,1,0:T(8,128)S(1)}, f32[16,32,256]{2,1,0:T(8,128)S(1)}, u32[]{:S(2)}, u32[]{:S(2)}) collective-permute-start(f32[16,32,256]{2,1,0:T(8,128)S(1)} %add_add_fusion.1.refs_0_), channel_id=1, source_target_pairs={{0,16},{16,0},{1,17},{17,1},{2,18},{18,2},{3,19},{19,3},{4,20},{20... | collective-permute-start | bytes 1572872 | tf_op jit(solution)/shard_map/ppermute | solution.py:387
  79.5 12.1 %collective-permute-start.18 = (f32[12,32,256]{2,1,0:T(8,128)S(1)}, f32[12,32,256]{2,1,0:T(8,128)S(1)}, u32[]{:S(2)}, u32[]{:S(2)}) collective-permute-start(f32[12,32,256]{2,1,0:T(8,128)S(1)} %get-tuple-element.41), channel_id=1, source_target_pairs={{0,12},{4,8},{24,20},{28,16},{1,13},{5,9},{25,21},{29,17},{2,14},{... | collective-permute-start | bytes 1179656 | tf_op jit(solution)/shard_map/ppermute | solution.py:398
  83.8 12.8 %collective-permute-start.19 = (f32[12,32,256]{2,1,0:T(8,128)S(1)}, f32[12,32,256]{2,1,0:T(8,128)S(1)}, u32[]{:S(2)}, u32[]{:S(2)}) collective-permute-start(f32[12,32,256]{2,1,0:T(8,128)S(1)} %get-tuple-element.42), channel_id=1, source_target_pairs={{0,8},{4,12},{24,16},{28,20},{1,9},{5,13},{25,17},{29,21},{2,10},{... | collective-permute-start | bytes 1179656 | tf_op jit(solution)/shard_map/ppermute | solution.py:398
  85.2 11.4 %collective-permute-start.20 = (f32[12,32,256]{2,1,0:T(8,128)S(1)}, f32[12,32,256]{2,1,0:T(8,128)S(1)}, u32[]{:S(2)}, u32[]{:S(2)}) collective-permute-start(f32[12,32,256]{2,1,0:T(8,128)S(1)} %get-tuple-element.43), channel_id=1, source_target_pairs={{0,4},{8,12},{20,16},{28,24},{1,5},{9,13},{21,17},{29,25},{2,6},{1... | collective-permute-start | bytes 1179656 | tf_op jit(solution)/shard_map/ppermute | solution.py:398
  88.9 8.7 %collective-permute-start.10 = (f32[12,32,256]{2,1,0:T(8,128)S(1)}, f32[12,32,256]{2,1,0:T(8,128)S(1)}, u32[]{:S(2)}, u32[]{:S(2)}) collective-permute-start(f32[12,32,256]{2,1,0:T(8,128)S(1)} %get-tuple-element.35), channel_id=1, source_target_pairs={{0,4},{8,12},{20,16},{28,24},{1,5},{9,13},{21,17},{29,25},{2,6},{1... | collective-permute-start | bytes 1179656 | tf_op jit(solution)/shard_map/ppermute | solution.py:398
  90.2 11.6 %collective-permute-start.8 = (f32[12,32,256]{2,1,0:T(8,128)S(1)}, f32[12,32,256]{2,1,0:T(8,128)S(1)}, u32[]{:S(2)}, u32[]{:S(2)}) collective-permute-start(f32[12,32,256]{2,1,0:T(8,128)S(1)} %get-tuple-element.33), channel_id=1, source_target_pairs={{0,12},{4,8},{24,20},{28,16},{1,13},{5,9},{25,21},{29,17},{2,14},{... | collective-permute-start | bytes 1179656 | tf_op jit(solution)/shard_map/ppermute | solution.py:398
  91.5 12.4 %collective-permute-start.9 = (f32[12,32,256]{2,1,0:T(8,128)S(1)}, f32[12,32,256]{2,1,0:T(8,128)S(1)}, u32[]{:S(2)}, u32[]{:S(2)}) collective-permute-start(f32[12,32,256]{2,1,0:T(8,128)S(1)} %get-tuple-element.34), channel_id=1, source_target_pairs={{0,8},{4,12},{24,16},{28,20},{1,9},{5,13},{25,17},{29,21},{2,10},{... | collective-permute-start | bytes 1179656 | tf_op jit(solution)/shard_map/ppermute | solution.py:398
  107.2 5.5 %collective-permute-start.22 = (f32[160,128]{1,0:T(8,128)S(1)}, f32[160,128]{1,0:T(8,128)S(1)}, u32[]{:S(2)}, u32[]{:S(2)}) collective-permute-start(f32[160,128]{1,0:T(8,128)S(1)} %get-tuple-element.55), channel_id=1, source_target_pairs={{0,12},{4,8},{8,4},{12,0},{1,13},{5,9},{9,5},{13,1},{2,14},{6,10},... | collective-permute-start | bytes 245768 | tf_op jit(solution)/shard_map/ppermute | solution.py:406
  109.8 5.6 %collective-permute-start.24 = (f32[160,128]{1,0:T(8,128)S(1)}, f32[160,128]{1,0:T(8,128)S(1)}, u32[]{:S(2)}, u32[]{:S(2)}) collective-permute-start(f32[160,128]{1,0:T(8,128)S(1)} %get-tuple-element.56), channel_id=1, source_target_pairs={{0,4},{4,0},{8,12},{12,8},{1,5},{5,1},{9,13},{13,9},{2,6},{6,2},{1... | collective-permute-start | bytes 245768 | tf_op jit(solution)/shard_map/ppermute | solution.py:406
  115.4 6.4 %collective-permute-start.25 = (f32[160,128]{1,0:T(8,128)S(1)}, f32[160,128]{1,0:T(8,128)S(1)}, u32[]{:S(2)}, u32[]{:S(2)}) collective-permute-start(f32[160,128]{1,0:T(8,128)S(1)} %fusion.1), channel_id=1, source_target_pairs={{0,3},{1,2},{2,1},{3,0},{4,7},{5,6},{6,5},{7,4},{8,11},{9,10},{10,... | collective-permute-start | bytes 245768 | tf_op jit(solution)/shard_map/ppermute | solution.py:406
  118.9 7.5 %collective-permute-start.26 = (f32[160,128]{1,0:T(8,128)S(1)}, f32[160,128]{1,0:T(8,128)S(1)}, u32[]{:S(2)}, u32[]{:S(2)}) collective-permute-start(f32[160,128]{1,0:T(8,128)S(1)} %fusion.1), channel_id=1, source_target_pairs={{0,2},{1,3},{2,0},{3,1},{4,6},{5,7},{6,4},{7,5},{8,10},{9,11},{10,... | collective-permute-start | bytes 245768 | tf_op jit(solution)/shard_map/ppermute | solution.py:406
  120.4 6.0 %collective-permute-start.27 = (f32[160,128]{1,0:T(8,128)S(1)}, f32[160,128]{1,0:T(8,128)S(1)}, u32[]{:S(2)}, u32[]{:S(2)}) collective-permute-start(f32[160,128]{1,0:T(8,128)S(1)} %fusion.1), channel_id=1, source_target_pairs={{0,1},{1,0},{2,3},{3,2},{4,5},{5,4},{6,7},{7,6},{8,9},{9,8},{10,11... | collective-permute-start | bytes 245768 | tf_op jit(solution)/shard_map/ppermute | solution.py:406
  126.4 4.7 %collective-permute-start.28 = (f32[160,128]{1,0:T(8,128)S(1)}, f32[160,128]{1,0:T(8,128)S(1)}, u32[]{:S(2)}, u32[]{:S(2)}) collective-permute-start(f32[160,128]{1,0:T(8,128)S(1)} %add_add_fusion.2), channel_id=1, source_target_pairs={{0,4},{4,0},{8,12},{12,8},{1,5},{5,1},{9,13},{13,9},{2,6},{6,2},{1... | collective-permute-start | bytes 245768 | tf_op jit(solution)/shard_map/ppermute | solution.py:406
  127.3 5.3 %collective-permute-start.29 = (f32[160,128]{1,0:T(8,128)S(1)}, f32[160,128]{1,0:T(8,128)S(1)}, u32[]{:S(2)}, u32[]{:S(2)}) collective-permute-start(f32[160,128]{1,0:T(8,128)S(1)} %add_add_fusion.2), channel_id=1, source_target_pairs={{0,8},{4,12},{8,0},{12,4},{1,9},{5,13},{9,1},{13,5},{2,10},{6,14},... | collective-permute-start | bytes 245768 | tf_op jit(solution)/shard_map/ppermute | solution.py:406
  129.2 5.3 %collective-permute-start.30 = (f32[160,128]{1,0:T(8,128)S(1)}, f32[160,128]{1,0:T(8,128)S(1)}, u32[]{:S(2)}, u32[]{:S(2)}) collective-permute-start(f32[160,128]{1,0:T(8,128)S(1)} %add_add_fusion.2), channel_id=1, source_target_pairs={{0,12},{4,8},{8,4},{12,0},{1,13},{5,9},{9,5},{13,1},{2,14},{6,10},... | collective-permute-start | bytes 245768 | tf_op jit(solution)/shard_map/ppermute | solution.py:406
  300.1 10.7 %collective-permute-start.32 = (f32[384,128]{1,0:T(8,128)S(1)}, f32[384,128]{1,0:T(8,128)S(1)}, u32[]{:S(2)}, u32[]{:S(2)}) collective-permute-start(f32[384,128]{1,0:T(8,128)S(1)} %get-tuple-element.48), channel_id=1, source_target_pairs={{0,1},{1,0},{2,3},{3,2},{4,5},{5,4},{6,7},{7,6},{8,9},{9,8},{10,11... | collective-permute-start | bytes 589832 | tf_op jit(solution)/shard_map/ppermute | solution.py:406
  300.6 17.6 %collective-permute-start.33 = (f32[384,128]{1,0:T(8,128)S(1)}, f32[384,128]{1,0:T(8,128)S(1)}, u32[]{:S(2)}, u32[]{:S(2)}) collective-permute-start(f32[384,128]{1,0:T(8,128)S(1)} %get-tuple-element.49), channel_id=1, source_target_pairs={{0,2},{1,3},{2,0},{3,1},{4,6},{5,7},{6,4},{7,5},{8,10},{9,11},{10,... | collective-permute-start | bytes 589832 | tf_op jit(solution)/shard_map/ppermute | solution.py:406
  303.9 14.2 %collective-permute-start.34 = (f32[384,128]{1,0:T(8,128)S(1)}, f32[384,128]{1,0:T(8,128)S(1)}, u32[]{:S(2)}, u32[]{:S(2)}) collective-permute-start(f32[384,128]{1,0:T(8,128)S(1)} %get-tuple-element.50), channel_id=1, source_target_pairs={{0,3},{1,2},{2,1},{3,0},{4,7},{5,6},{6,5},{7,4},{8,11},{9,10},{10,... | collective-permute-start | bytes 589832 | tf_op jit(solution)/shard_map/ppermute | solution.py:406
  (4 other events, 40.6 us)

commit v3 on v2

--- a/solution.py
+++ b/solution.py
@@ -21,10 +21,14 @@
     outs_each = chunks if chunk is None else 1
     width = sketch.shape[1] // chunks
     across = width * outs_each
-    step = max(blocks // 2, 1) if chunk is None else max(blocks // 4, 1)
-
-    def kernel(dest_ref, a_ref, b_ref, *outs):
-        product = jnp.dot(a_ref[...].reshape(step * sub, depth), b_ref[...], preferred_element_type=jnp.float32)
+    step = max(blocks // 2, 1)
+    fetches = 4 if step % 4 == 0 else 1
+    fetched = step // fetches
+
+    def kernel(dest_ref, *refs):
+        a_refs, b_ref, outs = refs[:fetches], refs[fetches], refs[fetches + 1 :]
+        a = jnp.concatenate([r[...].reshape(fetched * sub, depth) for r in a_refs], axis=0)
+        product = jnp.dot(a, b_ref[...], preferred_element_type=jnp.float32)
         rows = pl.ds(pl.program_id(1) * step, step)
         for k in range(count):
 
@@ -41,7 +45,10 @@
             num_scalar_prefetch=1,
             grid=(count, blocks // step),
             in_specs=[
-                pl.BlockSpec((step, sub, depth), lambda p, g, d: (g, d[p], 0)),
+                pl.BlockSpec((fetched, sub, depth), lambda p, g, d, i=i: (g * fetches + i, d[p], 0))
+                for i in range(fetches)
+            ]
+            + [
                 pl.BlockSpec((depth, across), lambda p, g, d: (0, chunk or 0)),
             ],
             out_specs=[pl.BlockSpec(memory_space=pltpu.VMEM)] * (count * outs_each),
@@ -53,7 +60,7 @@
         ),
         compiler_params=grant(28),
         name="product_pieces",
-    )(jnp.stack(dests), panel, sketch)
+    )(jnp.stack(dests), *[panel] * fetches, sketch)
     return [outs[k * outs_each : (k + 1) * outs_each] for k in range(count)]
 
 
@@ -365,7 +372,15 @@
     wants.append(col_here)
     panel = pltpu.with_memory_space_constraint(panel, pltpu.HBM)
     sketch = pltpu.with_memory_space_constraint(sketch, pltpu.HBM)
-    products = [[product_pieces(panel, sketch, wants[:1], sub, COLUMN_CHUNKS, h)[0][0] for h in range(COLUMN_CHUNKS)]]
+    ends = (col_here == 0) | (col_here == cols - 1)
+
+    def first_piece(chunk):
+        return product_pieces(panel, sketch, wants[:1], sub, COLUMN_CHUNKS, chunk)[0][0]
+
+    def no_piece():
+        return jnp.zeros((blocks, sub, sketch_cols // COLUMN_CHUNKS), jnp.float32)
+
+    products = [[lax.cond(ends, lambda h=h: first_piece(h), no_piece) for h in range(COLUMN_CHUNKS)]]
     products += product_pieces(panel, sketch, wants[1:], sub, COLUMN_CHUNKS)
 
     arrived = []

time: 321 us -> 320 us (level)
    ppermute x6, starting transfers between devices: 24.4 us -> 20.6 us  [shards(): came_up = lax.ppermute(up, 'col', [(i, i + 1) for i in range(stage)])]
  transfers between devices with their start and end apart: 35 -> 35, of which waited for: 20 -> 21; matrix products, arithmetic and copies ran while one was open for 3% -> 3% of each run, Pallas kernels for 5% -> 5%
where the time goes in v3:
time: 320 us; the launch traced here: 318 us
  Pallas kernels  186 us (58%)
  starting transfers between devices  63.1 us (20%)
  waiting for transfers between devices  56.9 us (18%)
  other arithmetic  10.7 us (3%)
    pallas_call x1, Pallas kernels, basis_pieces(): pl.pallas_call(kernel, out_shape=[jax.ShapeDtypeStruct((rows, tile), jnp....  164 us
    ppermute x14, waiting for transfers between devices, swap(): lax.ppermute(x, name, [(i, i ^ level) for i in range(lax.axis_size(name))])  31.4 us
    ppermute x6, starting transfers between devices, shards(): came_up = lax.ppermute(up, 'col', [(i, i + 1) for i in range(stage)])  20.6 us
    ppermute x6, waiting for transfers between devices, shards(): came_up = lax.ppermute(up, 'col', [(i, i + 1) for i in range(stage)])  18.3 us
    ppermute x6, starting transfers between devices, shards(): came.append(lax.ppermute(slotted[k], both, pairs))  17.4 us
    ppermute x14, starting transfers between devices, swap(): lax.ppermute(x, name, [(i, i ^ level) for i in range(lax.axis_size(name))])  17.2 us
    pallas_call x3, Pallas kernels, product_pieces(): pl.pallas_call(kernel, out_shape=[jax.ShapeDtypeStruct((blocks, sub, widt...  16.9 us
    ppermute x6, starting transfers between devices, shards(): lax.ppermute(down, 'col', [(i, i - 1) for i in range(cols - stage, cols)])  7.7 us
  transfers between devices with their start and end apart: 35, of which 21 were waited for; matrix products, arithmetic and copies ran while one was open for 3% of the time, Pallas kernels for 5%

profile of v3, /device:TPU:0, one launch (start us, length us, event | category | flops | bytes accessed | tf_op | source)
XLA Modules:
  0.0 318.0 jit_solution(10475752710490101516)
XLA Ops:
  0.0 3.3 %conditional.3 = (f32[16,32,256]{2,1,0:T(8,128)}) conditional(s32[]{:T(128)} %convert_element_type.4, () %tuple.19, (s32[]{:T(128)}, bf16[16,128,2048]{2,1,0:T(8,128)(2,1)}, bf16[2048,512]{1,0:T(8,128)(2,1)}) %tuple.28), branch_computations={%region_3.4_spmd, %region_4.5_spmd} | conditional | flops 536870912 | bytes 3670024 | solution.py:383
  0.0 3.3 %product_pieces.4 = f32[16,32,256]{2,1,0:T(8,128)} custom-call(s32[1]{0:T(128)} %bitcast.1.dest_ref, bf16[16,128,2048]{2,1,0:T(8,128)(2,1)} %get-tuple-element.27.refs_0_.refs_1_.refs_2_.refs_3_, bf16[16,128,2048]{2,1,0:T(8,128)(2,1)} %get-tuple-element.27.refs_0_.refs_1_.refs_2_.refs_3_, ...), custom_call_target="tpu_custom_call" | custom-call | flops 536870912 | bytes 3670016 | tf_op jit(solution)/shard_map/cond/branch_1_fun/product_pieces/pallas_call | solution.py:41
  3.3 2.5 collective-permute-start.11
  7.3 3.3 %conditional.2 = (f32[16,32,256]{2,1,0:T(8,128)}) conditional(s32[]{:T(128)} %convert_element_type.4, () %tuple.17, (s32[]{:T(128)}, bf16[16,128,2048]{2,1,0:T(8,128)(2,1)}, bf16[2048,512]{1,0:T(8,128)(2,1)}) %tuple.29), branch_computations={%region_1.2_spmd, %region_2.3_spmd} | conditional | flops 536870912 | bytes 3670024 | solution.py:383
  7.3 3.3 %product_pieces.3 = f32[16,32,256]{2,1,0:T(8,128)} custom-call(s32[1]{0:T(128)} %bitcast.dest_ref, bf16[16,128,2048]{2,1,0:T(8,128)(2,1)} %get-tuple-element.24.refs_0_.refs_1_.refs_2_.refs_3_, bf16[16,128,2048]{2,1,0:T(8,128)(2,1)} %get-tuple-element.24.refs_0_.refs_1_.refs_2_.refs_3_, ...), custom_call_target="tpu_custom_call" | custom-call | flops 536870912 | bytes 3670016 | tf_op jit(solution)/shard_map/cond/branch_1_fun/product_pieces/pallas_call | solution.py:41
  13.5 10.3 %product_pieces.5 = (f32[16,32,256]{2,1,0:T(8,128)S(1)}, f32[16,32,256]{2,1,0:T(8,128)S(1)}, f32[16,32,256]{2,1,0:T(8,128)S(1)}, f32[16,32,256]{2,1,0:T(8,128)S(...) custom-call(s32[4]{0:T(128)S(1)} %pad_add_fusion.2.dest_ref, ...), custom_call_target="tpu_custom_call" | custom-call | flops 4294967296 | bytes 14680064 | tf_op jit(solution)/shard_map/product_pieces/pallas_call | solution.py:41
  27.1 2.6 collective-permute-done.1
  30.5 2.1 fusion.3
  32.6 5.1 %collective-permute-start.2 = (f32[16,32,256]{2,1,0:T(8,128)}, f32[16,32,256]{2,1,0:T(8,128)}, u32[]{:S(2)}, u32[]{:S(2)}) collective-permute-start(f32[16,32,256]{2,1,0:T(8,128)} %get-tuple-element.77), channel_id=1, source_target_pairs={{0,1},{1,2},{4,5},{5,6},{8,9},{9,10},{12,13},{13,14},{16,17},{17,1... | collective-permute-start | bytes 1572872 | tf_op jit(solution)/shard_map/ppermute | solution.py:396
  39.1 1.7 collective-permute-done.12
  40.9 5.2 %collective-permute-start.13 = (f32[16,32,256]{2,1,0:T(8,128)S(1)}, f32[16,32,256]{2,1,0:T(8,128)}, u32[]{:S(2)}, u32[]{:S(2)}) collective-permute-start(f32[16,32,256]{2,1,0:T(8,128)S(1)} %add.118), channel_id=1, source_target_pairs={{0,1},{1,2},{2,3},{4,5},{5,6},{6,7},{8,9},{9,10},{10,11},{12,13},{... | collective-permute-start | bytes 1572872 | tf_op jit(solution)/shard_map/ppermute | solution.py:396
  48.3 3.8 %collective-permute-done.2 = f32[16,32,256]{2,1,0:T(8,128)} collective-permute-done((f32[16,32,256]{2,1,0:T(8,128)}, f32[16,32,256]{2,1,0:T(8,128)}, u32[]{:S(2)}, u32[]{:S(2)}) %collective-permute-start.2) | collective-permute-done | bytes 524320 | tf_op jit(solution)/shard_map/ppermute | solution.py:396
  52.1 1.9 add.112
  54.0 5.2 %collective-permute-start.3 = (f32[16,32,256]{2,1,0:T(8,128)}, f32[16,32,256]{2,1,0:T(8,128)}, u32[]{:S(2)}, u32[]{:S(2)}) collective-permute-start(f32[16,32,256]{2,1,0:T(8,128)} %add.112), channel_id=1, source_target_pairs={{0,1},{1,2},{2,3},{4,5},{5,6},{6,7},{8,9},{9,10},{10,11},{12,13},{... | collective-permute-start | bytes 1572872 | tf_op jit(solution)/shard_map/ppermute | solution.py:396
  64.7 8.7 %collective-permute-done.3 = f32[16,32,256]{2,1,0:T(8,128)} collective-permute-done((f32[16,32,256]{2,1,0:T(8,128)}, f32[16,32,256]{2,1,0:T(8,128)}, u32[]{:S(2)}, u32[]{:S(2)}) %collective-permute-start.3) | collective-permute-done | bytes 524320 | tf_op jit(solution)/shard_map/ppermute | solution.py:396
  77.1 5.2 %collective-permute-start.18 = (f32[12,32,256]{2,1,0:T(8,128)S(1)}, f32[12,32,256]{2,1,0:T(8,128)S(1)}, u32[]{:S(2)}, u32[]{:S(2)}) collective-permute-start(f32[12,32,256]{2,1,0:T(8,128)S(1)} %get-tuple-element.65), channel_id=1, source_target_pairs={{0,12},{4,8},{24,20},{28,16},{1,13},{5,9},{25,21},{29,17},{2,14},{... | collective-permute-start | bytes 1179656 | tf_op jit(solution)/shard_map/ppermute | solution.py:413
  83.6 2.5 collective-permute-start.20
  90.0 5.8 %collective-permute-start.9 = (f32[12,32,256]{2,1,0:T(8,128)S(1)}, f32[12,32,256]{2,1,0:T(8,128)S(1)}, u32[]{:S(2)}, u32[]{:S(2)}) collective-permute-start(f32[12,32,256]{2,1,0:T(8,128)S(1)} %get-tuple-element.58), channel_id=1, source_target_pairs={{0,8},{4,12},{24,16},{28,20},{1,9},{5,13},{25,17},{29,21},{2,10},{... | collective-permute-start | bytes 1179656 | tf_op jit(solution)/shard_map/ppermute | solution.py:413
  96.0 4.3 %collective-permute-done.8.refs_1_ = f32[12,32,256]{2,1,0:T(8,128)S(1)} collective-permute-done((f32[12,32,256]{2,1,0:T(8,128)S(1)}, f32[12,32,256]{2,1,0:T(8,128)S(1)}, u32[]{:S(2)}, u32[]{:S(2)}) %collective-permute-start.8) | collective-permute-done | bytes 393248 | tf_op jit(solution)/shard_map/ppermute | solution.py:413
  100.3 2.5 collective-permute-done.9.refs_2_
  104.3 1.6 collective-permute-done.21
  106.0 2.2 collective-permute-start.22
  111.5 1.7 collective-permute-done.23
  114.3 3.3 %collective-permute-start.25 = (f32[160,128]{1,0:T(8,128)S(1)}, f32[160,128]{1,0:T(8,128)S(1)}, u32[]{:S(2)}, u32[]{:S(2)}) collective-permute-start(f32[160,128]{1,0:T(8,128)S(1)} %fusion.1), channel_id=1, source_target_pairs={{0,3},{1,2},{2,1},{3,0},{4,7},{5,6},{6,5},{7,4},{8,11},{9,10},{10,... | collective-permute-start | bytes 245768 | tf_op jit(solution)/shard_map/ppermute | solution.py:421
  120.7 4.3 %collective-permute-done.26 = f32[160,128]{1,0:T(8,128)S(1)} collective-permute-done((f32[160,128]{1,0:T(8,128)S(1)}, f32[160,128]{1,0:T(8,128)S(1)}, u32[]{:S(2)}, u32[]{:S(2)}) %collective-permute-start.26) | collective-permute-done | bytes 81952 | tf_op jit(solution)/shard_map/ppermute | solution.py:421
  125.9 1.9 collective-permute-start.29
  131.2 1.9 collective-permute-done.30
  133.2 1.6 collective-permute-done.31.refs_1_
  134.8 163.8 %basis_pieces.1 = (f32[384,128]{1,0:T(8,128)S(1)}, f32[384,128]{1,0:T(8,128)S(1)}, f32[384,128]{1,0:T(8,128)S(1)}, f32[384,128]{1,0:T(8,128)S(1)}) custom-call(s32[3]{0:T(128)S(1)} %pad_add_fusion.1.here_ref, f32[640,128]{1,0:T(8,128)S(1)} %pad_maximum_fusion.refs_0_, f32[640,128]{1,0:T(8,128)S(1)} %collective-permute-done.31.refs_1_, ...), custom_call_target="tpu_custom_call" | custom-call | flops 1610612736 | bytes 1835008 | tf_op jit(solution)/shard_map/basis_pieces/pallas_call | solution.py:292
  299.2 3.4 %collective-permute-start.33 = (f32[384,128]{1,0:T(8,128)S(1)}, f32[384,128]{1,0:T(8,128)S(1)}, u32[]{:S(2)}, u32[]{:S(2)}) collective-permute-start(f32[384,128]{1,0:T(8,128)S(1)} %get-tuple-element.73), channel_id=1, source_target_pairs={{0,2},{1,3},{2,0},{3,1},{4,6},{5,7},{6,4},{7,5},{8,10},{9,11},{10,... | collective-permute-start | bytes 589832 | tf_op jit(solution)/shard_map/ppermute | solution.py:421
  303.1 6.2 %collective-permute-done.32.refs_1_ = f32[384,128]{1,0:T(8,128)S(1)} collective-permute-done((f32[384,128]{1,0:T(8,128)S(1)}, f32[384,128]{1,0:T(8,128)S(1)}, u32[]{:S(2)}, u32[]{:S(2)}) %collective-permute-start.32) | collective-permute-done | bytes 196640 | tf_op jit(solution)/shard_map/ppermute | solution.py:421
  309.4 7.4 %collective-permute-done.33.refs_2_ = f32[384,128]{1,0:T(8,128)S(1)} collective-permute-done((f32[384,128]{1,0:T(8,128)S(1)}, f32[384,128]{1,0:T(8,128)S(1)}, u32[]{:S(2)}, u32[]{:S(2)}) %collective-permute-start.33) | collective-permute-done | bytes 196640 | tf_op jit(solution)/shard_map/ppermute | solution.py:421
  (75 shorter events, 42.3 us)
Async XLA Ops:
  3.3 20.6 %collective-permute-start.11 = (f32[16,32,256]{2,1,0:T(8,128)}, f32[16,32,256]{2,1,0:T(8,128)S(1)}, u32[]{:S(2)}, u32[]{:S(2)}) collective-permute-start(f32[16,32,256]{2,1,0:T(8,128)} %get-tuple-element.83), channel_id=1, source_target_pairs={{0,1},{4,5},{8,9},{12,13},{16,17},{20,21},{24,25},{28,29}} | collective-permute-start | bytes 1572872 | tf_op jit(solution)/shard_map/ppermute | solution.py:396
  5.8 18.0 %collective-permute-start.14 = (f32[16,32,256]{2,1,0:T(8,128)}, f32[16,32,256]{2,1,0:T(8,128)}, u32[]{:S(2)}, u32[]{:S(2)}) collective-permute-start(f32[16,32,256]{2,1,0:T(8,128)} %get-tuple-element.83), channel_id=1, source_target_pairs={{3,2},{7,6},{11,10},{15,14},{19,18},{23,22},{27,26},{31,30}} | collective-permute-start | bytes 1572872 | tf_op jit(solution)/shard_map/ppermute | solution.py:397
  10.6 19.1 %collective-permute-start.1 = (f32[16,32,256]{2,1,0:T(8,128)}, f32[16,32,256]{2,1,0:T(8,128)S(1)}, u32[]{:S(2)}, u32[]{:S(2)}) collective-permute-start(f32[16,32,256]{2,1,0:T(8,128)} %get-tuple-element.82), channel_id=1, source_target_pairs={{0,1},{4,5},{8,9},{12,13},{16,17},{20,21},{24,25},{28,29}} | collective-permute-start | bytes 1572872 | tf_op jit(solution)/shard_map/ppermute | solution.py:396
  11.9 17.7 %collective-permute-start.4 = (f32[16,32,256]{2,1,0:T(8,128)}, f32[16,32,256]{2,1,0:T(8,128)}, u32[]{:S(2)}, u32[]{:S(2)}) collective-permute-start(f32[16,32,256]{2,1,0:T(8,128)} %get-tuple-element.82), channel_id=1, source_target_pairs={{3,2},{7,6},{11,10},{15,14},{19,18},{23,22},{27,26},{31,30}} | collective-permute-start | bytes 1572872 | tf_op jit(solution)/shard_map/ppermute | solution.py:397
  25.0 15.8 %collective-permute-start.12 = (f32[16,32,256]{2,1,0:T(8,128)S(1)}, f32[16,32,256]{2,1,0:T(8,128)S(1)}, u32[]{:S(2)}, u32[]{:S(2)}) collective-permute-start(f32[16,32,256]{2,1,0:T(8,128)S(1)} %get-tuple-element.75), channel_id=1, source_target_pairs={{0,1},{1,2},{4,5},{5,6},{8,9},{9,10},{12,13},{13,14},{16,17},{17,1... | collective-permute-start | bytes 1572872 | tf_op jit(solution)/shard_map/ppermute | solution.py:396
  26.4 19.7 %collective-permute-start.15 = (f32[16,32,256]{2,1,0:T(8,128)S(1)}, f32[16,32,256]{2,1,0:T(8,128)S(1)}, u32[]{:S(2)}, u32[]{:S(2)}) collective-permute-start(f32[16,32,256]{2,1,0:T(8,128)S(1)} %get-tuple-element.76), channel_id=1, source_target_pairs={{2,1},{3,2},{6,5},{7,6},{10,9},{11,10},{14,13},{15,14},{18,17},{19... | collective-permute-start | bytes 1572872 | tf_op jit(solution)/shard_map/ppermute | solution.py:397
  32.6 19.5 %collective-permute-start.2 = (f32[16,32,256]{2,1,0:T(8,128)}, f32[16,32,256]{2,1,0:T(8,128)}, u32[]{:S(2)}, u32[]{:S(2)}) collective-permute-start(f32[16,32,256]{2,1,0:T(8,128)} %get-tuple-element.77), channel_id=1, source_target_pairs={{0,1},{1,2},{4,5},{5,6},{8,9},{9,10},{12,13},{13,14},{16,17},{17,1... | collective-permute-start | bytes 1572872 | tf_op jit(solution)/shard_map/ppermute | solution.py:396
  37.7 21.6 %collective-permute-start.5 = (f32[16,32,256]{2,1,0:T(8,128)S(1)}, f32[16,32,256]{2,1,0:T(8,128)}, u32[]{:S(2)}, u32[]{:S(2)}) collective-permute-start(f32[16,32,256]{2,1,0:T(8,128)S(1)} %get-tuple-element.78), channel_id=1, source_target_pairs={{2,1},{3,2},{6,5},{7,6},{10,9},{11,10},{14,13},{15,14},{18,17},{19... | collective-permute-start | bytes 1572872 | tf_op jit(solution)/shard_map/ppermute | solution.py:397
  40.9 22.4 %collective-permute-start.13 = (f32[16,32,256]{2,1,0:T(8,128)S(1)}, f32[16,32,256]{2,1,0:T(8,128)}, u32[]{:S(2)}, u32[]{:S(2)}) collective-permute-start(f32[16,32,256]{2,1,0:T(8,128)S(1)} %add.118), channel_id=1, source_target_pairs={{0,1},{1,2},{2,3},{4,5},{5,6},{6,7},{8,9},{9,10},{10,11},{12,13},{... | collective-permute-start | bytes 1572872 | tf_op jit(solution)/shard_map/ppermute | solution.py:396
  46.9 16.3 %collective-permute-start.16 = (f32[16,32,256]{2,1,0:T(8,128)}, f32[16,32,256]{2,1,0:T(8,128)}, u32[]{:S(2)}, u32[]{:S(2)}) collective-permute-start(f32[16,32,256]{2,1,0:T(8,128)} %add.121), channel_id=1, source_target_pairs={{1,0},{2,1},{3,2},{5,4},{6,5},{7,6},{9,8},{10,9},{11,10},{13,12},{... | collective-permute-start | bytes 1572872 | tf_op jit(solution)/shard_map/ppermute | solution.py:397
  48.2 16.4 %collective-permute-start = (s32[64]{0:T(128)S(1)}, s32[64]{0:T(128)S(1)}, u32[]{:S(2)}, u32[]{:S(2)}) collective-permute-start(s32[64]{0:T(128)S(1)} %bitcast.18), channel_id=1, source_target_pairs={{0,16},{16,0},{1,17},{17,1},{2,18},{18,2},{3,19},{19,3},{4,20},{20... | collective-permute-start | bytes 776 | tf_op jit(solution)/shard_map/ppermute | solution.py:354
  54.0 19.4 %collective-permute-start.3 = (f32[16,32,256]{2,1,0:T(8,128)}, f32[16,32,256]{2,1,0:T(8,128)}, u32[]{:S(2)}, u32[]{:S(2)}) collective-permute-start(f32[16,32,256]{2,1,0:T(8,128)} %add.112), channel_id=1, source_target_pairs={{0,1},{1,2},{2,3},{4,5},{5,6},{6,7},{8,9},{9,10},{10,11},{12,13},{... | collective-permute-start | bytes 1572872 | tf_op jit(solution)/shard_map/ppermute | solution.py:396
  60.3 13.4 %collective-permute-start.6 = (f32[16,32,256]{2,1,0:T(8,128)S(1)}, f32[16,32,256]{2,1,0:T(8,128)}, u32[]{:S(2)}, u32[]{:S(2)}) collective-permute-start(f32[16,32,256]{2,1,0:T(8,128)S(1)} %add.115), channel_id=1, source_target_pairs={{1,0},{2,1},{3,2},{5,4},{6,5},{7,6},{9,8},{10,9},{11,10},{13,12},{... | collective-permute-start | bytes 1572872 | tf_op jit(solution)/shard_map/ppermute | solution.py:397
  64.6 11.3 %collective-permute-start.17 = (f32[16,32,256]{2,1,0:T(8,128)S(1)}, f32[16,32,256]{2,1,0:T(8,128)S(1)}, u32[]{:S(2)}, u32[]{:S(2)}) collective-permute-start(f32[16,32,256]{2,1,0:T(8,128)S(1)} %add_add_fusion.refs_0_), channel_id=1, source_target_pairs={{0,16},{16,0},{1,17},{17,1},{2,18},{18,2},{3,19},{19,3},{4,20},{20... | collective-permute-start | bytes 1572872 | tf_op jit(solution)/shard_map/ppermute | solution.py:402
  75.0 11.1 %collective-permute-start.7 = (f32[16,32,256]{2,1,0:T(8,128)S(1)}, f32[16,32,256]{2,1,0:T(8,128)S(1)}, u32[]{:S(2)}, u32[]{:S(2)}) collective-permute-start(f32[16,32,256]{2,1,0:T(8,128)S(1)} %add_add_fusion.1.refs_0_), channel_id=1, source_target_pairs={{0,16},{16,0},{1,17},{17,1},{2,18},{18,2},{3,19},{19,3},{4,20},{20... | collective-permute-start | bytes 1572872 | tf_op jit(solution)/shard_map/ppermute | solution.py:402
  77.1 12.9 %collective-permute-start.18 = (f32[12,32,256]{2,1,0:T(8,128)S(1)}, f32[12,32,256]{2,1,0:T(8,128)S(1)}, u32[]{:S(2)}, u32[]{:S(2)}) collective-permute-start(f32[12,32,256]{2,1,0:T(8,128)S(1)} %get-tuple-element.65), channel_id=1, source_target_pairs={{0,12},{4,8},{24,20},{28,16},{1,13},{5,9},{25,21},{29,17},{2,14},{... | collective-permute-start | bytes 1179656 | tf_op jit(solution)/shard_map/ppermute | solution.py:413
  82.3 13.6 %collective-permute-start.19 = (f32[12,32,256]{2,1,0:T(8,128)S(1)}, f32[12,32,256]{2,1,0:T(8,128)S(1)}, u32[]{:S(2)}, u32[]{:S(2)}) collective-permute-start(f32[12,32,256]{2,1,0:T(8,128)S(1)} %get-tuple-element.66), channel_id=1, source_target_pairs={{0,8},{4,12},{24,16},{28,20},{1,9},{5,13},{25,17},{29,21},{2,10},{... | collective-permute-start | bytes 1179656 | tf_op jit(solution)/shard_map/ppermute | solution.py:413
  83.6 12.3 %collective-permute-start.20 = (f32[12,32,256]{2,1,0:T(8,128)S(1)}, f32[12,32,256]{2,1,0:T(8,128)S(1)}, u32[]{:S(2)}, u32[]{:S(2)}) collective-permute-start(f32[12,32,256]{2,1,0:T(8,128)S(1)} %get-tuple-element.67), channel_id=1, source_target_pairs={{0,4},{8,12},{20,16},{28,24},{1,5},{9,13},{21,17},{29,25},{2,6},{1... | collective-permute-start | bytes 1179656 | tf_op jit(solution)/shard_map/ppermute | solution.py:413
  87.3 8.7 %collective-permute-start.10 = (f32[12,32,256]{2,1,0:T(8,128)S(1)}, f32[12,32,256]{2,1,0:T(8,128)S(1)}, u32[]{:S(2)}, u32[]{:S(2)}) collective-permute-start(f32[12,32,256]{2,1,0:T(8,128)S(1)} %get-tuple-element.59), channel_id=1, source_target_pairs={{0,4},{8,12},{20,16},{28,24},{1,5},{9,13},{21,17},{29,25},{2,6},{1... | collective-permute-start | bytes 1179656 | tf_op jit(solution)/shard_map/ppermute | solution.py:413
  88.7 11.6 %collective-permute-start.8 = (f32[12,32,256]{2,1,0:T(8,128)S(1)}, f32[12,32,256]{2,1,0:T(8,128)S(1)}, u32[]{:S(2)}, u32[]{:S(2)}) collective-permute-start(f32[12,32,256]{2,1,0:T(8,128)S(1)} %get-tuple-element.57), channel_id=1, source_target_pairs={{0,12},{4,8},{24,20},{28,16},{1,13},{5,9},{25,21},{29,17},{2,14},{... | collective-permute-start | bytes 1179656 | tf_op jit(solution)/shard_map/ppermute | solution.py:413
  90.0 12.8 %collective-permute-start.9 = (f32[12,32,256]{2,1,0:T(8,128)S(1)}, f32[12,32,256]{2,1,0:T(8,128)S(1)}, u32[]{:S(2)}, u32[]{:S(2)}) collective-permute-start(f32[12,32,256]{2,1,0:T(8,128)S(1)} %get-tuple-element.58), channel_id=1, source_target_pairs={{0,8},{4,12},{24,16},{28,20},{1,9},{5,13},{25,17},{29,21},{2,10},{... | collective-permute-start | bytes 1179656 | tf_op jit(solution)/shard_map/ppermute | solution.py:413
  106.0 5.5 %collective-permute-start.22 = (f32[160,128]{1,0:T(8,128)S(1)}, f32[160,128]{1,0:T(8,128)S(1)}, u32[]{:S(2)}, u32[]{:S(2)}) collective-permute-start(f32[160,128]{1,0:T(8,128)S(1)} %get-tuple-element.79), channel_id=1, source_target_pairs={{0,12},{4,8},{8,4},{12,0},{1,13},{5,9},{9,5},{13,1},{2,14},{6,10},... | collective-permute-start | bytes 245768 | tf_op jit(solution)/shard_map/ppermute | solution.py:421
  108.2 5.0 %collective-permute-start.23 = (f32[160,128]{1,0:T(8,128)S(1)}, f32[160,128]{1,0:T(8,128)S(1)}, u32[]{:S(2)}, u32[]{:S(2)}) collective-permute-start(f32[160,128]{1,0:T(8,128)S(1)} %get-tuple-element.81), channel_id=1, source_target_pairs={{0,8},{4,12},{8,0},{12,4},{1,9},{5,13},{9,1},{13,5},{2,10},{6,14},... | collective-permute-start | bytes 245768 | tf_op jit(solution)/shard_map/ppermute | solution.py:421
  108.6 5.6 %collective-permute-start.24 = (f32[160,128]{1,0:T(8,128)S(1)}, f32[160,128]{1,0:T(8,128)S(1)}, u32[]{:S(2)}, u32[]{:S(2)}) collective-permute-start(f32[160,128]{1,0:T(8,128)S(1)} %get-tuple-element.80), channel_id=1, source_target_pairs={{0,4},{4,0},{8,12},{12,8},{1,5},{5,1},{9,13},{13,9},{2,6},{6,2},{1... | collective-permute-start | bytes 245768 | tf_op jit(solution)/shard_map/ppermute | solution.py:421
  114.3 6.4 %collective-permute-start.25 = (f32[160,128]{1,0:T(8,128)S(1)}, f32[160,128]{1,0:T(8,128)S(1)}, u32[]{:S(2)}, u32[]{:S(2)}) collective-permute-start(f32[160,128]{1,0:T(8,128)S(1)} %fusion.1), channel_id=1, source_target_pairs={{0,3},{1,2},{2,1},{3,0},{4,7},{5,6},{6,5},{7,4},{8,11},{9,10},{10,... | collective-permute-start | bytes 245768 | tf_op jit(solution)/shard_map/ppermute | solution.py:421
  117.6 7.4 %collective-permute-start.26 = (f32[160,128]{1,0:T(8,128)S(1)}, f32[160,128]{1,0:T(8,128)S(1)}, u32[]{:S(2)}, u32[]{:S(2)}) collective-permute-start(f32[160,128]{1,0:T(8,128)S(1)} %fusion.1), channel_id=1, source_target_pairs={{0,2},{1,3},{2,0},{3,1},{4,6},{5,7},{6,4},{7,5},{8,10},{9,11},{10,... | collective-permute-start | bytes 245768 | tf_op jit(solution)/shard_map/ppermute | solution.py:421
  118.8 6.2 %collective-permute-start.27 = (f32[160,128]{1,0:T(8,128)S(1)}, f32[160,128]{1,0:T(8,128)S(1)}, u32[]{:S(2)}, u32[]{:S(2)}) collective-permute-start(f32[160,128]{1,0:T(8,128)S(1)} %fusion.1), channel_id=1, source_target_pairs={{0,1},{1,0},{2,3},{3,2},{4,5},{5,4},{6,7},{7,6},{8,9},{9,8},{10,11... | collective-permute-start | bytes 245768 | tf_op jit(solution)/shard_map/ppermute | solution.py:421
  125.9 5.3 %collective-permute-start.29 = (f32[160,128]{1,0:T(8,128)S(1)}, f32[160,128]{1,0:T(8,128)S(1)}, u32[]{:S(2)}, u32[]{:S(2)}) collective-permute-start(f32[160,128]{1,0:T(8,128)S(1)} %add_add_fusion.2), channel_id=1, source_target_pairs={{0,8},{4,12},{8,0},{12,4},{1,9},{5,13},{9,1},{13,5},{2,10},{6,14},... | collective-permute-start | bytes 245768 | tf_op jit(solution)/shard_map/ppermute | solution.py:421
  127.8 5.3 %collective-permute-start.30 = (f32[160,128]{1,0:T(8,128)S(1)}, f32[160,128]{1,0:T(8,128)S(1)}, u32[]{:S(2)}, u32[]{:S(2)}) collective-permute-start(f32[160,128]{1,0:T(8,128)S(1)} %add_add_fusion.2), channel_id=1, source_target_pairs={{0,12},{4,8},{8,4},{12,0},{1,13},{5,9},{9,5},{13,1},{2,14},{6,10},... | collective-permute-start | bytes 245768 | tf_op jit(solution)/shard_map/ppermute | solution.py:421
  298.7 10.7 %collective-permute-start.32 = (f32[384,128]{1,0:T(8,128)S(1)}, f32[384,128]{1,0:T(8,128)S(1)}, u32[]{:S(2)}, u32[]{:S(2)}) collective-permute-start(f32[384,128]{1,0:T(8,128)S(1)} %get-tuple-element.72), channel_id=1, source_target_pairs={{0,1},{1,0},{2,3},{3,2},{4,5},{5,4},{6,7},{7,6},{8,9},{9,8},{10,11... | collective-permute-start | bytes 589832 | tf_op jit(solution)/shard_map/ppermute | solution.py:421
  299.2 17.6 %collective-permute-start.33 = (f32[384,128]{1,0:T(8,128)S(1)}, f32[384,128]{1,0:T(8,128)S(1)}, u32[]{:S(2)}, u32[]{:S(2)}) collective-permute-start(f32[384,128]{1,0:T(8,128)S(1)} %get-tuple-element.73), channel_id=1, source_target_pairs={{0,2},{1,3},{2,0},{3,1},{4,6},{5,7},{6,4},{7,5},{8,10},{9,11},{10,... | collective-permute-start | bytes 589832 | tf_op jit(solution)/shard_map/ppermute | solution.py:421
  302.6 14.2 %collective-permute-start.34 = (f32[384,128]{1,0:T(8,128)S(1)}, f32[384,128]{1,0:T(8,128)S(1)}, u32[]{:S(2)}, u32[]{:S(2)}) collective-permute-start(f32[384,128]{1,0:T(8,128)S(1)} %get-tuple-element.74), channel_id=1, source_target_pairs={{0,3},{1,2},{2,1},{3,0},{4,7},{5,6},{6,5},{7,4},{8,11},{9,10},{10,... | collective-permute-start | bytes 589832 | tf_op jit(solution)/shard_map/ppermute | solution.py:421
  (5 other events, 33.4 us)

commit v4 on v3

--- a/solution.py
+++ b/solution.py
@@ -58,7 +58,7 @@
             bytes_accessed=count * blocks * sub * (2 * depth + 4 * across) + 2 * depth * across,
             transcendentals=0,
         ),
-        compiler_params=grant(28),
+        compiler_params=grant(18),
         name="product_pieces",
     )(jnp.stack(dests), *[panel] * fetches, sketch)
     return [outs[k * outs_each : (k + 1) * outs_each] for k in range(count)]
@@ -171,7 +171,8 @@
 
     def kernel(here_ref, *refs):
         piece_refs, share_ref = refs[:siblings], refs[siblings]
-        out_refs, (packed_ref, g_ref, x_ref, e_ref) = refs[siblings + 1 : -4], refs[-4:]
+        out_refs, strip_ref = refs[siblings + 1 : -5], refs[-5]
+        packed_ref, g_ref, x_ref, e_ref = refs[-4:]
         for s in range(siblings):
             for m in range(members):
                 spot = ((here_ref[0] ^ s) * members + (here_ref[1] ^ m)) * piece
@@ -278,27 +279,50 @@
 
             lax.fori_loop(0, n, eliminate, 0)
 
-        split_share = split(share_ref[...])
+        strip_ref[...] = x_ref[pl.ds(pl.multiple_of(here_ref[2] * tile, tile), tile), :]
         for i in range(count):
-            upto = slice(0, (i + 1) * tile)
-            strip = split(x_ref[i * tile : (i + 1) * tile, upto])
-            product = triple(on_last, (split_share[0][:, upto], split_share[1][:, upto]), strip)
-            for k in range(count):
-
-                @pl.when(here_ref[2] == (i ^ k))
-                def _():
-                    out_refs[k][...] = product
+
+            @pl.when(here_ref[2] != i)
+            def _():
+                upto = slice(0, (i + 1) * tile)
+                strip = split(x_ref[i * tile : (i + 1) * tile, upto])
+                share = split(share_ref[:, upto])
+                product = triple(on_last, share, strip)
+                for k in range(1, count):
+
+                    @pl.when(here_ref[2] == (i ^ k))
+                    def _():
+                        out_refs[k - 1][...] = product
 
     return pl.pallas_call(
         kernel,
-        out_shape=[jax.ShapeDtypeStruct((rows, tile), jnp.float32)] * count,
+        out_shape=[jax.ShapeDtypeStruct((rows, tile), jnp.float32)] * (count - 1)
+        + [jax.ShapeDtypeStruct((tile, n), jnp.float32)],
         in_specs=[pl.BlockSpec(memory_space=pltpu.SMEM)] + [pl.BlockSpec(memory_space=pltpu.VMEM)] * (1 + siblings),
         out_specs=[pl.BlockSpec(memory_space=pltpu.VMEM)] * count,
         scratch_shapes=[pltpu.VMEM((height, tile), jnp.float32)] + [pltpu.VMEM((n, n), jnp.float32)] * 3,
         cost_estimate=pl.CostEstimate(flops=12 * n * n * n, bytes_accessed=4 * n * (n + rows), transcendentals=0),
-        compiler_params=grant(40),
+        compiler_params=grant(26),
         name="basis_pieces",
     )(here, *pieces, share)
+
+
+def own_piece(share, strip):
+    rows, n = share.shape
+    tile = strip.shape[0]
+
+    def kernel(share_ref, strip_ref, out_ref):
+        out_ref[...] = triple(on_last, split(share_ref[...]), split(strip_ref[...]))
+
+    return pl.pallas_call(
+        kernel,
+        out_shape=jax.ShapeDtypeStruct((rows, tile), jnp.float32),
+        in_specs=[pl.BlockSpec(memory_space=pltpu.VMEM)] * 2,
+        out_specs=pl.BlockSpec(memory_space=pltpu.VMEM),
+        cost_estimate=pl.CostEstimate(flops=6 * rows * n * tile, bytes_accessed=4 * rows * (n + tile), transcendentals=0),
+        compiler_params=grant(12),
+        name="own_piece",
+    )(share, strip)
 
 
 def lay_out(pieces, here, slots, sub, blk):
@@ -436,9 +460,9 @@
     for level in levels:
         pieces = pieces + [swap(p, "front", level) for p in pieces]
 
-    basis = basis_pieces(pieces, share, here, rows, width)
-    came = {k: swap(basis[k], "col", k) for k in range(1, cols)[::-1]}
-    pieces = [basis[0]] + [came[k] for k in range(1, cols)]
+    *basis, strip = basis_pieces(pieces, share, here, rows, width)
+    came = {k: swap(basis[k - 1], "col", k) for k in range(1, cols)[::-1]}
+    pieces = [own_piece(share, strip)] + [came[k] for k in range(1, cols)]
     return lay_out(pieces, col_here, slots, sub, BLK)
 
 

time: 320 us -> 318 us (level)
  no operation moved by 1% of the time
where the time goes in v4:
time: 318 us; the launch traced here: 317 us
  Pallas kernels  185 us (58%)
  starting transfers between devices  63.1 us (20%)
  waiting for transfers between devices  56.2 us (18%)
  other arithmetic  10.7 us (3%)
    pallas_call x1, Pallas kernels, basis_pieces(): pl.pallas_call(kernel, out_shape=[jax.ShapeDtypeStruct((rows, tile), jnp....  163 us
    ppermute x14, waiting for transfers between devices, swap(): lax.ppermute(x, name, [(i, i ^ level) for i in range(lax.axis_size(name))])  30.7 us
    ppermute x6, starting transfers between devices, shards(): came_up = lax.ppermute(up, 'col', [(i, i + 1) for i in range(stage)])  20.6 us
    ppermute x6, waiting for transfers between devices, shards(): came_up = lax.ppermute(up, 'col', [(i, i + 1) for i in range(stage)])  18.3 us
    ppermute x6, starting transfers between devices, shards(): came.append(lax.ppermute(slotted[k], both, pairs))  17.4 us
    ppermute x14, starting transfers between devices, swap(): lax.ppermute(x, name, [(i, i ^ level) for i in range(lax.axis_size(name))])  17.2 us
    pallas_call x3, Pallas kernels, product_pieces(): pl.pallas_call(kernel, out_shape=[jax.ShapeDtypeStruct((blocks, sub, widt...  16.9 us
    ppermute x6, starting transfers between devices, shards(): lax.ppermute(down, 'col', [(i, i - 1) for i in range(cols - stage, cols)])  7.7 us
  transfers between devices with their start and end apart: 35, of which 21 were waited for; matrix products, arithmetic and copies ran while one was open for 3% of the time, Pallas kernels for 5%

profile of v4, /device:TPU:0, one launch (start us, length us, event | category | flops | bytes accessed | tf_op | source)
XLA Modules:
  0.0 316.7 jit_solution(3339333632852420070)
XLA Ops:
  0.0 3.3 %conditional.3 = (f32[16,32,256]{2,1,0:T(8,128)}) conditional(s32[]{:T(128)} %convert_element_type.4, () %tuple.19, (s32[]{:T(128)}, bf16[16,128,2048]{2,1,0:T(8,128)(2,1)}, bf16[2048,512]{1,0:T(8,128)(2,1)}) %tuple.28), branch_computations={%region_3.4_spmd, %region_4.5_spmd} | conditional | flops 536870912 | bytes 3670024 | solution.py:407
  0.0 3.3 %product_pieces.4 = f32[16,32,256]{2,1,0:T(8,128)} custom-call(s32[1]{0:T(128)} %bitcast.1.dest_ref, bf16[16,128,2048]{2,1,0:T(8,128)(2,1)} %get-tuple-element.27.refs_0_.refs_1_.refs_2_.refs_3_, bf16[16,128,2048]{2,1,0:T(8,128)(2,1)} %get-tuple-element.27.refs_0_.refs_1_.refs_2_.refs_3_, ...), custom_call_target="tpu_custom_call" | custom-call | flops 536870912 | bytes 3670016 | tf_op jit(solution)/shard_map/cond/branch_1_fun/product_pieces/pallas_call | solution.py:41
  3.3 2.5 collective-permute-start.11
  7.3 3.3 %conditional.2 = (f32[16,32,256]{2,1,0:T(8,128)}) conditional(s32[]{:T(128)} %convert_element_type.4, () %tuple.17, (s32[]{:T(128)}, bf16[16,128,2048]{2,1,0:T(8,128)(2,1)}, bf16[2048,512]{1,0:T(8,128)(2,1)}) %tuple.29), branch_computations={%region_1.2_spmd, %region_2.3_spmd} | conditional | flops 536870912 | bytes 3670024 | solution.py:407
  7.3 3.3 %product_pieces.3 = f32[16,32,256]{2,1,0:T(8,128)} custom-call(s32[1]{0:T(128)} %bitcast.dest_ref, bf16[16,128,2048]{2,1,0:T(8,128)(2,1)} %get-tuple-element.24.refs_0_.refs_1_.refs_2_.refs_3_, bf16[16,128,2048]{2,1,0:T(8,128)(2,1)} %get-tuple-element.24.refs_0_.refs_1_.refs_2_.refs_3_, ...), custom_call_target="tpu_custom_call" | custom-call | flops 536870912 | bytes 3670016 | tf_op jit(solution)/shard_map/cond/branch_1_fun/product_pieces/pallas_call | solution.py:41
  13.5 10.3 %product_pieces.5 = (f32[16,32,256]{2,1,0:T(8,128)S(1)}, f32[16,32,256]{2,1,0:T(8,128)S(1)}, f32[16,32,256]{2,1,0:T(8,128)S(1)}, f32[16,32,256]{2,1,0:T(8,128)S(...) custom-call(s32[4]{0:T(128)S(1)} %pad_add_fusion.2.dest_ref, ...), custom_call_target="tpu_custom_call" | custom-call | flops 4294967296 | bytes 14680064 | tf_op jit(solution)/shard_map/product_pieces/pallas_call | solution.py:41
  27.1 2.6 collective-permute-done.1
  30.5 2.1 fusion.3
  32.6 5.1 %collective-permute-start.2 = (f32[16,32,256]{2,1,0:T(8,128)}, f32[16,32,256]{2,1,0:T(8,128)}, u32[]{:S(2)}, u32[]{:S(2)}) collective-permute-start(f32[16,32,256]{2,1,0:T(8,128)} %get-tuple-element.77), channel_id=1, source_target_pairs={{0,1},{1,2},{4,5},{5,6},{8,9},{9,10},{12,13},{13,14},{16,17},{17,1... | collective-permute-start | bytes 1572872 | tf_op jit(solution)/shard_map/ppermute | solution.py:420
  39.1 1.7 collective-permute-done.12
  40.9 5.2 %collective-permute-start.13 = (f32[16,32,256]{2,1,0:T(8,128)S(1)}, f32[16,32,256]{2,1,0:T(8,128)}, u32[]{:S(2)}, u32[]{:S(2)}) collective-permute-start(f32[16,32,256]{2,1,0:T(8,128)S(1)} %add.118), channel_id=1, source_target_pairs={{0,1},{1,2},{2,3},{4,5},{5,6},{6,7},{8,9},{9,10},{10,11},{12,13},{... | collective-permute-start | bytes 1572872 | tf_op jit(solution)/shard_map/ppermute | solution.py:420
  48.3 3.8 %collective-permute-done.2 = f32[16,32,256]{2,1,0:T(8,128)} collective-permute-done((f32[16,32,256]{2,1,0:T(8,128)}, f32[16,32,256]{2,1,0:T(8,128)}, u32[]{:S(2)}, u32[]{:S(2)}) %collective-permute-start.2) | collective-permute-done | bytes 524320 | tf_op jit(solution)/shard_map/ppermute | solution.py:420
  52.1 1.9 add.112
  54.0 5.2 %collective-permute-start.3 = (f32[16,32,256]{2,1,0:T(8,128)}, f32[16,32,256]{2,1,0:T(8,128)}, u32[]{:S(2)}, u32[]{:S(2)}) collective-permute-start(f32[16,32,256]{2,1,0:T(8,128)} %add.112), channel_id=1, source_target_pairs={{0,1},{1,2},{2,3},{4,5},{5,6},{6,7},{8,9},{9,10},{10,11},{12,13},{... | collective-permute-start | bytes 1572872 | tf_op jit(solution)/shard_map/ppermute | solution.py:420
  64.7 8.7 %collective-permute-done.3 = f32[16,32,256]{2,1,0:T(8,128)} collective-permute-done((f32[16,32,256]{2,1,0:T(8,128)}, f32[16,32,256]{2,1,0:T(8,128)}, u32[]{:S(2)}, u32[]{:S(2)}) %collective-permute-start.3) | collective-permute-done | bytes 524320 | tf_op jit(solution)/shard_map/ppermute | solution.py:420
  77.1 5.2 %collective-permute-start.18 = (f32[12,32,256]{2,1,0:T(8,128)S(1)}, f32[12,32,256]{2,1,0:T(8,128)S(1)}, u32[]{:S(2)}, u32[]{:S(2)}) collective-permute-start(f32[12,32,256]{2,1,0:T(8,128)S(1)} %get-tuple-element.65), channel_id=1, source_target_pairs={{0,12},{4,8},{24,20},{28,16},{1,13},{5,9},{25,21},{29,17},{2,14},{... | collective-permute-start | bytes 1179656 | tf_op jit(solution)/shard_map/ppermute | solution.py:437
  83.6 2.5 collective-permute-start.20
  90.0 5.8 %collective-permute-start.9 = (f32[12,32,256]{2,1,0:T(8,128)S(1)}, f32[12,32,256]{2,1,0:T(8,128)S(1)}, u32[]{:S(2)}, u32[]{:S(2)}) collective-permute-start(f32[12,32,256]{2,1,0:T(8,128)S(1)} %get-tuple-element.58), channel_id=1, source_target_pairs={{0,8},{4,12},{24,16},{28,20},{1,9},{5,13},{25,17},{29,21},{2,10},{... | collective-permute-start | bytes 1179656 | tf_op jit(solution)/shard_map/ppermute | solution.py:437
  96.0 4.3 %collective-permute-done.8.refs_1_ = f32[12,32,256]{2,1,0:T(8,128)S(1)} collective-permute-done((f32[12,32,256]{2,1,0:T(8,128)S(1)}, f32[12,32,256]{2,1,0:T(8,128)S(1)}, u32[]{:S(2)}, u32[]{:S(2)}) %collective-permute-start.8) | collective-permute-done | bytes 393248 | tf_op jit(solution)/shard_map/ppermute | solution.py:437
  100.3 2.5 collective-permute-done.9.refs_2_
  104.3 1.6 collective-permute-done.21
  106.0 2.2 collective-permute-start.22
  111.5 1.7 collective-permute-done.23
  114.2 3.3 %collective-permute-start.25 = (f32[160,128]{1,0:T(8,128)S(1)}, f32[160,128]{1,0:T(8,128)S(1)}, u32[]{:S(2)}, u32[]{:S(2)}) collective-permute-start(f32[160,128]{1,0:T(8,128)S(1)} %fusion.1), channel_id=1, source_target_pairs={{0,3},{1,2},{2,1},{3,0},{4,7},{5,6},{6,5},{7,4},{8,11},{9,10},{10,... | collective-permute-start | bytes 245768 | tf_op jit(solution)/shard_map/ppermute | solution.py:445
  120.7 4.3 %collective-permute-done.26 = f32[160,128]{1,0:T(8,128)S(1)} collective-permute-done((f32[160,128]{1,0:T(8,128)S(1)}, f32[160,128]{1,0:T(8,128)S(1)}, u32[]{:S(2)}, u32[]{:S(2)}) %collective-permute-start.26) | collective-permute-done | bytes 81952 | tf_op jit(solution)/shard_map/ppermute | solution.py:445
  125.9 1.9 collective-permute-start.29
  131.2 1.9 collective-permute-done.30
  133.2 1.6 collective-permute-done.31.refs_1_
  134.9 162.7 %basis_pieces.1 = (f32[384,128]{1,0:T(8,128)S(1)}, f32[384,128]{1,0:T(8,128)S(1)}, f32[384,128]{1,0:T(8,128)S(1)}, f32[128,512]{1,0:T(8,128)S(1)}) custom-call(s32[3]{0:T(128)S(1)} %pad_add_fusion.1.here_ref, f32[640,128]{1,0:T(8,128)S(1)} %pad_maximum_fusion.refs_0_, f32[640,128]{1,0:T(8,128)S(1)} %collective-permute-done.31.refs_1_, ...), custom_call_target="tpu_custom_call" | custom-call | flops 1610612736 | bytes 1835008 | tf_op jit(solution)/shard_map/basis_pieces/pallas_call | solution.py:297
  298.0 3.2 %collective-permute-start.33 = (f32[384,128]{1,0:T(8,128)S(1)}, f32[384,128]{1,0:T(8,128)S(1)}, u32[]{:S(2)}, u32[]{:S(2)}) collective-permute-start(f32[384,128]{1,0:T(8,128)S(1)} %get-tuple-element.73), channel_id=1, source_target_pairs={{0,2},{1,3},{2,0},{3,1},{4,6},{5,7},{6,4},{7,5},{8,10},{9,11},{10,... | collective-permute-start | bytes 589832 | tf_op jit(solution)/shard_map/ppermute | solution.py:445
  302.5 5.8 %collective-permute-done.32.refs_1_ = f32[384,128]{1,0:T(8,128)S(1)} collective-permute-done((f32[384,128]{1,0:T(8,128)S(1)}, f32[384,128]{1,0:T(8,128)S(1)}, u32[]{:S(2)}, u32[]{:S(2)}) %collective-permute-start.32) | collective-permute-done | bytes 196640 | tf_op jit(solution)/shard_map/ppermute | solution.py:445
  308.3 7.2 %collective-permute-done.33.refs_2_ = f32[384,128]{1,0:T(8,128)S(1)} collective-permute-done((f32[384,128]{1,0:T(8,128)S(1)}, f32[384,128]{1,0:T(8,128)S(1)}, u32[]{:S(2)}, u32[]{:S(2)}) %collective-permute-start.33) | collective-permute-done | bytes 196640 | tf_op jit(solution)/shard_map/ppermute | solution.py:445
  (76 shorter events, 42.9 us)
Async XLA Ops:
  3.3 20.6 %collective-permute-start.11 = (f32[16,32,256]{2,1,0:T(8,128)}, f32[16,32,256]{2,1,0:T(8,128)S(1)}, u32[]{:S(2)}, u32[]{:S(2)}) collective-permute-start(f32[16,32,256]{2,1,0:T(8,128)} %get-tuple-element.83), channel_id=1, source_target_pairs={{0,1},{4,5},{8,9},{12,13},{16,17},{20,21},{24,25},{28,29}} | collective-permute-start | bytes 1572872 | tf_op jit(solution)/shard_map/ppermute | solution.py:420
  5.8 18.0 %collective-permute-start.14 = (f32[16,32,256]{2,1,0:T(8,128)}, f32[16,32,256]{2,1,0:T(8,128)}, u32[]{:S(2)}, u32[]{:S(2)}) collective-permute-start(f32[16,32,256]{2,1,0:T(8,128)} %get-tuple-element.83), channel_id=1, source_target_pairs={{3,2},{7,6},{11,10},{15,14},{19,18},{23,22},{27,26},{31,30}} | collective-permute-start | bytes 1572872 | tf_op jit(solution)/shard_map/ppermute | solution.py:421
  10.6 19.1 %collective-permute-start.1 = (f32[16,32,256]{2,1,0:T(8,128)}, f32[16,32,256]{2,1,0:T(8,128)S(1)}, u32[]{:S(2)}, u32[]{:S(2)}) collective-permute-start(f32[16,32,256]{2,1,0:T(8,128)} %get-tuple-element.82), channel_id=1, source_target_pairs={{0,1},{4,5},{8,9},{12,13},{16,17},{20,21},{24,25},{28,29}} | collective-permute-start | bytes 1572872 | tf_op jit(solution)/shard_map/ppermute | solution.py:420
  11.9 17.7 %collective-permute-start.4 = (f32[16,32,256]{2,1,0:T(8,128)}, f32[16,32,256]{2,1,0:T(8,128)}, u32[]{:S(2)}, u32[]{:S(2)}) collective-permute-start(f32[16,32,256]{2,1,0:T(8,128)} %get-tuple-element.82), channel_id=1, source_target_pairs={{3,2},{7,6},{11,10},{15,14},{19,18},{23,22},{27,26},{31,30}} | collective-permute-start | bytes 1572872 | tf_op jit(solution)/shard_map/ppermute | solution.py:421
  25.0 15.8 %collective-permute-start.12 = (f32[16,32,256]{2,1,0:T(8,128)S(1)}, f32[16,32,256]{2,1,0:T(8,128)S(1)}, u32[]{:S(2)}, u32[]{:S(2)}) collective-permute-start(f32[16,32,256]{2,1,0:T(8,128)S(1)} %get-tuple-element.75), channel_id=1, source_target_pairs={{0,1},{1,2},{4,5},{5,6},{8,9},{9,10},{12,13},{13,14},{16,17},{17,1... | collective-permute-start | bytes 1572872 | tf_op jit(solution)/shard_map/ppermute | solution.py:420
  26.4 19.7 %collective-permute-start.15 = (f32[16,32,256]{2,1,0:T(8,128)S(1)}, f32[16,32,256]{2,1,0:T(8,128)S(1)}, u32[]{:S(2)}, u32[]{:S(2)}) collective-permute-start(f32[16,32,256]{2,1,0:T(8,128)S(1)} %get-tuple-element.76), channel_id=1, source_target_pairs={{2,1},{3,2},{6,5},{7,6},{10,9},{11,10},{14,13},{15,14},{18,17},{19... | collective-permute-start | bytes 1572872 | tf_op jit(solution)/shard_map/ppermute | solution.py:421
  32.6 19.5 %collective-permute-start.2 = (f32[16,32,256]{2,1,0:T(8,128)}, f32[16,32,256]{2,1,0:T(8,128)}, u32[]{:S(2)}, u32[]{:S(2)}) collective-permute-start(f32[16,32,256]{2,1,0:T(8,128)} %get-tuple-element.77), channel_id=1, source_target_pairs={{0,1},{1,2},{4,5},{5,6},{8,9},{9,10},{12,13},{13,14},{16,17},{17,1... | collective-permute-start | bytes 1572872 | tf_op jit(solution)/shard_map/ppermute | solution.py:420
  37.7 21.6 %collective-permute-start.5 = (f32[16,32,256]{2,1,0:T(8,128)S(1)}, f32[16,32,256]{2,1,0:T(8,128)}, u32[]{:S(2)}, u32[]{:S(2)}) collective-permute-start(f32[16,32,256]{2,1,0:T(8,128)S(1)} %get-tuple-element.78), channel_id=1, source_target_pairs={{2,1},{3,2},{6,5},{7,6},{10,9},{11,10},{14,13},{15,14},{18,17},{19... | collective-permute-start | bytes 1572872 | tf_op jit(solution)/shard_map/ppermute | solution.py:421
  40.9 22.4 %collective-permute-start.13 = (f32[16,32,256]{2,1,0:T(8,128)S(1)}, f32[16,32,256]{2,1,0:T(8,128)}, u32[]{:S(2)}, u32[]{:S(2)}) collective-permute-start(f32[16,32,256]{2,1,0:T(8,128)S(1)} %add.118), channel_id=1, source_target_pairs={{0,1},{1,2},{2,3},{4,5},{5,6},{6,7},{8,9},{9,10},{10,11},{12,13},{... | collective-permute-start | bytes 1572872 | tf_op jit(solution)/shard_map/ppermute | solution.py:420
  46.9 16.3 %collective-permute-start.16 = (f32[16,32,256]{2,1,0:T(8,128)}, f32[16,32,256]{2,1,0:T(8,128)}, u32[]{:S(2)}, u32[]{:S(2)}) collective-permute-start(f32[16,32,256]{2,1,0:T(8,128)} %add.121), channel_id=1, source_target_pairs={{1,0},{2,1},{3,2},{5,4},{6,5},{7,6},{9,8},{10,9},{11,10},{13,12},{... | collective-permute-start | bytes 1572872 | tf_op jit(solution)/shard_map/ppermute | solution.py:421
  48.2 16.4 %collective-permute-start = (s32[64]{0:T(128)S(1)}, s32[64]{0:T(128)S(1)}, u32[]{:S(2)}, u32[]{:S(2)}) collective-permute-start(s32[64]{0:T(128)S(1)} %bitcast.18), channel_id=1, source_target_pairs={{0,16},{16,0},{1,17},{17,1},{2,18},{18,2},{3,19},{19,3},{4,20},{20... | collective-permute-start | bytes 776 | tf_op jit(solution)/shard_map/ppermute | solution.py:378
  54.0 19.4 %collective-permute-start.3 = (f32[16,32,256]{2,1,0:T(8,128)}, f32[16,32,256]{2,1,0:T(8,128)}, u32[]{:S(2)}, u32[]{:S(2)}) collective-permute-start(f32[16,32,256]{2,1,0:T(8,128)} %add.112), channel_id=1, source_target_pairs={{0,1},{1,2},{2,3},{4,5},{5,6},{6,7},{8,9},{9,10},{10,11},{12,13},{... | collective-permute-start | bytes 1572872 | tf_op jit(solution)/shard_map/ppermute | solution.py:420
  60.3 13.4 %collective-permute-start.6 = (f32[16,32,256]{2,1,0:T(8,128)S(1)}, f32[16,32,256]{2,1,0:T(8,128)}, u32[]{:S(2)}, u32[]{:S(2)}) collective-permute-start(f32[16,32,256]{2,1,0:T(8,128)S(1)} %add.115), channel_id=1, source_target_pairs={{1,0},{2,1},{3,2},{5,4},{6,5},{7,6},{9,8},{10,9},{11,10},{13,12},{... | collective-permute-start | bytes 1572872 | tf_op jit(solution)/shard_map/ppermute | solution.py:421
  64.6 11.3 %collective-permute-start.17 = (f32[16,32,256]{2,1,0:T(8,128)S(1)}, f32[16,32,256]{2,1,0:T(8,128)S(1)}, u32[]{:S(2)}, u32[]{:S(2)}) collective-permute-start(f32[16,32,256]{2,1,0:T(8,128)S(1)} %add_add_fusion.refs_0_), channel_id=1, source_target_pairs={{0,16},{16,0},{1,17},{17,1},{2,18},{18,2},{3,19},{19,3},{4,20},{20... | collective-permute-start | bytes 1572872 | tf_op jit(solution)/shard_map/ppermute | solution.py:426
  75.0 11.1 %collective-permute-start.7 = (f32[16,32,256]{2,1,0:T(8,128)S(1)}, f32[16,32,256]{2,1,0:T(8,128)S(1)}, u32[]{:S(2)}, u32[]{:S(2)}) collective-permute-start(f32[16,32,256]{2,1,0:T(8,128)S(1)} %add_add_fusion.1.refs_0_), channel_id=1, source_target_pairs={{0,16},{16,0},{1,17},{17,1},{2,18},{18,2},{3,19},{19,3},{4,20},{20... | collective-permute-start | bytes 1572872 | tf_op jit(solution)/shard_map/ppermute | solution.py:426
  77.1 12.9 %collective-permute-start.18 = (f32[12,32,256]{2,1,0:T(8,128)S(1)}, f32[12,32,256]{2,1,0:T(8,128)S(1)}, u32[]{:S(2)}, u32[]{:S(2)}) collective-permute-start(f32[12,32,256]{2,1,0:T(8,128)S(1)} %get-tuple-element.65), channel_id=1, source_target_pairs={{0,12},{4,8},{24,20},{28,16},{1,13},{5,9},{25,21},{29,17},{2,14},{... | collective-permute-start | bytes 1179656 | tf_op jit(solution)/shard_map/ppermute | solution.py:437
  82.3 13.6 %collective-permute-start.19 = (f32[12,32,256]{2,1,0:T(8,128)S(1)}, f32[12,32,256]{2,1,0:T(8,128)S(1)}, u32[]{:S(2)}, u32[]{:S(2)}) collective-permute-start(f32[12,32,256]{2,1,0:T(8,128)S(1)} %get-tuple-element.66), channel_id=1, source_target_pairs={{0,8},{4,12},{24,16},{28,20},{1,9},{5,13},{25,17},{29,21},{2,10},{... | collective-permute-start | bytes 1179656 | tf_op jit(solution)/shard_map/ppermute | solution.py:437
  83.6 12.3 %collective-permute-start.20 = (f32[12,32,256]{2,1,0:T(8,128)S(1)}, f32[12,32,256]{2,1,0:T(8,128)S(1)}, u32[]{:S(2)}, u32[]{:S(2)}) collective-permute-start(f32[12,32,256]{2,1,0:T(8,128)S(1)} %get-tuple-element.67), channel_id=1, source_target_pairs={{0,4},{8,12},{20,16},{28,24},{1,5},{9,13},{21,17},{29,25},{2,6},{1... | collective-permute-start | bytes 1179656 | tf_op jit(solution)/shard_map/ppermute | solution.py:437
  87.3 8.7 %collective-permute-start.10 = (f32[12,32,256]{2,1,0:T(8,128)S(1)}, f32[12,32,256]{2,1,0:T(8,128)S(1)}, u32[]{:S(2)}, u32[]{:S(2)}) collective-permute-start(f32[12,32,256]{2,1,0:T(8,128)S(1)} %get-tuple-element.59), channel_id=1, source_target_pairs={{0,4},{8,12},{20,16},{28,24},{1,5},{9,13},{21,17},{29,25},{2,6},{1... | collective-permute-start | bytes 1179656 | tf_op jit(solution)/shard_map/ppermute | solution.py:437
  88.7 11.6 %collective-permute-start.8 = (f32[12,32,256]{2,1,0:T(8,128)S(1)}, f32[12,32,256]{2,1,0:T(8,128)S(1)}, u32[]{:S(2)}, u32[]{:S(2)}) collective-permute-start(f32[12,32,256]{2,1,0:T(8,128)S(1)} %get-tuple-element.57), channel_id=1, source_target_pairs={{0,12},{4,8},{24,20},{28,16},{1,13},{5,9},{25,21},{29,17},{2,14},{... | collective-permute-start | bytes 1179656 | tf_op jit(solution)/shard_map/ppermute | solution.py:437
  90.0 12.8 %collective-permute-start.9 = (f32[12,32,256]{2,1,0:T(8,128)S(1)}, f32[12,32,256]{2,1,0:T(8,128)S(1)}, u32[]{:S(2)}, u32[]{:S(2)}) collective-permute-start(f32[12,32,256]{2,1,0:T(8,128)S(1)} %get-tuple-element.58), channel_id=1, source_target_pairs={{0,8},{4,12},{24,16},{28,20},{1,9},{5,13},{25,17},{29,21},{2,10},{... | collective-permute-start | bytes 1179656 | tf_op jit(solution)/shard_map/ppermute | solution.py:437
  106.0 5.5 %collective-permute-start.22 = (f32[160,128]{1,0:T(8,128)S(1)}, f32[160,128]{1,0:T(8,128)S(1)}, u32[]{:S(2)}, u32[]{:S(2)}) collective-permute-start(f32[160,128]{1,0:T(8,128)S(1)} %get-tuple-element.79), channel_id=1, source_target_pairs={{0,12},{4,8},{8,4},{12,0},{1,13},{5,9},{9,5},{13,1},{2,14},{6,10},... | collective-permute-start | bytes 245768 | tf_op jit(solution)/shard_map/ppermute | solution.py:445
  108.2 5.0 %collective-permute-start.23 = (f32[160,128]{1,0:T(8,128)S(1)}, f32[160,128]{1,0:T(8,128)S(1)}, u32[]{:S(2)}, u32[]{:S(2)}) collective-permute-start(f32[160,128]{1,0:T(8,128)S(1)} %get-tuple-element.81), channel_id=1, source_target_pairs={{0,8},{4,12},{8,0},{12,4},{1,9},{5,13},{9,1},{13,5},{2,10},{6,14},... | collective-permute-start | bytes 245768 | tf_op jit(solution)/shard_map/ppermute | solution.py:445
  108.6 5.6 %collective-permute-start.24 = (f32[160,128]{1,0:T(8,128)S(1)}, f32[160,128]{1,0:T(8,128)S(1)}, u32[]{:S(2)}, u32[]{:S(2)}) collective-permute-start(f32[160,128]{1,0:T(8,128)S(1)} %get-tuple-element.80), channel_id=1, source_target_pairs={{0,4},{4,0},{8,12},{12,8},{1,5},{5,1},{9,13},{13,9},{2,6},{6,2},{1... | collective-permute-start | bytes 245768 | tf_op jit(solution)/shard_map/ppermute | solution.py:445
  114.2 6.4 %collective-permute-start.25 = (f32[160,128]{1,0:T(8,128)S(1)}, f32[160,128]{1,0:T(8,128)S(1)}, u32[]{:S(2)}, u32[]{:S(2)}) collective-permute-start(f32[160,128]{1,0:T(8,128)S(1)} %fusion.1), channel_id=1, source_target_pairs={{0,3},{1,2},{2,1},{3,0},{4,7},{5,6},{6,5},{7,4},{8,11},{9,10},{10,... | collective-permute-start | bytes 245768 | tf_op jit(solution)/shard_map/ppermute | solution.py:445
  117.6 7.4 %collective-permute-start.26 = (f32[160,128]{1,0:T(8,128)S(1)}, f32[160,128]{1,0:T(8,128)S(1)}, u32[]{:S(2)}, u32[]{:S(2)}) collective-permute-start(f32[160,128]{1,0:T(8,128)S(1)} %fusion.1), channel_id=1, source_target_pairs={{0,2},{1,3},{2,0},{3,1},{4,6},{5,7},{6,4},{7,5},{8,10},{9,11},{10,... | collective-permute-start | bytes 245768 | tf_op jit(solution)/shard_map/ppermute | solution.py:445
  118.8 6.2 %collective-permute-start.27 = (f32[160,128]{1,0:T(8,128)S(1)}, f32[160,128]{1,0:T(8,128)S(1)}, u32[]{:S(2)}, u32[]{:S(2)}) collective-permute-start(f32[160,128]{1,0:T(8,128)S(1)} %fusion.1), channel_id=1, source_target_pairs={{0,1},{1,0},{2,3},{3,2},{4,5},{5,4},{6,7},{7,6},{8,9},{9,8},{10,11... | collective-permute-start | bytes 245768 | tf_op jit(solution)/shard_map/ppermute | solution.py:445
  125.9 5.3 %collective-permute-start.29 = (f32[160,128]{1,0:T(8,128)S(1)}, f32[160,128]{1,0:T(8,128)S(1)}, u32[]{:S(2)}, u32[]{:S(2)}) collective-permute-start(f32[160,128]{1,0:T(8,128)S(1)} %add_add_fusion.2), channel_id=1, source_target_pairs={{0,8},{4,12},{8,0},{12,4},{1,9},{5,13},{9,1},{13,5},{2,10},{6,14},... | collective-permute-start | bytes 245768 | tf_op jit(solution)/shard_map/ppermute | solution.py:445
  127.8 5.3 %collective-permute-start.30 = (f32[160,128]{1,0:T(8,128)S(1)}, f32[160,128]{1,0:T(8,128)S(1)}, u32[]{:S(2)}, u32[]{:S(2)}) collective-permute-start(f32[160,128]{1,0:T(8,128)S(1)} %add_add_fusion.2), channel_id=1, source_target_pairs={{0,12},{4,8},{8,4},{12,0},{1,13},{5,9},{9,5},{13,1},{2,14},{6,10},... | collective-permute-start | bytes 245768 | tf_op jit(solution)/shard_map/ppermute | solution.py:445
  297.6 10.7 %collective-permute-start.32 = (f32[384,128]{1,0:T(8,128)S(1)}, f32[384,128]{1,0:T(8,128)S(1)}, u32[]{:S(2)}, u32[]{:S(2)}) collective-permute-start(f32[384,128]{1,0:T(8,128)S(1)} %get-tuple-element.72), channel_id=1, source_target_pairs={{0,1},{1,0},{2,3},{3,2},{4,5},{5,4},{6,7},{7,6},{8,9},{9,8},{10,11... | collective-permute-start | bytes 589832 | tf_op jit(solution)/shard_map/ppermute | solution.py:445
  298.0 17.4 %collective-permute-start.33 = (f32[384,128]{1,0:T(8,128)S(1)}, f32[384,128]{1,0:T(8,128)S(1)}, u32[]{:S(2)}, u32[]{:S(2)}) collective-permute-start(f32[384,128]{1,0:T(8,128)S(1)} %get-tuple-element.73), channel_id=1, source_target_pairs={{0,2},{1,3},{2,0},{3,1},{4,6},{5,7},{6,4},{7,5},{8,10},{9,11},{10,... | collective-permute-start | bytes 589832 | tf_op jit(solution)/shard_map/ppermute | solution.py:445
  301.3 14.2 %collective-permute-start.34 = (f32[384,128]{1,0:T(8,128)S(1)}, f32[384,128]{1,0:T(8,128)S(1)}, u32[]{:S(2)}, u32[]{:S(2)}) collective-permute-start(f32[384,128]{1,0:T(8,128)S(1)} %get-tuple-element.74), channel_id=1, source_target_pairs={{0,3},{1,2},{2,1},{3,0},{4,7},{5,6},{6,5},{7,4},{8,11},{9,10},{10,... | collective-permute-start | bytes 589832 | tf_op jit(solution)/shard_map/ppermute | solution.py:445
  (5 other events, 33.4 us)

commit v5 on v4

--- a/solution.py
+++ b/solution.py
@@ -415,8 +415,13 @@
             up = down = next(pieces)[chunk]
             if stage > cols // 2:
                 down = next(pieces)[chunk]
-            if came_up is not None:
+            if came_up is not None and came_up is came_down:
+                up = down = up + came_up
+            elif came_up is not None:
                 up, down = up + came_up, down + came_down
+            if stage == 1 and cols > 3:
+                came_up = came_down = lax.ppermute(up, "col", [(0, 1), (cols - 1, cols - 2)])
+                continue
             came_up = lax.ppermute(up, "col", [(i, i + 1) for i in range(stage)])
             came_down = lax.ppermute(down, "col", [(i, i - 1) for i in range(cols - stage, cols)])
         held = [next(pieces)[chunk] + came_up + came_down]

time: 318 us -> 316 us (level)
  waiting for transfers between devices: 56.2 us -> 61.3 us
  starting transfers between devices: 63.1 us -> 58.6 us
    ppermute x0 -> x2, waiting for transfers between devices: none -> 6.14 us  [shards(): lax.ppermute(up, 'col', [(0, 1), (cols - 1, cols - 2)])]
    ppermute x0 -> x2, starting transfers between devices: none -> 3.85 us  [shards(): lax.ppermute(up, 'col', [(0, 1), (cols - 1, cols - 2)])]
    ppermute x6 -> x4, starting transfers between devices: 20.6 us -> 17.2 us  [shards(): came_up = lax.ppermute(up, 'col', [(i, i + 1) for i in range(stage)])]
    add x6 -> x4, other arithmetic: 7.23 us -> 3.96 us  [shards(): up, down = (up + came_up, down + came_down)]
    ppermute x6 -> x4, starting transfers between devices: 7.7 us -> 4.71 us  [shards(): lax.ppermute(down, 'col', [(i, i - 1) for i in range(cols - stage, cols)])]
    ppermute x6 -> x4, waiting for transfers between devices: 18.3 us -> 17.8 us  [shards(): came_up = lax.ppermute(up, 'col', [(i, i + 1) for i in range(stage)])]
  transfers between devices with their start and end apart: 35 -> 33, of which waited for: 21 -> 19; matrix products, arithmetic and copies ran while one was open for 3% -> 3% of each run, Pallas kernels for 5% -> 5%
where the time goes in v5:
time: 316 us; the launch traced here: 314 us
  Pallas kernels  185 us (59%)
  waiting for transfers between devices  61.3 us (19%)
  starting transfers between devices  58.6 us (19%)
  other arithmetic  8.32 us (3%)
    pallas_call x1, Pallas kernels, basis_pieces(): pl.pallas_call(kernel, out_shape=[jax.ShapeDtypeStruct((rows, tile), jnp....  163 us
    ppermute x14, waiting for transfers between devices, swap(): lax.ppermute(x, name, [(i, i ^ level) for i in range(lax.axis_size(name))])  29.4 us
    ppermute x4, waiting for transfers between devices, shards(): came_up = lax.ppermute(up, 'col', [(i, i + 1) for i in range(stage)])  17.8 us
    ppermute x4, starting transfers between devices, shards(): came_up = lax.ppermute(up, 'col', [(i, i + 1) for i in range(stage)])  17.2 us
    ppermute x14, starting transfers between devices, swap(): lax.ppermute(x, name, [(i, i ^ level) for i in range(lax.axis_size(name))])  17.1 us
    pallas_call x3, Pallas kernels, product_pieces(): pl.pallas_call(kernel, out_shape=[jax.ShapeDtypeStruct((blocks, sub, widt...  16.9 us
    ppermute x6, starting transfers between devices, shards(): came.append(lax.ppermute(slotted[k], both, pairs))  15.5 us
    ppermute x6, waiting for transfers between devices, shards(): came.append(lax.ppermute(slotted[k], both, pairs))  6.71 us
  transfers between devices with their start and end apart: 33, of which 19 were waited for; matrix products, arithmetic and copies ran while one was open for 3% of the time, Pallas kernels for 5%

profile of v5, /device:TPU:0, one launch (start us, length us, event | category | flops | bytes accessed | tf_op | source)
XLA Modules:
  0.0 314.1 jit_solution(2852977808588542840)
XLA Ops:
  0.0 3.3 %conditional.3 = (f32[16,32,256]{2,1,0:T(8,128)}) conditional(s32[]{:T(128)} %convert_element_type.4, () %tuple.19, (s32[]{:T(128)}, bf16[16,128,2048]{2,1,0:T(8,128)(2,1)}, bf16[2048,512]{1,0:T(8,128)(2,1)}) %tuple.26), branch_computations={%region_3.4_spmd, %region_4.5_spmd} | conditional | flops 536870912 | bytes 3670024 | solution.py:407
  0.0 3.3 %product_pieces.4 = f32[16,32,256]{2,1,0:T(8,128)} custom-call(s32[1]{0:T(128)} %bitcast.1.dest_ref, bf16[16,128,2048]{2,1,0:T(8,128)(2,1)} %get-tuple-element.27.refs_0_.refs_1_.refs_2_.refs_3_, bf16[16,128,2048]{2,1,0:T(8,128)(2,1)} %get-tuple-element.27.refs_0_.refs_1_.refs_2_.refs_3_, ...), custom_call_target="tpu_custom_call" | custom-call | flops 536870912 | bytes 3670016 | tf_op jit(solution)/shard_map/cond/branch_1_fun/product_pieces/pallas_call | solution.py:41
  3.3 2.5 collective-permute-start.10
  5.8 3.4 %conditional.2 = (f32[16,32,256]{2,1,0:T(8,128)}) conditional(s32[]{:T(128)} %convert_element_type.4, () %tuple.17, (s32[]{:T(128)}, bf16[16,128,2048]{2,1,0:T(8,128)(2,1)}, bf16[2048,512]{1,0:T(8,128)(2,1)}) %tuple.27), branch_computations={%region_1.2_spmd, %region_2.3_spmd} | conditional | flops 536870912 | bytes 3670024 | solution.py:407
  5.8 3.3 %product_pieces.3 = f32[16,32,256]{2,1,0:T(8,128)} custom-call(s32[1]{0:T(128)} %bitcast.dest_ref, bf16[16,128,2048]{2,1,0:T(8,128)(2,1)} %get-tuple-element.24.refs_0_.refs_1_.refs_2_.refs_3_, bf16[16,128,2048]{2,1,0:T(8,128)(2,1)} %get-tuple-element.24.refs_0_.refs_1_.refs_2_.refs_3_, ...), custom_call_target="tpu_custom_call" | custom-call | flops 536870912 | bytes 3670016 | tf_op jit(solution)/shard_map/cond/branch_1_fun/product_pieces/pallas_call | solution.py:41
  10.6 10.3 %product_pieces.5 = (f32[16,32,256]{2,1,0:T(8,128)S(1)}, f32[16,32,256]{2,1,0:T(8,128)S(1)}, f32[16,32,256]{2,1,0:T(8,128)S(1)}, f32[16,32,256]{2,1,0:T(8,128)S(...) custom-call(s32[4]{0:T(128)S(1)} %pad_add_fusion.2.dest_ref, ...), custom_call_target="tpu_custom_call" | custom-call | flops 4294967296 | bytes 14680064 | tf_op jit(solution)/shard_map/product_pieces/pallas_call | solution.py:41
  21.0 1.8 collective-permute-start.11
  23.5 6.1 %collective-permute-done.1 = f32[16,32,256]{2,1,0:T(8,128)S(1)} collective-permute-done((f32[16,32,256]{2,1,0:T(8,128)}, f32[16,32,256]{2,1,0:T(8,128)S(1)}, u32[]{:S(2)}, u32[]{:S(2)}) %collective-permute-start.1) | collective-permute-done | bytes 524320 | tf_op jit(solution)/shard_map/ppermute | solution.py:423
  30.5 5.1 %collective-permute-start.2 = (f32[16,32,256]{2,1,0:T(8,128)}, f32[16,32,256]{2,1,0:T(8,128)}, u32[]{:S(2)}, u32[]{:S(2)}) collective-permute-start(f32[16,32,256]{2,1,0:T(8,128)} %add.105), channel_id=1, source_target_pairs={{0,1},{1,2},{4,5},{5,6},{8,9},{9,10},{12,13},{13,14},{16,17},{17,1... | collective-permute-start | bytes 1572872 | tf_op jit(solution)/shard_map/ppermute | solution.py:425
  37.0 3.7 %collective-permute-done.11 = f32[16,32,256]{2,1,0:T(8,128)S(1)} collective-permute-done((f32[16,32,256]{2,1,0:T(8,128)S(1)}, f32[16,32,256]{2,1,0:T(8,128)S(1)}, u32[]{:S(2)}, u32[]{:S(2)}) %collective-permute-start.11) | collective-permute-done | bytes 524320 | tf_op jit(solution)/shard_map/ppermute | solution.py:425
  40.8 5.2 %collective-permute-start.12 = (f32[16,32,256]{2,1,0:T(8,128)S(1)}, f32[16,32,256]{2,1,0:T(8,128)}, u32[]{:S(2)}, u32[]{:S(2)}) collective-permute-start(f32[16,32,256]{2,1,0:T(8,128)S(1)} %add.111), channel_id=1, source_target_pairs={{0,1},{1,2},{2,3},{4,5},{5,6},{6,7},{8,9},{9,10},{10,11},{12,13},{... | collective-permute-start | bytes 1572872 | tf_op jit(solution)/shard_map/ppermute | solution.py:425
  47.6 4.6 %collective-permute-done.2 = f32[16,32,256]{2,1,0:T(8,128)} collective-permute-done((f32[16,32,256]{2,1,0:T(8,128)}, f32[16,32,256]{2,1,0:T(8,128)}, u32[]{:S(2)}, u32[]{:S(2)}) %collective-permute-start.2) | collective-permute-done | bytes 524320 | tf_op jit(solution)/shard_map/ppermute | solution.py:425
  52.1 1.9 add.106
  54.0 5.2 %collective-permute-start.3 = (f32[16,32,256]{2,1,0:T(8,128)}, f32[16,32,256]{2,1,0:T(8,128)}, u32[]{:S(2)}, u32[]{:S(2)}) collective-permute-start(f32[16,32,256]{2,1,0:T(8,128)} %add.106), channel_id=1, source_target_pairs={{0,1},{1,2},{2,3},{4,5},{5,6},{6,7},{8,9},{9,10},{10,11},{12,13},{... | collective-permute-start | bytes 1572872 | tf_op jit(solution)/shard_map/ppermute | solution.py:425
  59.2 1.9 add.108
  64.7 8.7 %collective-permute-done.3 = f32[16,32,256]{2,1,0:T(8,128)} collective-permute-done((f32[16,32,256]{2,1,0:T(8,128)}, f32[16,32,256]{2,1,0:T(8,128)}, u32[]{:S(2)}, u32[]{:S(2)}) %collective-permute-start.3) | collective-permute-done | bytes 524320 | tf_op jit(solution)/shard_map/ppermute | solution.py:425
  78.1 5.2 %collective-permute-start.16 = (f32[12,32,256]{2,1,0:T(8,128)S(1)}, f32[12,32,256]{2,1,0:T(8,128)S(1)}, u32[]{:S(2)}, u32[]{:S(2)}) collective-permute-start(f32[12,32,256]{2,1,0:T(8,128)S(1)} %get-tuple-element.65), channel_id=1, source_target_pairs={{0,12},{4,8},{24,20},{28,16},{1,13},{5,9},{25,21},{29,17},{2,14},{... | collective-permute-start | bytes 1179656 | tf_op jit(solution)/shard_map/ppermute | solution.py:442
  84.6 2.5 collective-permute-start.18
  91.0 3.9 %collective-permute-start.9 = (f32[12,32,256]{2,1,0:T(8,128)S(1)}, f32[12,32,256]{2,1,0:T(8,128)S(1)}, u32[]{:S(2)}, u32[]{:S(2)}) collective-permute-start(f32[12,32,256]{2,1,0:T(8,128)S(1)} %get-tuple-element.59), channel_id=1, source_target_pairs={{0,4},{8,12},{20,16},{28,24},{1,5},{9,13},{21,17},{29,25},{2,6},{1... | collective-permute-start | bytes 1179656 | tf_op jit(solution)/shard_map/ppermute | solution.py:442
  94.9 2.1 collective-permute-done.7.refs_1_
  97.0 4.6 %collective-permute-done.8.refs_2_ = f32[12,32,256]{2,1,0:T(8,128)S(1)} collective-permute-done((f32[12,32,256]{2,1,0:T(8,128)S(1)}, f32[12,32,256]{2,1,0:T(8,128)S(1)}, u32[]{:S(2)}, u32[]{:S(2)}) %collective-permute-start.8) | collective-permute-done | bytes 393248 | tf_op jit(solution)/shard_map/ppermute | solution.py:442
  104.9 3.0 collective-permute-start.20
  108.9 1.8 collective-permute-done.20
  113.2 1.9 collective-permute-start.23
  117.6 2.7 collective-permute-done.23
  120.3 2.8 collective-permute-done.24
  123.2 2.1 collective-permute-start.26
  128.0 3.0 collective-permute-done.27
  132.7 162.7 %basis_pieces.1 = (f32[384,128]{1,0:T(8,128)S(1)}, f32[384,128]{1,0:T(8,128)S(1)}, f32[384,128]{1,0:T(8,128)S(1)}, f32[128,512]{1,0:T(8,128)S(1)}) custom-call(s32[3]{0:T(128)S(1)} %pad_add_fusion.1.here_ref, f32[640,128]{1,0:T(8,128)S(1)} %pad_maximum_fusion.refs_0_, f32[640,128]{1,0:T(8,128)S(1)} %collective-permute-done.29.refs_1_, ...), custom_call_target="tpu_custom_call" | custom-call | flops 1610612736 | bytes 1835008 | tf_op jit(solution)/shard_map/basis_pieces/pallas_call | solution.py:297
  295.5 3.2 %collective-permute-start.31 = (f32[384,128]{1,0:T(8,128)S(1)}, f32[384,128]{1,0:T(8,128)S(1)}, u32[]{:S(2)}, u32[]{:S(2)}) collective-permute-start(f32[384,128]{1,0:T(8,128)S(1)} %get-tuple-element.73), channel_id=1, source_target_pairs={{0,2},{1,3},{2,0},{3,1},{4,6},{5,7},{6,4},{7,5},{8,10},{9,11},{10,... | collective-permute-start | bytes 589832 | tf_op jit(solution)/shard_map/ppermute | solution.py:450
  300.4 5.8 %collective-permute-done.30.refs_1_ = f32[384,128]{1,0:T(8,128)S(1)} collective-permute-done((f32[384,128]{1,0:T(8,128)S(1)}, f32[384,128]{1,0:T(8,128)S(1)}, u32[]{:S(2)}, u32[]{:S(2)}) %collective-permute-start.30) | collective-permute-done | bytes 196640 | tf_op jit(solution)/shard_map/ppermute | solution.py:450
  306.1 6.8 %collective-permute-done.31.refs_2_ = f32[384,128]{1,0:T(8,128)S(1)} collective-permute-done((f32[384,128]{1,0:T(8,128)S(1)}, f32[384,128]{1,0:T(8,128)S(1)}, u32[]{:S(2)}, u32[]{:S(2)}) %collective-permute-start.31) | collective-permute-done | bytes 196640 | tf_op jit(solution)/shard_map/ppermute | solution.py:450
  (70 shorter events, 36.0 us)
Async XLA Ops:
  3.3 17.7 %collective-permute-start.10 = (f32[16,32,256]{2,1,0:T(8,128)}, f32[16,32,256]{2,1,0:T(8,128)S(1)}, u32[]{:S(2)}, u32[]{:S(2)}) collective-permute-start(f32[16,32,256]{2,1,0:T(8,128)} %get-tuple-element.79), channel_id=1, source_target_pairs={{0,1},{3,2},{4,5},{7,6},{8,9},{11,10},{12,13},{15,14},{16,17},{19,... | collective-permute-start | bytes 1572872 | tf_op jit(solution)/shard_map/ppermute | solution.py:423
  9.2 20.5 %collective-permute-start.1 = (f32[16,32,256]{2,1,0:T(8,128)}, f32[16,32,256]{2,1,0:T(8,128)S(1)}, u32[]{:S(2)}, u32[]{:S(2)}) collective-permute-start(f32[16,32,256]{2,1,0:T(8,128)} %get-tuple-element.78), channel_id=1, source_target_pairs={{0,1},{3,2},{4,5},{7,6},{8,9},{11,10},{12,13},{15,14},{16,17},{19,... | collective-permute-start | bytes 1572872 | tf_op jit(solution)/shard_map/ppermute | solution.py:423
  21.0 19.7 %collective-permute-start.11 = (f32[16,32,256]{2,1,0:T(8,128)S(1)}, f32[16,32,256]{2,1,0:T(8,128)S(1)}, u32[]{:S(2)}, u32[]{:S(2)}) collective-permute-start(f32[16,32,256]{2,1,0:T(8,128)S(1)} %add.110), channel_id=1, source_target_pairs={{0,1},{1,2},{4,5},{5,6},{8,9},{9,10},{12,13},{13,14},{16,17},{17,1... | collective-permute-start | bytes 1572872 | tf_op jit(solution)/shard_map/ppermute | solution.py:425
  22.8 23.3 %collective-permute-start.13 = (f32[16,32,256]{2,1,0:T(8,128)S(1)}, f32[16,32,256]{2,1,0:T(8,128)S(1)}, u32[]{:S(2)}, u32[]{:S(2)}) collective-permute-start(f32[16,32,256]{2,1,0:T(8,128)S(1)} %add.110), channel_id=1, source_target_pairs={{2,1},{3,2},{6,5},{7,6},{10,9},{11,10},{14,13},{15,14},{18,17},{19... | collective-permute-start | bytes 1572872 | tf_op jit(solution)/shard_map/ppermute | solution.py:426
  30.5 21.6 %collective-permute-start.2 = (f32[16,32,256]{2,1,0:T(8,128)}, f32[16,32,256]{2,1,0:T(8,128)}, u32[]{:S(2)}, u32[]{:S(2)}) collective-permute-start(f32[16,32,256]{2,1,0:T(8,128)} %add.105), channel_id=1, source_target_pairs={{0,1},{1,2},{4,5},{5,6},{8,9},{9,10},{12,13},{13,14},{16,17},{17,1... | collective-permute-start | bytes 1572872 | tf_op jit(solution)/shard_map/ppermute | solution.py:425
  35.6 23.6 %collective-permute-start.4 = (f32[16,32,256]{2,1,0:T(8,128)}, f32[16,32,256]{2,1,0:T(8,128)}, u32[]{:S(2)}, u32[]{:S(2)}) collective-permute-start(f32[16,32,256]{2,1,0:T(8,128)} %add.105), channel_id=1, source_target_pairs={{2,1},{3,2},{6,5},{7,6},{10,9},{11,10},{14,13},{15,14},{18,17},{19... | collective-permute-start | bytes 1572872 | tf_op jit(solution)/shard_map/ppermute | solution.py:426
  40.8 22.4 %collective-permute-start.12 = (f32[16,32,256]{2,1,0:T(8,128)S(1)}, f32[16,32,256]{2,1,0:T(8,128)}, u32[]{:S(2)}, u32[]{:S(2)}) collective-permute-start(f32[16,32,256]{2,1,0:T(8,128)S(1)} %add.111), channel_id=1, source_target_pairs={{0,1},{1,2},{2,3},{4,5},{5,6},{6,7},{8,9},{9,10},{10,11},{12,13},{... | collective-permute-start | bytes 1572872 | tf_op jit(solution)/shard_map/ppermute | solution.py:425
  46.1 17.1 %collective-permute-start.14 = (f32[16,32,256]{2,1,0:T(8,128)S(1)}, f32[16,32,256]{2,1,0:T(8,128)}, u32[]{:S(2)}, u32[]{:S(2)}) collective-permute-start(f32[16,32,256]{2,1,0:T(8,128)S(1)} %add.113), channel_id=1, source_target_pairs={{1,0},{2,1},{3,2},{5,4},{6,5},{7,6},{9,8},{10,9},{11,10},{13,12},{... | collective-permute-start | bytes 1572872 | tf_op jit(solution)/shard_map/ppermute | solution.py:426
  47.4 17.2 %collective-permute-start = (s32[64]{0:T(128)S(1)}, s32[64]{0:T(128)S(1)}, u32[]{:S(2)}, u32[]{:S(2)}) collective-permute-start(s32[64]{0:T(128)S(1)} %bitcast.18), channel_id=1, source_target_pairs={{0,16},{16,0},{1,17},{17,1},{2,18},{18,2},{3,19},{19,3},{4,20},{20... | collective-permute-start | bytes 776 | tf_op jit(solution)/shard_map/ppermute | solution.py:378
  54.0 19.4 %collective-permute-start.3 = (f32[16,32,256]{2,1,0:T(8,128)}, f32[16,32,256]{2,1,0:T(8,128)}, u32[]{:S(2)}, u32[]{:S(2)}) collective-permute-start(f32[16,32,256]{2,1,0:T(8,128)} %add.106), channel_id=1, source_target_pairs={{0,1},{1,2},{2,3},{4,5},{5,6},{6,7},{8,9},{9,10},{10,11},{12,13},{... | collective-permute-start | bytes 1572872 | tf_op jit(solution)/shard_map/ppermute | solution.py:425
  61.1 13.6 %collective-permute-start.5 = (f32[16,32,256]{2,1,0:T(8,128)}, f32[16,32,256]{2,1,0:T(8,128)}, u32[]{:S(2)}, u32[]{:S(2)}) collective-permute-start(f32[16,32,256]{2,1,0:T(8,128)} %add.108), channel_id=1, source_target_pairs={{1,0},{2,1},{3,2},{5,4},{6,5},{7,6},{9,8},{10,9},{11,10},{13,12},{... | collective-permute-start | bytes 1572872 | tf_op jit(solution)/shard_map/ppermute | solution.py:426
  64.5 12.3 %collective-permute-start.15 = (f32[16,32,256]{2,1,0:T(8,128)S(1)}, f32[16,32,256]{2,1,0:T(8,128)S(1)}, u32[]{:S(2)}, u32[]{:S(2)}) collective-permute-start(f32[16,32,256]{2,1,0:T(8,128)S(1)} %add_add_fusion.refs_0_), channel_id=1, source_target_pairs={{0,16},{16,0},{1,17},{17,1},{2,18},{18,2},{3,19},{19,3},{4,20},{20... | collective-permute-start | bytes 1572872 | tf_op jit(solution)/shard_map/ppermute | solution.py:431
  76.0 11.1 %collective-permute-start.6 = (f32[16,32,256]{2,1,0:T(8,128)S(1)}, f32[16,32,256]{2,1,0:T(8,128)S(1)}, u32[]{:S(2)}, u32[]{:S(2)}) collective-permute-start(f32[16,32,256]{2,1,0:T(8,128)S(1)} %add_add_fusion.1.refs_0_), channel_id=1, source_target_pairs={{0,16},{16,0},{1,17},{17,1},{2,18},{18,2},{3,19},{19,3},{4,20},{20... | collective-permute-start | bytes 1572872 | tf_op jit(solution)/shard_map/ppermute | solution.py:431
  78.1 12.9 %collective-permute-start.16 = (f32[12,32,256]{2,1,0:T(8,128)S(1)}, f32[12,32,256]{2,1,0:T(8,128)S(1)}, u32[]{:S(2)}, u32[]{:S(2)}) collective-permute-start(f32[12,32,256]{2,1,0:T(8,128)S(1)} %get-tuple-element.65), channel_id=1, source_target_pairs={{0,12},{4,8},{24,20},{28,16},{1,13},{5,9},{25,21},{29,17},{2,14},{... | collective-permute-start | bytes 1179656 | tf_op jit(solution)/shard_map/ppermute | solution.py:442
  83.3 11.7 %collective-permute-start.17 = (f32[12,32,256]{2,1,0:T(8,128)S(1)}, f32[12,32,256]{2,1,0:T(8,128)S(1)}, u32[]{:S(2)}, u32[]{:S(2)}) collective-permute-start(f32[12,32,256]{2,1,0:T(8,128)S(1)} %get-tuple-element.66), channel_id=1, source_target_pairs={{0,8},{4,12},{24,16},{28,20},{1,9},{5,13},{25,17},{29,21},{2,10},{... | collective-permute-start | bytes 1179656 | tf_op jit(solution)/shard_map/ppermute | solution.py:442
  84.6 10.3 %collective-permute-start.18 = (f32[12,32,256]{2,1,0:T(8,128)S(1)}, f32[12,32,256]{2,1,0:T(8,128)S(1)}, u32[]{:S(2)}, u32[]{:S(2)}) collective-permute-start(f32[12,32,256]{2,1,0:T(8,128)S(1)} %get-tuple-element.67), channel_id=1, source_target_pairs={{0,4},{8,12},{20,16},{28,24},{1,5},{9,13},{21,17},{29,25},{2,6},{1... | collective-permute-start | bytes 1179656 | tf_op jit(solution)/shard_map/ppermute | solution.py:442
  88.3 8.7 %collective-permute-start.7 = (f32[12,32,256]{2,1,0:T(8,128)S(1)}, f32[12,32,256]{2,1,0:T(8,128)S(1)}, u32[]{:S(2)}, u32[]{:S(2)}) collective-permute-start(f32[12,32,256]{2,1,0:T(8,128)S(1)} %get-tuple-element.57), channel_id=1, source_target_pairs={{0,12},{4,8},{24,20},{28,16},{1,13},{5,9},{25,21},{29,17},{2,14},{... | collective-permute-start | bytes 1179656 | tf_op jit(solution)/shard_map/ppermute | solution.py:442
  89.6 12.0 %collective-permute-start.8 = (f32[12,32,256]{2,1,0:T(8,128)S(1)}, f32[12,32,256]{2,1,0:T(8,128)S(1)}, u32[]{:S(2)}, u32[]{:S(2)}) collective-permute-start(f32[12,32,256]{2,1,0:T(8,128)S(1)} %get-tuple-element.58), channel_id=1, source_target_pairs={{0,8},{4,12},{24,16},{28,20},{1,9},{5,13},{25,17},{29,21},{2,10},{... | collective-permute-start | bytes 1179656 | tf_op jit(solution)/shard_map/ppermute | solution.py:442
  91.0 10.7 %collective-permute-start.9 = (f32[12,32,256]{2,1,0:T(8,128)S(1)}, f32[12,32,256]{2,1,0:T(8,128)S(1)}, u32[]{:S(2)}, u32[]{:S(2)}) collective-permute-start(f32[12,32,256]{2,1,0:T(8,128)S(1)} %get-tuple-element.59), channel_id=1, source_target_pairs={{0,4},{8,12},{20,16},{28,24},{1,5},{9,13},{21,17},{29,25},{2,6},{1... | collective-permute-start | bytes 1179656 | tf_op jit(solution)/shard_map/ppermute | solution.py:442
  103.1 1.7 collective-permute-start.19
  104.9 5.8 %collective-permute-start.20 = (f32[160,128]{1,0:T(8,128)S(1)}, f32[160,128]{1,0:T(8,128)S(1)}, u32[]{:S(2)}, u32[]{:S(2)}) collective-permute-start(f32[160,128]{1,0:T(8,128)S(1)} %get-tuple-element.75), channel_id=1, source_target_pairs={{0,12},{4,8},{8,4},{12,0},{1,13},{5,9},{9,5},{13,1},{2,14},{6,10},... | collective-permute-start | bytes 245768 | tf_op jit(solution)/shard_map/ppermute | solution.py:450
  107.8 4.5 %collective-permute-start.21 = (f32[160,128]{1,0:T(8,128)S(1)}, f32[160,128]{1,0:T(8,128)S(1)}, u32[]{:S(2)}, u32[]{:S(2)}) collective-permute-start(f32[160,128]{1,0:T(8,128)S(1)} %get-tuple-element.77), channel_id=1, source_target_pairs={{0,8},{4,12},{8,0},{12,4},{1,9},{5,13},{9,1},{13,5},{2,10},{6,14},... | collective-permute-start | bytes 245768 | tf_op jit(solution)/shard_map/ppermute | solution.py:450
  108.5 4.7 %collective-permute-start.22 = (f32[160,128]{1,0:T(8,128)S(1)}, f32[160,128]{1,0:T(8,128)S(1)}, u32[]{:S(2)}, u32[]{:S(2)}) collective-permute-start(f32[160,128]{1,0:T(8,128)S(1)} %get-tuple-element.76), channel_id=1, source_target_pairs={{0,4},{4,0},{8,12},{12,8},{1,5},{5,1},{9,13},{13,9},{2,6},{6,2},{1... | collective-permute-start | bytes 245768 | tf_op jit(solution)/shard_map/ppermute | solution.py:450
  113.2 7.2 %collective-permute-start.23 = (f32[160,128]{1,0:T(8,128)S(1)}, f32[160,128]{1,0:T(8,128)S(1)}, u32[]{:S(2)}, u32[]{:S(2)}) collective-permute-start(f32[160,128]{1,0:T(8,128)S(1)} %fusion.1), channel_id=1, source_target_pairs={{0,3},{1,2},{2,1},{3,0},{4,7},{5,6},{6,5},{7,4},{8,11},{9,10},{10,... | collective-permute-start | bytes 245768 | tf_op jit(solution)/shard_map/ppermute | solution.py:450
  115.1 8.1 %collective-permute-start.24 = (f32[160,128]{1,0:T(8,128)S(1)}, f32[160,128]{1,0:T(8,128)S(1)}, u32[]{:S(2)}, u32[]{:S(2)}) collective-permute-start(f32[160,128]{1,0:T(8,128)S(1)} %fusion.1), channel_id=1, source_target_pairs={{0,2},{1,3},{2,0},{3,1},{4,6},{5,7},{6,4},{7,5},{8,10},{9,11},{10,... | collective-permute-start | bytes 245768 | tf_op jit(solution)/shard_map/ppermute | solution.py:450
  116.2 7.0 %collective-permute-start.25 = (f32[160,128]{1,0:T(8,128)S(1)}, f32[160,128]{1,0:T(8,128)S(1)}, u32[]{:S(2)}, u32[]{:S(2)}) collective-permute-start(f32[160,128]{1,0:T(8,128)S(1)} %fusion.1), channel_id=1, source_target_pairs={{0,1},{1,0},{2,3},{3,2},{4,5},{5,4},{6,7},{7,6},{8,9},{9,8},{10,11... | collective-permute-start | bytes 245768 | tf_op jit(solution)/shard_map/ppermute | solution.py:450
  123.2 4.8 %collective-permute-start.26 = (f32[160,128]{1,0:T(8,128)S(1)}, f32[160,128]{1,0:T(8,128)S(1)}, u32[]{:S(2)}, u32[]{:S(2)}) collective-permute-start(f32[160,128]{1,0:T(8,128)S(1)} %add_add_fusion.2), channel_id=1, source_target_pairs={{0,4},{4,0},{8,12},{12,8},{1,5},{5,1},{9,13},{13,9},{2,6},{6,2},{1... | collective-permute-start | bytes 245768 | tf_op jit(solution)/shard_map/ppermute | solution.py:450
  125.3 5.7 %collective-permute-start.27 = (f32[160,128]{1,0:T(8,128)S(1)}, f32[160,128]{1,0:T(8,128)S(1)}, u32[]{:S(2)}, u32[]{:S(2)}) collective-permute-start(f32[160,128]{1,0:T(8,128)S(1)} %add_add_fusion.2), channel_id=1, source_target_pairs={{0,8},{4,12},{8,0},{12,4},{1,9},{5,13},{9,1},{13,5},{2,10},{6,14},... | collective-permute-start | bytes 245768 | tf_op jit(solution)/shard_map/ppermute | solution.py:450
  125.4 5.6 %collective-permute-start.28 = (f32[160,128]{1,0:T(8,128)S(1)}, f32[160,128]{1,0:T(8,128)S(1)}, u32[]{:S(2)}, u32[]{:S(2)}) collective-permute-start(f32[160,128]{1,0:T(8,128)S(1)} %add_add_fusion.2), channel_id=1, source_target_pairs={{0,12},{4,8},{8,4},{12,0},{1,13},{5,9},{9,5},{13,1},{2,14},{6,10},... | collective-permute-start | bytes 245768 | tf_op jit(solution)/shard_map/ppermute | solution.py:450
  295.5 10.7 %collective-permute-start.30 = (f32[384,128]{1,0:T(8,128)S(1)}, f32[384,128]{1,0:T(8,128)S(1)}, u32[]{:S(2)}, u32[]{:S(2)}) collective-permute-start(f32[384,128]{1,0:T(8,128)S(1)} %get-tuple-element.72), channel_id=1, source_target_pairs={{0,1},{1,0},{2,3},{3,2},{4,5},{5,4},{6,7},{7,6},{8,9},{9,8},{10,11... | collective-permute-start | bytes 589832 | tf_op jit(solution)/shard_map/ppermute | solution.py:450
  295.5 17.4 %collective-permute-start.31 = (f32[384,128]{1,0:T(8,128)S(1)}, f32[384,128]{1,0:T(8,128)S(1)}, u32[]{:S(2)}, u32[]{:S(2)}) collective-permute-start(f32[384,128]{1,0:T(8,128)S(1)} %get-tuple-element.73), channel_id=1, source_target_pairs={{0,2},{1,3},{2,0},{3,1},{4,6},{5,7},{6,4},{7,5},{8,10},{9,11},{10,... | collective-permute-start | bytes 589832 | tf_op jit(solution)/shard_map/ppermute | solution.py:450
  298.7 14.2 %collective-permute-start.32 = (f32[384,128]{1,0:T(8,128)S(1)}, f32[384,128]{1,0:T(8,128)S(1)}, u32[]{:S(2)}, u32[]{:S(2)}) collective-permute-start(f32[384,128]{1,0:T(8,128)S(1)} %get-tuple-element.74), channel_id=1, source_target_pairs={{0,3},{1,2},{2,1},{3,0},{4,7},{5,6},{6,5},{7,4},{8,11},{9,10},{10,... | collective-permute-start | bytes 589832 | tf_op jit(solution)/shard_map/ppermute | solution.py:450
  (2 other events, 38.5 us)

commit v6 on v5

--- a/solution.py
+++ b/solution.py
@@ -91,7 +91,7 @@
         in_specs=[pl.BlockSpec(memory_space=pltpu.SMEM)] + [pl.BlockSpec(memory_space=pltpu.VMEM)] * children,
         out_specs=[pl.BlockSpec(memory_space=pltpu.VMEM)] * offsets,
         cost_estimate=pl.CostEstimate(flops=moved, bytes_accessed=moved, transcendentals=0),
-        compiler_params=grant(12),
+        compiler_params=grant(8),
         name="pack_slots",
     )(inverse.reshape(-1), *held)
 
@@ -155,7 +155,7 @@
         cost_estimate=pl.CostEstimate(
             flops=6 * height * tile * rows, bytes_accessed=4 * (len(flat) + 1) * rows * width, transcendentals=0
         ),
-        compiler_params=grant(20),
+        compiler_params=grant(14),
         name="gram_pieces",
     )(here, *flat)
     return outs[0], list(outs[1:])
@@ -320,7 +320,7 @@
         in_specs=[pl.BlockSpec(memory_space=pltpu.VMEM)] * 2,
         out_specs=pl.BlockSpec(memory_space=pltpu.VMEM),
         cost_estimate=pl.CostEstimate(flops=6 * rows * n * tile, bytes_accessed=4 * rows * (n + tile), transcendentals=0),
-        compiler_params=grant(12),
+        compiler_params=grant(8),
         name="own_piece",
     )(share, strip)
 
@@ -343,7 +343,7 @@
         in_specs=[pl.BlockSpec(memory_space=pltpu.SMEM)] + [pl.BlockSpec(memory_space=pltpu.VMEM)] * len(pieces),
         out_specs=pl.BlockSpec(memory_space=pltpu.VMEM),
         scratch_shapes=[pltpu.VMEM((slots, blk, width), jnp.float32)],
-        compiler_params=grant(12),
+        compiler_params=grant(8),
         name="lay_out",
     )(here.reshape(1), *pieces)
 

time: 316 us -> 316 us (level)
  no operation moved by 1% of the time
where the time goes in v6:
time: 316 us; the launch traced here: 314 us
  Pallas kernels  185 us (59%)
  waiting for transfers between devices  61.3 us (19%)
  starting transfers between devices  58.6 us (19%)
  other arithmetic  8.33 us (3%)
    pallas_call x1, Pallas kernels, basis_pieces(): pl.pallas_call(kernel, out_shape=[jax.ShapeDtypeStruct((rows, tile), jnp....  163 us
    ppermute x14, waiting for transfers between devices, swap(): lax.ppermute(x, name, [(i, i ^ level) for i in range(lax.axis_size(name))])  29.4 us
    ppermute x4, waiting for transfers between devices, shards(): came_up = lax.ppermute(up, 'col', [(i, i + 1) for i in range(stage)])  17.8 us
    ppermute x4, starting transfers between devices, shards(): came_up = lax.ppermute(up, 'col', [(i, i + 1) for i in range(stage)])  17.2 us
    ppermute x14, starting transfers between devices, swap(): lax.ppermute(x, name, [(i, i ^ level) for i in range(lax.axis_size(name))])  17.1 us
    pallas_call x3, Pallas kernels, product_pieces(): pl.pallas_call(kernel, out_shape=[jax.ShapeDtypeStruct((blocks, sub, widt...  16.9 us
    ppermute x6, starting transfers between devices, shards(): came.append(lax.ppermute(slotted[k], both, pairs))  15.5 us
    ppermute x6, waiting for transfers between devices, shards(): came.append(lax.ppermute(slotted[k], both, pairs))  6.71 us
  transfers between devices with their start and end apart: 33, of which 19 were waited for; matrix products, arithmetic and copies ran while one was open for 3% of the time, Pallas kernels for 5%

profile of v6, /device:TPU:0, one launch (start us, length us, event | category | flops | bytes accessed | tf_op | source)
XLA Modules:
  0.0 314.2 jit_solution(9661897832332088975)
XLA Ops:
  0.0 3.3 %conditional.3 = (f32[16,32,256]{2,1,0:T(8,128)}) conditional(s32[]{:T(128)} %convert_element_type.4, () %tuple.19, (s32[]{:T(128)}, bf16[16,128,2048]{2,1,0:T(8,128)(2,1)}, bf16[2048,512]{1,0:T(8,128)(2,1)}) %tuple.26), branch_computations={%region_3.4_spmd, %region_4.5_spmd} | conditional | flops 536870912 | bytes 3670024 | solution.py:407
  0.0 3.3 %product_pieces.4 = f32[16,32,256]{2,1,0:T(8,128)} custom-call(s32[1]{0:T(128)} %bitcast.1.dest_ref, bf16[16,128,2048]{2,1,0:T(8,128)(2,1)} %get-tuple-element.27.refs_0_.refs_1_.refs_2_.refs_3_, bf16[16,128,2048]{2,1,0:T(8,128)(2,1)} %get-tuple-element.27.refs_0_.refs_1_.refs_2_.refs_3_, ...), custom_call_target="tpu_custom_call" | custom-call | flops 536870912 | bytes 3670016 | tf_op jit(solution)/shard_map/cond/branch_1_fun/product_pieces/pallas_call | solution.py:41
  3.3 2.5 collective-permute-start.10
  5.8 3.4 %conditional.2 = (f32[16,32,256]{2,1,0:T(8,128)}) conditional(s32[]{:T(128)} %convert_element_type.4, () %tuple.17, (s32[]{:T(128)}, bf16[16,128,2048]{2,1,0:T(8,128)(2,1)}, bf16[2048,512]{1,0:T(8,128)(2,1)}) %tuple.27), branch_computations={%region_1.2_spmd, %region_2.3_spmd} | conditional | flops 536870912 | bytes 3670024 | solution.py:407
  5.8 3.3 %product_pieces.3 = f32[16,32,256]{2,1,0:T(8,128)} custom-call(s32[1]{0:T(128)} %bitcast.dest_ref, bf16[16,128,2048]{2,1,0:T(8,128)(2,1)} %get-tuple-element.24.refs_0_.refs_1_.refs_2_.refs_3_, bf16[16,128,2048]{2,1,0:T(8,128)(2,1)} %get-tuple-element.24.refs_0_.refs_1_.refs_2_.refs_3_, ...), custom_call_target="tpu_custom_call" | custom-call | flops 536870912 | bytes 3670016 | tf_op jit(solution)/shard_map/cond/branch_1_fun/product_pieces/pallas_call | solution.py:41
  10.6 10.3 %product_pieces.5 = (f32[16,32,256]{2,1,0:T(8,128)S(1)}, f32[16,32,256]{2,1,0:T(8,128)S(1)}, f32[16,32,256]{2,1,0:T(8,128)S(1)}, f32[16,32,256]{2,1,0:T(8,128)S(...) custom-call(s32[4]{0:T(128)S(1)} %pad_add_fusion.2.dest_ref, ...), custom_call_target="tpu_custom_call" | custom-call | flops 4294967296 | bytes 14680064 | tf_op jit(solution)/shard_map/product_pieces/pallas_call | solution.py:41
  21.0 1.8 collective-permute-start.11
  23.5 6.1 %collective-permute-done.1 = f32[16,32,256]{2,1,0:T(8,128)S(1)} collective-permute-done((f32[16,32,256]{2,1,0:T(8,128)}, f32[16,32,256]{2,1,0:T(8,128)S(1)}, u32[]{:S(2)}, u32[]{:S(2)}) %collective-permute-start.1) | collective-permute-done | bytes 524320 | tf_op jit(solution)/shard_map/ppermute | solution.py:423
  30.5 5.1 %collective-permute-start.2 = (f32[16,32,256]{2,1,0:T(8,128)}, f32[16,32,256]{2,1,0:T(8,128)}, u32[]{:S(2)}, u32[]{:S(2)}) collective-permute-start(f32[16,32,256]{2,1,0:T(8,128)} %add.105), channel_id=1, source_target_pairs={{0,1},{1,2},{4,5},{5,6},{8,9},{9,10},{12,13},{13,14},{16,17},{17,1... | collective-permute-start | bytes 1572872 | tf_op jit(solution)/shard_map/ppermute | solution.py:425
  37.0 3.7 %collective-permute-done.11 = f32[16,32,256]{2,1,0:T(8,128)S(1)} collective-permute-done((f32[16,32,256]{2,1,0:T(8,128)S(1)}, f32[16,32,256]{2,1,0:T(8,128)S(1)}, u32[]{:S(2)}, u32[]{:S(2)}) %collective-permute-start.11) | collective-permute-done | bytes 524320 | tf_op jit(solution)/shard_map/ppermute | solution.py:425
  40.8 5.2 %collective-permute-start.12 = (f32[16,32,256]{2,1,0:T(8,128)S(1)}, f32[16,32,256]{2,1,0:T(8,128)}, u32[]{:S(2)}, u32[]{:S(2)}) collective-permute-start(f32[16,32,256]{2,1,0:T(8,128)S(1)} %add.111), channel_id=1, source_target_pairs={{0,1},{1,2},{2,3},{4,5},{5,6},{6,7},{8,9},{9,10},{10,11},{12,13},{... | collective-permute-start | bytes 1572872 | tf_op jit(solution)/shard_map/ppermute | solution.py:425
  47.6 4.6 %collective-permute-done.2 = f32[16,32,256]{2,1,0:T(8,128)} collective-permute-done((f32[16,32,256]{2,1,0:T(8,128)}, f32[16,32,256]{2,1,0:T(8,128)}, u32[]{:S(2)}, u32[]{:S(2)}) %collective-permute-start.2) | collective-permute-done | bytes 524320 | tf_op jit(solution)/shard_map/ppermute | solution.py:425
  52.1 1.9 add.106
  54.0 5.2 %collective-permute-start.3 = (f32[16,32,256]{2,1,0:T(8,128)}, f32[16,32,256]{2,1,0:T(8,128)}, u32[]{:S(2)}, u32[]{:S(2)}) collective-permute-start(f32[16,32,256]{2,1,0:T(8,128)} %add.106), channel_id=1, source_target_pairs={{0,1},{1,2},{2,3},{4,5},{5,6},{6,7},{8,9},{9,10},{10,11},{12,13},{... | collective-permute-start | bytes 1572872 | tf_op jit(solution)/shard_map/ppermute | solution.py:425
  59.2 1.9 add.108
  64.7 8.7 %collective-permute-done.3 = f32[16,32,256]{2,1,0:T(8,128)} collective-permute-done((f32[16,32,256]{2,1,0:T(8,128)}, f32[16,32,256]{2,1,0:T(8,128)}, u32[]{:S(2)}, u32[]{:S(2)}) %collective-permute-start.3) | collective-permute-done | bytes 524320 | tf_op jit(solution)/shard_map/ppermute | solution.py:425
  78.1 5.2 %collective-permute-start.16 = (f32[12,32,256]{2,1,0:T(8,128)S(1)}, f32[12,32,256]{2,1,0:T(8,128)S(1)}, u32[]{:S(2)}, u32[]{:S(2)}) collective-permute-start(f32[12,32,256]{2,1,0:T(8,128)S(1)} %get-tuple-element.65), channel_id=1, source_target_pairs={{0,12},{4,8},{24,20},{28,16},{1,13},{5,9},{25,21},{29,17},{2,14},{... | collective-permute-start | bytes 1179656 | tf_op jit(solution)/shard_map/ppermute | solution.py:442
  84.6 2.5 collective-permute-start.18
  91.0 3.9 %collective-permute-start.9 = (f32[12,32,256]{2,1,0:T(8,128)S(1)}, f32[12,32,256]{2,1,0:T(8,128)S(1)}, u32[]{:S(2)}, u32[]{:S(2)}) collective-permute-start(f32[12,32,256]{2,1,0:T(8,128)S(1)} %get-tuple-element.59), channel_id=1, source_target_pairs={{0,4},{8,12},{20,16},{28,24},{1,5},{9,13},{21,17},{29,25},{2,6},{1... | collective-permute-start | bytes 1179656 | tf_op jit(solution)/shard_map/ppermute | solution.py:442
  94.9 2.1 collective-permute-done.7.refs_1_
  97.0 4.6 %collective-permute-done.8.refs_2_ = f32[12,32,256]{2,1,0:T(8,128)S(1)} collective-permute-done((f32[12,32,256]{2,1,0:T(8,128)S(1)}, f32[12,32,256]{2,1,0:T(8,128)S(1)}, u32[]{:S(2)}, u32[]{:S(2)}) %collective-permute-start.8) | collective-permute-done | bytes 393248 | tf_op jit(solution)/shard_map/ppermute | solution.py:442
  104.9 3.0 collective-permute-start.20
  108.9 1.8 collective-permute-done.20
  113.2 1.9 collective-permute-start.23
  117.6 2.7 collective-permute-done.23
  120.4 2.8 collective-permute-done.24
  123.2 2.1 collective-permute-start.26
  128.0 3.0 collective-permute-done.27
  132.7 162.7 %basis_pieces.1 = (f32[384,128]{1,0:T(8,128)S(1)}, f32[384,128]{1,0:T(8,128)S(1)}, f32[384,128]{1,0:T(8,128)S(1)}, f32[128,512]{1,0:T(8,128)S(1)}) custom-call(s32[3]{0:T(128)S(1)} %pad_add_fusion.1.here_ref, f32[640,128]{1,0:T(8,128)S(1)} %pad_maximum_fusion.refs_0_, f32[640,128]{1,0:T(8,128)S(1)} %collective-permute-done.29.refs_1_, ...), custom_call_target="tpu_custom_call" | custom-call | flops 1610612736 | bytes 1835008 | tf_op jit(solution)/shard_map/basis_pieces/pallas_call | solution.py:297
  295.5 3.2 %collective-permute-start.31 = (f32[384,128]{1,0:T(8,128)S(1)}, f32[384,128]{1,0:T(8,128)S(1)}, u32[]{:S(2)}, u32[]{:S(2)}) collective-permute-start(f32[384,128]{1,0:T(8,128)S(1)} %get-tuple-element.73), channel_id=1, source_target_pairs={{0,2},{1,3},{2,0},{3,1},{4,6},{5,7},{6,4},{7,5},{8,10},{9,11},{10,... | collective-permute-start | bytes 589832 | tf_op jit(solution)/shard_map/ppermute | solution.py:450
  300.4 5.8 %collective-permute-done.30.refs_1_ = f32[384,128]{1,0:T(8,128)S(1)} collective-permute-done((f32[384,128]{1,0:T(8,128)S(1)}, f32[384,128]{1,0:T(8,128)S(1)}, u32[]{:S(2)}, u32[]{:S(2)}) %collective-permute-start.30) | collective-permute-done | bytes 196640 | tf_op jit(solution)/shard_map/ppermute | solution.py:450
  306.2 6.8 %collective-permute-done.31.refs_2_ = f32[384,128]{1,0:T(8,128)S(1)} collective-permute-done((f32[384,128]{1,0:T(8,128)S(1)}, f32[384,128]{1,0:T(8,128)S(1)}, u32[]{:S(2)}, u32[]{:S(2)}) %collective-permute-start.31) | collective-permute-done | bytes 196640 | tf_op jit(solution)/shard_map/ppermute | solution.py:450
  (70 shorter events, 36.0 us)
Async XLA Ops:
  3.3 17.7 %collective-permute-start.10 = (f32[16,32,256]{2,1,0:T(8,128)}, f32[16,32,256]{2,1,0:T(8,128)S(1)}, u32[]{:S(2)}, u32[]{:S(2)}) collective-permute-start(f32[16,32,256]{2,1,0:T(8,128)} %get-tuple-element.79), channel_id=1, source_target_pairs={{0,1},{3,2},{4,5},{7,6},{8,9},{11,10},{12,13},{15,14},{16,17},{19,... | collective-permute-start | bytes 1572872 | tf_op jit(solution)/shard_map/ppermute | solution.py:423
  9.2 20.5 %collective-permute-start.1 = (f32[16,32,256]{2,1,0:T(8,128)}, f32[16,32,256]{2,1,0:T(8,128)S(1)}, u32[]{:S(2)}, u32[]{:S(2)}) collective-permute-start(f32[16,32,256]{2,1,0:T(8,128)} %get-tuple-element.78), channel_id=1, source_target_pairs={{0,1},{3,2},{4,5},{7,6},{8,9},{11,10},{12,13},{15,14},{16,17},{19,... | collective-permute-start | bytes 1572872 | tf_op jit(solution)/shard_map/ppermute | solution.py:423
  21.0 19.7 %collective-permute-start.11 = (f32[16,32,256]{2,1,0:T(8,128)S(1)}, f32[16,32,256]{2,1,0:T(8,128)S(1)}, u32[]{:S(2)}, u32[]{:S(2)}) collective-permute-start(f32[16,32,256]{2,1,0:T(8,128)S(1)} %add.110), channel_id=1, source_target_pairs={{0,1},{1,2},{4,5},{5,6},{8,9},{9,10},{12,13},{13,14},{16,17},{17,1... | collective-permute-start | bytes 1572872 | tf_op jit(solution)/shard_map/ppermute | solution.py:425
  22.8 23.3 %collective-permute-start.13 = (f32[16,32,256]{2,1,0:T(8,128)S(1)}, f32[16,32,256]{2,1,0:T(8,128)S(1)}, u32[]{:S(2)}, u32[]{:S(2)}) collective-permute-start(f32[16,32,256]{2,1,0:T(8,128)S(1)} %add.110), channel_id=1, source_target_pairs={{2,1},{3,2},{6,5},{7,6},{10,9},{11,10},{14,13},{15,14},{18,17},{19... | collective-permute-start | bytes 1572872 | tf_op jit(solution)/shard_map/ppermute | solution.py:426
  30.5 21.6 %collective-permute-start.2 = (f32[16,32,256]{2,1,0:T(8,128)}, f32[16,32,256]{2,1,0:T(8,128)}, u32[]{:S(2)}, u32[]{:S(2)}) collective-permute-start(f32[16,32,256]{2,1,0:T(8,128)} %add.105), channel_id=1, source_target_pairs={{0,1},{1,2},{4,5},{5,6},{8,9},{9,10},{12,13},{13,14},{16,17},{17,1... | collective-permute-start | bytes 1572872 | tf_op jit(solution)/shard_map/ppermute | solution.py:425
  35.6 23.6 %collective-permute-start.4 = (f32[16,32,256]{2,1,0:T(8,128)}, f32[16,32,256]{2,1,0:T(8,128)}, u32[]{:S(2)}, u32[]{:S(2)}) collective-permute-start(f32[16,32,256]{2,1,0:T(8,128)} %add.105), channel_id=1, source_target_pairs={{2,1},{3,2},{6,5},{7,6},{10,9},{11,10},{14,13},{15,14},{18,17},{19... | collective-permute-start | bytes 1572872 | tf_op jit(solution)/shard_map/ppermute | solution.py:426
  40.8 22.4 %collective-permute-start.12 = (f32[16,32,256]{2,1,0:T(8,128)S(1)}, f32[16,32,256]{2,1,0:T(8,128)}, u32[]{:S(2)}, u32[]{:S(2)}) collective-permute-start(f32[16,32,256]{2,1,0:T(8,128)S(1)} %add.111), channel_id=1, source_target_pairs={{0,1},{1,2},{2,3},{4,5},{5,6},{6,7},{8,9},{9,10},{10,11},{12,13},{... | collective-permute-start | bytes 1572872 | tf_op jit(solution)/shard_map/ppermute | solution.py:425
  46.1 17.1 %collective-permute-start.14 = (f32[16,32,256]{2,1,0:T(8,128)S(1)}, f32[16,32,256]{2,1,0:T(8,128)}, u32[]{:S(2)}, u32[]{:S(2)}) collective-permute-start(f32[16,32,256]{2,1,0:T(8,128)S(1)} %add.113), channel_id=1, source_target_pairs={{1,0},{2,1},{3,2},{5,4},{6,5},{7,6},{9,8},{10,9},{11,10},{13,12},{... | collective-permute-start | bytes 1572872 | tf_op jit(solution)/shard_map/ppermute | solution.py:426
  47.4 17.2 %collective-permute-start = (s32[64]{0:T(128)S(1)}, s32[64]{0:T(128)S(1)}, u32[]{:S(2)}, u32[]{:S(2)}) collective-permute-start(s32[64]{0:T(128)S(1)} %bitcast.18), channel_id=1, source_target_pairs={{0,16},{16,0},{1,17},{17,1},{2,18},{18,2},{3,19},{19,3},{4,20},{20... | collective-permute-start | bytes 776 | tf_op jit(solution)/shard_map/ppermute | solution.py:378
  54.0 19.4 %collective-permute-start.3 = (f32[16,32,256]{2,1,0:T(8,128)}, f32[16,32,256]{2,1,0:T(8,128)}, u32[]{:S(2)}, u32[]{:S(2)}) collective-permute-start(f32[16,32,256]{2,1,0:T(8,128)} %add.106), channel_id=1, source_target_pairs={{0,1},{1,2},{2,3},{4,5},{5,6},{6,7},{8,9},{9,10},{10,11},{12,13},{... | collective-permute-start | bytes 1572872 | tf_op jit(solution)/shard_map/ppermute | solution.py:425
  61.1 13.6 %collective-permute-start.5 = (f32[16,32,256]{2,1,0:T(8,128)}, f32[16,32,256]{2,1,0:T(8,128)}, u32[]{:S(2)}, u32[]{:S(2)}) collective-permute-start(f32[16,32,256]{2,1,0:T(8,128)} %add.108), channel_id=1, source_target_pairs={{1,0},{2,1},{3,2},{5,4},{6,5},{7,6},{9,8},{10,9},{11,10},{13,12},{... | collective-permute-start | bytes 1572872 | tf_op jit(solution)/shard_map/ppermute | solution.py:426
  64.5 12.3 %collective-permute-start.15 = (f32[16,32,256]{2,1,0:T(8,128)S(1)}, f32[16,32,256]{2,1,0:T(8,128)S(1)}, u32[]{:S(2)}, u32[]{:S(2)}) collective-permute-start(f32[16,32,256]{2,1,0:T(8,128)S(1)} %add_add_fusion.refs_0_), channel_id=1, source_target_pairs={{0,16},{16,0},{1,17},{17,1},{2,18},{18,2},{3,19},{19,3},{4,20},{20... | collective-permute-start | bytes 1572872 | tf_op jit(solution)/shard_map/ppermute | solution.py:431
  76.0 11.1 %collective-permute-start.6 = (f32[16,32,256]{2,1,0:T(8,128)S(1)}, f32[16,32,256]{2,1,0:T(8,128)S(1)}, u32[]{:S(2)}, u32[]{:S(2)}) collective-permute-start(f32[16,32,256]{2,1,0:T(8,128)S(1)} %add_add_fusion.1.refs_0_), channel_id=1, source_target_pairs={{0,16},{16,0},{1,17},{17,1},{2,18},{18,2},{3,19},{19,3},{4,20},{20... | collective-permute-start | bytes 1572872 | tf_op jit(solution)/shard_map/ppermute | solution.py:431
  78.1 12.9 %collective-permute-start.16 = (f32[12,32,256]{2,1,0:T(8,128)S(1)}, f32[12,32,256]{2,1,0:T(8,128)S(1)}, u32[]{:S(2)}, u32[]{:S(2)}) collective-permute-start(f32[12,32,256]{2,1,0:T(8,128)S(1)} %get-tuple-element.65), channel_id=1, source_target_pairs={{0,12},{4,8},{24,20},{28,16},{1,13},{5,9},{25,21},{29,17},{2,14},{... | collective-permute-start | bytes 1179656 | tf_op jit(solution)/shard_map/ppermute | solution.py:442
  83.3 11.7 %collective-permute-start.17 = (f32[12,32,256]{2,1,0:T(8,128)S(1)}, f32[12,32,256]{2,1,0:T(8,128)S(1)}, u32[]{:S(2)}, u32[]{:S(2)}) collective-permute-start(f32[12,32,256]{2,1,0:T(8,128)S(1)} %get-tuple-element.66), channel_id=1, source_target_pairs={{0,8},{4,12},{24,16},{28,20},{1,9},{5,13},{25,17},{29,21},{2,10},{... | collective-permute-start | bytes 1179656 | tf_op jit(solution)/shard_map/ppermute | solution.py:442
  84.6 10.3 %collective-permute-start.18 = (f32[12,32,256]{2,1,0:T(8,128)S(1)}, f32[12,32,256]{2,1,0:T(8,128)S(1)}, u32[]{:S(2)}, u32[]{:S(2)}) collective-permute-start(f32[12,32,256]{2,1,0:T(8,128)S(1)} %get-tuple-element.67), channel_id=1, source_target_pairs={{0,4},{8,12},{20,16},{28,24},{1,5},{9,13},{21,17},{29,25},{2,6},{1... | collective-permute-start | bytes 1179656 | tf_op jit(solution)/shard_map/ppermute | solution.py:442
  88.3 8.7 %collective-permute-start.7 = (f32[12,32,256]{2,1,0:T(8,128)S(1)}, f32[12,32,256]{2,1,0:T(8,128)S(1)}, u32[]{:S(2)}, u32[]{:S(2)}) collective-permute-start(f32[12,32,256]{2,1,0:T(8,128)S(1)} %get-tuple-element.57), channel_id=1, source_target_pairs={{0,12},{4,8},{24,20},{28,16},{1,13},{5,9},{25,21},{29,17},{2,14},{... | collective-permute-start | bytes 1179656 | tf_op jit(solution)/shard_map/ppermute | solution.py:442
  89.6 12.0 %collective-permute-start.8 = (f32[12,32,256]{2,1,0:T(8,128)S(1)}, f32[12,32,256]{2,1,0:T(8,128)S(1)}, u32[]{:S(2)}, u32[]{:S(2)}) collective-permute-start(f32[12,32,256]{2,1,0:T(8,128)S(1)} %get-tuple-element.58), channel_id=1, source_target_pairs={{0,8},{4,12},{24,16},{28,20},{1,9},{5,13},{25,17},{29,21},{2,10},{... | collective-permute-start | bytes 1179656 | tf_op jit(solution)/shard_map/ppermute | solution.py:442
  91.0 10.7 %collective-permute-start.9 = (f32[12,32,256]{2,1,0:T(8,128)S(1)}, f32[12,32,256]{2,1,0:T(8,128)S(1)}, u32[]{:S(2)}, u32[]{:S(2)}) collective-permute-start(f32[12,32,256]{2,1,0:T(8,128)S(1)} %get-tuple-element.59), channel_id=1, source_target_pairs={{0,4},{8,12},{20,16},{28,24},{1,5},{9,13},{21,17},{29,25},{2,6},{1... | collective-permute-start | bytes 1179656 | tf_op jit(solution)/shard_map/ppermute | solution.py:442
  103.1 1.7 collective-permute-start.19
  104.9 5.8 %collective-permute-start.20 = (f32[160,128]{1,0:T(8,128)S(1)}, f32[160,128]{1,0:T(8,128)S(1)}, u32[]{:S(2)}, u32[]{:S(2)}) collective-permute-start(f32[160,128]{1,0:T(8,128)S(1)} %get-tuple-element.75), channel_id=1, source_target_pairs={{0,12},{4,8},{8,4},{12,0},{1,13},{5,9},{9,5},{13,1},{2,14},{6,10},... | collective-permute-start | bytes 245768 | tf_op jit(solution)/shard_map/ppermute | solution.py:450
  107.8 4.5 %collective-permute-start.21 = (f32[160,128]{1,0:T(8,128)S(1)}, f32[160,128]{1,0:T(8,128)S(1)}, u32[]{:S(2)}, u32[]{:S(2)}) collective-permute-start(f32[160,128]{1,0:T(8,128)S(1)} %get-tuple-element.77), channel_id=1, source_target_pairs={{0,8},{4,12},{8,0},{12,4},{1,9},{5,13},{9,1},{13,5},{2,10},{6,14},... | collective-permute-start | bytes 245768 | tf_op jit(solution)/shard_map/ppermute | solution.py:450
  108.5 4.7 %collective-permute-start.22 = (f32[160,128]{1,0:T(8,128)S(1)}, f32[160,128]{1,0:T(8,128)S(1)}, u32[]{:S(2)}, u32[]{:S(2)}) collective-permute-start(f32[160,128]{1,0:T(8,128)S(1)} %get-tuple-element.76), channel_id=1, source_target_pairs={{0,4},{4,0},{8,12},{12,8},{1,5},{5,1},{9,13},{13,9},{2,6},{6,2},{1... | collective-permute-start | bytes 245768 | tf_op jit(solution)/shard_map/ppermute | solution.py:450
  113.2 7.2 %collective-permute-start.23 = (f32[160,128]{1,0:T(8,128)S(1)}, f32[160,128]{1,0:T(8,128)S(1)}, u32[]{:S(2)}, u32[]{:S(2)}) collective-permute-start(f32[160,128]{1,0:T(8,128)S(1)} %fusion.1), channel_id=1, source_target_pairs={{0,3},{1,2},{2,1},{3,0},{4,7},{5,6},{6,5},{7,4},{8,11},{9,10},{10,... | collective-permute-start | bytes 245768 | tf_op jit(solution)/shard_map/ppermute | solution.py:450
  115.1 8.1 %collective-permute-start.24 = (f32[160,128]{1,0:T(8,128)S(1)}, f32[160,128]{1,0:T(8,128)S(1)}, u32[]{:S(2)}, u32[]{:S(2)}) collective-permute-start(f32[160,128]{1,0:T(8,128)S(1)} %fusion.1), channel_id=1, source_target_pairs={{0,2},{1,3},{2,0},{3,1},{4,6},{5,7},{6,4},{7,5},{8,10},{9,11},{10,... | collective-permute-start | bytes 245768 | tf_op jit(solution)/shard_map/ppermute | solution.py:450
  116.2 7.0 %collective-permute-start.25 = (f32[160,128]{1,0:T(8,128)S(1)}, f32[160,128]{1,0:T(8,128)S(1)}, u32[]{:S(2)}, u32[]{:S(2)}) collective-permute-start(f32[160,128]{1,0:T(8,128)S(1)} %fusion.1), channel_id=1, source_target_pairs={{0,1},{1,0},{2,3},{3,2},{4,5},{5,4},{6,7},{7,6},{8,9},{9,8},{10,11... | collective-permute-start | bytes 245768 | tf_op jit(solution)/shard_map/ppermute | solution.py:450
  123.2 4.8 %collective-permute-start.26 = (f32[160,128]{1,0:T(8,128)S(1)}, f32[160,128]{1,0:T(8,128)S(1)}, u32[]{:S(2)}, u32[]{:S(2)}) collective-permute-start(f32[160,128]{1,0:T(8,128)S(1)} %add_add_fusion.2), channel_id=1, source_target_pairs={{0,4},{4,0},{8,12},{12,8},{1,5},{5,1},{9,13},{13,9},{2,6},{6,2},{1... | collective-permute-start | bytes 245768 | tf_op jit(solution)/shard_map/ppermute | solution.py:450
  125.3 5.7 %collective-permute-start.27 = (f32[160,128]{1,0:T(8,128)S(1)}, f32[160,128]{1,0:T(8,128)S(1)}, u32[]{:S(2)}, u32[]{:S(2)}) collective-permute-start(f32[160,128]{1,0:T(8,128)S(1)} %add_add_fusion.2), channel_id=1, source_target_pairs={{0,8},{4,12},{8,0},{12,4},{1,9},{5,13},{9,1},{13,5},{2,10},{6,14},... | collective-permute-start | bytes 245768 | tf_op jit(solution)/shard_map/ppermute | solution.py:450
  125.4 5.6 %collective-permute-start.28 = (f32[160,128]{1,0:T(8,128)S(1)}, f32[160,128]{1,0:T(8,128)S(1)}, u32[]{:S(2)}, u32[]{:S(2)}) collective-permute-start(f32[160,128]{1,0:T(8,128)S(1)} %add_add_fusion.2), channel_id=1, source_target_pairs={{0,12},{4,8},{8,4},{12,0},{1,13},{5,9},{9,5},{13,1},{2,14},{6,10},... | collective-permute-start | bytes 245768 | tf_op jit(solution)/shard_map/ppermute | solution.py:450
  295.5 10.7 %collective-permute-start.30 = (f32[384,128]{1,0:T(8,128)S(1)}, f32[384,128]{1,0:T(8,128)S(1)}, u32[]{:S(2)}, u32[]{:S(2)}) collective-permute-start(f32[384,128]{1,0:T(8,128)S(1)} %get-tuple-element.72), channel_id=1, source_target_pairs={{0,1},{1,0},{2,3},{3,2},{4,5},{5,4},{6,7},{7,6},{8,9},{9,8},{10,11... | collective-permute-start | bytes 589832 | tf_op jit(solution)/shard_map/ppermute | solution.py:450
  295.5 17.4 %collective-permute-start.31 = (f32[384,128]{1,0:T(8,128)S(1)}, f32[384,128]{1,0:T(8,128)S(1)}, u32[]{:S(2)}, u32[]{:S(2)}) collective-permute-start(f32[384,128]{1,0:T(8,128)S(1)} %get-tuple-element.73), channel_id=1, source_target_pairs={{0,2},{1,3},{2,0},{3,1},{4,6},{5,7},{6,4},{7,5},{8,10},{9,11},{10,... | collective-permute-start | bytes 589832 | tf_op jit(solution)/shard_map/ppermute | solution.py:450
  298.7 14.2 %collective-permute-start.32 = (f32[384,128]{1,0:T(8,128)S(1)}, f32[384,128]{1,0:T(8,128)S(1)}, u32[]{:S(2)}, u32[]{:S(2)}) collective-permute-start(f32[384,128]{1,0:T(8,128)S(1)} %get-tuple-element.74), channel_id=1, source_target_pairs={{0,3},{1,2},{2,1},{3,0},{4,7},{5,6},{6,5},{7,4},{8,11},{9,10},{10,... | collective-permute-start | bytes 589832 | tf_op jit(solution)/shard_map/ppermute | solution.py:450
  (2 other events, 38.5 us)
